TPU v7x, 32 devices: a whole 2x2x4 slice. The times are simulated.
32 devices in a mesh: ctx: 4 (over x, core), fsdp: 8 (over z, y).
Axes of the slice: x: 2, y: 2, z: 4, core: 2. Of those that a mesh axis runs over, the one named last changes fastest.
Arguments:
- inputs: bfloat16 [2, 8, 512, 1024], P(None, 'fsdp', 'ctx'), may hold values from -6 to 6
- cotangent: bfloat16 [2, 8, 512, 1024], P(None, 'fsdp', 'ctx'), may hold values from -6 to 6
- lengths: int32 [2, 8], P(None, 'fsdp'), may hold values from 128 to 512, as said below
- query_weight: bfloat16 [1024, 1024], P('fsdp'), may hold values from -0.1875 to 0.1875
- key_weight: bfloat16 [1024, 1024], P('fsdp'), may hold values from -0.1875 to 0.1875
- value_weight: bfloat16 [1024, 1024], P('fsdp'), may hold values from -0.1875 to 0.1875
- output_weight: bfloat16 [1024, 1024], P('fsdp'), may hold values from -0.75 to 0.75
- query_bias: bfloat16 [1024], P('fsdp'), may hold values from -3 to 3
- value_bias: bfloat16 [1024], P('fsdp'), may hold values from -3 to 3
- output_bias: bfloat16 [1024], P('fsdp'), may hold values from -2 to 2
- first_gain: bfloat16 [1024], P('fsdp'), may hold values from 0.099609375 to 1.8984375
- first_shift: bfloat16 [1024], P('fsdp'), may hold values from -2 to 2
- inner_weight: bfloat16 [1024, 4096], P('fsdp'), may hold values from -0.1875 to 0.1875
- inner_bias: bfloat16 [4096], P('fsdp'), may hold values from -3 to 3
- outer_weight: bfloat16 [4096, 1024], P('fsdp'), may hold values from -0.09375 to 0.09375
- outer_bias: bfloat16 [1024], P('fsdp'), may hold values from -2 to 2
- second_gain: bfloat16 [1024], P('fsdp'), may hold values from 0.099609375 to 1.8984375
- second_shift: bfloat16 [1024], P('fsdp'), may hold values from -2 to 2
Outputs:
- layer_output: bfloat16 [2, 8, 512, 1024], P(None, 'fsdp', 'ctx')
- input_gradient: float32 [2, 8, 512, 1024], P(None, 'fsdp', 'ctx')
- query_weight_gradient: float32 [1024, 1024], P('fsdp')
- key_weight_gradient: float32 [1024, 1024], P('fsdp')
- value_weight_gradient: float32 [1024, 1024], P('fsdp')
- output_weight_gradient: float32 [1024, 1024], P('fsdp')
- query_bias_gradient: float32 [1024], P('fsdp')
- value_bias_gradient: float32 [1024], P('fsdp')
- output_bias_gradient: float32 [1024], P('fsdp')
- first_gain_gradient: float32 [1024], P('fsdp')
- first_shift_gradient: float32 [1024], P('fsdp')
- inner_weight_gradient: float32 [1024, 4096], P('fsdp')
- inner_bias_gradient: float32 [4096], P('fsdp')
- outer_weight_gradient: float32 [4096, 1024], P('fsdp')
- outer_bias_gradient: float32 [1024], P('fsdp')
- second_gain_gradient: float32 [1024], P('fsdp')
- second_shift_gradient: float32 [1024], P('fsdp')
Inputs may be any that keep to these rules, and one draw needn't show every extreme that they name: The valid slots of a sequence are its first lengths entries; in every micro-batch some sequence fills all 512 slots.
All inputs are finite; a program needn't handle non-finite values.
Results may differ from a plain program's by a relative error of at most 0.018.
Values may be sent and summed in bfloat16 or wider, within the bound.
A program may use at most 256 MiB of HBM per device.

v0:
```python
import functools

import jax
import jax.numpy as jnp
from jax import lax
from jax.experimental import pallas as pl
from jax.experimental.pallas import tpu as pltpu
from jax.sharding import PartitionSpec as P

HEAD_DIM = 64
EPSILON = 1e-06
F32 = jnp.float32
BF16 = jnp.bfloat16

GATHER_SPLIT = ((256, 384), (256, 128), (512, 384), (160, 32))
REDUCE_SPLIT = ((768, 256), (128, 48), (256, 128), (1024, 128))
GATHER_ORDER = (
    0, 1, 9, 2, 3, 4, 13, 5, 6, 7, 10, 8, 11, 70, 32, 71, 69, 18, 35, 75, 33, 31, 76, 14, 16, 38,
    34, 41, 48, 37, 40, 12, 73, 22, 21, 17, 46, 78, 74, 24, 89, 43, 19, 81, 79, 107, 15, 27, 20,
    39, 45, 83, 72, 50, 23, 77, 86, 88, 36, 42, 29, 145, 108, 57, 146, 26, 84, 109, 147, 92, 54,
    111, 94, 30, 44, 80, 25, 55, 149, 114, 60, 62, 51, 113, 90, 95, 82, 152, 151, 116, 52, 110,
    47, 154, 97, 56, 87, 100, 117, 96, 155, 119, 49, 157, 150, 105, 59, 148, 85, 67, 121, 124,
    221, 93, 126, 28, 98, 159, 222, 112, 115, 53, 160, 102, 153, 162, 156, 183, 122, 184, 223, 63,
    165, 185, 58, 168, 130, 225, 187, 120, 158, 91, 127, 65, 164, 101, 103, 132, 227, 190, 128,
    228, 138, 166, 171, 189, 61, 186, 224, 133, 240, 99, 64, 241, 176, 230, 191, 188, 170, 231,
    118, 226, 229, 106, 202, 242, 204, 131, 161, 136, 247, 192, 66, 169, 193, 232, 141, 181, 123,
    172, 143, 174, 173, 209, 129, 68, 194, 163, 125, 246, 212, 233, 167, 135, 211, 248, 250, 178,
    205, 203, 195, 210, 235, 140, 249, 104, 200, 198, 179, 134, 234, 208, 182, 238, 244, 213, 137,
    206, 139, 177, 197, 243, 144, 180, 252, 257, 142, 236, 219, 239, 217, 201, 196, 254, 207, 214,
    199, 245, 251, 215, 255, 258, 175, 237, 253, 216, 256, 218, 220, 259,
)
REDUCE_ORDER = (
    0, 1, 9, 2, 3, 4, 5, 6, 7, 8, 10, 11, 32, 34, 220, 30, 218, 12, 14, 216, 13, 18, 28, 25, 15,
    17, 214, 16, 19, 20, 23, 21, 22, 31, 217, 24, 221, 29, 215, 33, 219, 222, 35, 36, 37, 27, 38,
    42, 223, 224, 226, 40, 43, 39, 225, 227, 85, 228, 41, 87, 84, 45, 86, 51, 44, 47, 88, 53, 89,
    90, 69, 70, 67, 68, 133, 46, 137, 26, 135, 136, 73, 74, 138, 57, 55, 165, 134, 71, 72, 166,
    168, 167, 139, 170, 171, 169, 59, 92, 91, 118, 119, 48, 94, 77, 49, 93, 75, 76, 63, 78, 54,
    79, 80, 81, 229, 61, 100, 116, 117, 95, 102, 96, 141, 140, 52, 122, 110, 123, 58, 120, 121,
    106, 126, 97, 143, 56, 142, 124, 125, 112, 173, 104, 172, 108, 128, 98, 127, 145, 144, 174,
    151, 157, 153, 199, 175, 129, 155, 161, 130, 197, 159, 203, 146, 183, 147, 198, 60, 149, 177,
    181, 185, 201, 189, 200, 202, 193, 176, 187, 62, 204, 101, 50, 64, 207, 208, 65, 205, 82, 103,
    178, 179, 206, 105, 152, 148, 150, 209, 107, 210, 211, 109, 131, 191, 156, 111, 154, 182, 83,
    184, 160, 158, 188, 113, 114, 99, 186, 192, 180, 190, 212, 162, 163, 194, 195, 66, 213, 115,
    164, 132, 196, 230,
)

MESH = pl.DeviceIdType.MESH
LINE = 4
PAIR = 2


class Place:
    def __init__(self):
        self.ctx = lax.axis_index("ctx")
        self.shard = lax.axis_index("fsdp")
        self.side = lax.div(self.ctx, 2)
        self.core = lax.rem(self.ctx, 2)
        self.line = lax.div(self.shard, PAIR)
        self.pair = lax.rem(self.shard, PAIR)

    def ahead(self, way):
        return (self.ctx, self.shard + way * PAIR)

    def across(self):
        return (self.ctx, self.shard + 1 - 2 * self.pair)

    def beside(self):
        return (self.ctx + 2 - 4 * self.side, self.shard)

    def twin(self):
        return (self.ctx + 1 - 2 * self.core, self.shard)

    def has(self, way, steps):
        if steps == 0:
            return None
        return self.line >= steps if way > 0 else self.line <= LINE - 1 - steps

    def can(self, way):
        return self.line <= LINE - 2 if way > 0 else self.line >= 1

    def shard_of(self, way, steps, other):
        pair = 1 - self.pair if other else self.pair
        return (self.line - way * steps) * PAIR + pair


def when(conditions, action):
    held = [c for c in conditions if c is not None]
    if not held:
        action()
        return
    both = held[0]
    for c in held[1:]:
        both = jnp.logical_and(both, c)
    pl.when(both)(action)


def greet(place):
    barrier = pltpu.get_barrier_semaphore()
    for peer in (place.across(), place.beside(), place.twin()):
        pl.semaphore_signal(barrier, inc=1, device_id=peer, device_id_type=MESH)
    for way in (1, -1):
        when(
            [place.can(way)],
            lambda way=way: pl.semaphore_signal(
                barrier, inc=1, device_id=place.ahead(way), device_id_type=MESH
            ),
        )
    lines = jnp.minimum(place.line, 1) + jnp.minimum(LINE - 1 - place.line, 1)
    pl.semaphore_wait(barrier, 3 + lines)


class Flow:
    def __init__(self, array, shard_rows, region, order="line", sides=False, cores=True):
        self.array = array
        self.shard_rows = shard_rows
        self.region = region
        self.order = order
        self.sides = sides
        self.cores = cores

    def view(self, ref, shard, core, side):
        row, rows, column, columns = self.region(core, side)
        start = row if shard is None else shard * self.shard_rows + row
        if not isinstance(start, int):
            start = pl.multiple_of(start, 16)
        if not isinstance(column, int):
            column = pl.multiple_of(column, 128)
        return ref.at[pl.ds(start, rows), pl.ds(column, columns)]


def positions(order):
    found = []
    if order == "line":
        found.append(("P", 1, 0, True))
        for steps in range(1, LINE):
            for way in (1, -1):
                found.append(("L", way, steps, False))
                found.append(("P", way, steps, True))
    else:
        found.append(("P", 1, 0, True))
        for steps in range(1, LINE):
            for way in (1, -1):
                found.append(("L", way, steps, False))
                found.append(("L", way, steps, True))
    return found


class Labels:
    def __init__(self):
        self.numbers = {}

    def __call__(self, key):
        return self.numbers.setdefault(key, len(self.numbers))


def gather_labels(flows):
    labels = Labels()
    for number, flow in enumerate(flows):
        for spot in positions(flow.order):
            labels((number, "in") + spot)
            if flow.sides:
                labels((number, "side") + spot)
            if flow.cores:
                labels((number, "twin") + spot)
                if flow.sides:
                    labels((number, "twinside") + spot)
    return labels


class Gather:
    def __init__(self, place, flows, owns, fulls, send, recv):
        self.place, self.flows, self.owns, self.fulls = place, flows, owns, fulls
        self.send, self.recv = send, recv
        self.labels = gather_labels(flows)
        self.sent = []

    def copy(self, number, key, spot, peer, core, side, own=False):
        flow = self.flows[number]
        place = self.place
        if own:
            shard = place.shard
            source = flow.view(self.owns[flow.array], None, core, side)
        else:
            shard = place.shard_of(*spot[1:])
            source = flow.view(self.fulls[flow.array], shard, core, side)
        target = flow.view(self.fulls[flow.array], shard, core, side)
        label = self.labels((number,) + key)
        return pltpu.make_async_remote_copy(
            source,
            target,
            self.send.at[label],
            self.recv.at[label],
            device_id=peer,
            device_id_type=MESH,
        )

    def start(self, conditions, copy):
        when(conditions, copy.start)
        self.sent.append((conditions, copy))

    def begin(self, number):
        flow, place = self.flows[number], self.place
        core, side = place.core, place.side
        here = (None, 1, 0, False)
        for way in (1, -1):
            self.start(
                [place.can(way)],
                self.copy(
                    number, ("in", "L", way, 1, False), here, place.ahead(way), core, side, True
                ),
            )
        self.start(
            [],
            self.copy(number, ("in", "P", 1, 0, True), here, place.across(), core, side, True),
        )

    def arrive(self, number, spot):
        flow, place = self.flows[number], self.place
        kind, way, steps, other = spot
        core, side = place.core, place.side
        there = place.has(way, steps)

        def take():
            self.copy(number, ("in",) + spot, spot, place.across(), core, side).wait_recv()

        when([there], take)

        def onward(extra, key, peer):
            self.start(
                [c for c in (there, extra) if c is not None],
                self.copy(number, key, spot, peer, core, side),
            )

        if kind == "L" and steps + 1 < LINE:
            onward(place.can(way), ("in", "L", way, steps + 1, other), place.ahead(way))
        if kind == "L" and flow.order == "line":
            onward(None, ("in", "P", way, steps, True), place.across())
        if kind == "P" and flow.order == "pair":
            for direction in (1, -1):
                onward(
                    place.can(direction), ("in", "L", direction, 1, True), place.ahead(direction)
                )
        if flow.sides:
            onward(None, ("side",) + spot, place.beside())
        if flow.cores:
            onward(None, ("twin",) + spot, place.twin())

    def arrive_side(self, number, spot):
        flow, place = self.flows[number], self.place
        there = place.has(*spot[1:3])
        core, side = place.core, 1 - place.side
        when(
            [there],
            lambda: self.copy(
                number, ("side",) + spot, spot, place.beside(), core, side
            ).wait_recv(),
        )
        if flow.cores:
            self.start(
                [there] if there is not None else [],
                self.copy(number, ("twinside",) + spot, spot, place.twin(), core, side),
            )

    def arrive_twin(self, number, spot):
        flow, place = self.flows[number], self.place
        there = place.has(*spot[1:3])
        core = 1 - place.core
        if flow.cores:
            when(
                [there],
                lambda: self.copy(
                    number, ("twin",) + spot, spot, place.twin(), core, place.side
                ).wait_recv(),
            )
            if flow.sides:
                when(
                    [there],
                    lambda: self.copy(
                        number, ("twinside",) + spot, spot, place.twin(), core, 1 - place.side
                    ).wait_recv(),
                )

    def actions(self):
        found = []
        for n, flow in enumerate(self.flows):
            found.append((("begin", n), lambda n=n: self.begin(n)))
        for index in range(len(positions("line"))):
            for n, flow in enumerate(self.flows):
                spot = positions(flow.order)[index]
                found.append((("in", n, spot), lambda n=n, spot=spot: self.arrive(n, spot)))
                if flow.sides:
                    found.append(
                        (("side", n, spot), lambda n=n, spot=spot: self.arrive_side(n, spot))
                    )
        found.append((("last",), self.finish))
        return found

    def finish(self):
        for number, flow in enumerate(self.flows):
            for spot in positions(flow.order):
                self.arrive_twin(number, spot)
        for conditions, copy in self.sent:
            when(conditions, copy.wait_send)


class Swap:
    def __init__(self, place, ins, outs, send, recv, local):
        side = place.side
        self.away = [
            pltpu.make_async_remote_copy(
                here.at[1 - side],
                there.at[side],
                send.at[k],
                recv.at[k],
                device_id=place.beside(),
                device_id_type=MESH,
            )
            for k, (here, there) in enumerate(zip(ins, outs))
        ]
        self.stay = [
            pltpu.make_async_copy(here.at[side], there.at[side], local.at[k])
            for k, (here, there) in enumerate(zip(ins, outs))
        ]

    def start(self):
        for copy in self.away + self.stay:
            copy.start()

    def finish(self):
        for copy in self.away + self.stay:
            copy.wait()


def swap_scratch(count):
    return [pltpu.SemaphoreType.DMA((count,))] * 3


def gather_kernel(flows, spots, blocks, order, *refs):
    count = max(array for array, _ in spots) + 1
    shares, refs = refs[: len(spots)], refs[len(spots) :]
    ins, refs = refs[:blocks], refs[blocks:]
    fulls, refs = refs[:count], refs[count:]
    outs, refs = refs[:blocks], refs[blocks:]
    owns, refs = refs[:count], refs[count:]
    send, recv, local, load = refs[:4]
    place = Place()
    loads = [
        pltpu.make_async_copy(
            share, owns[array].at[:, pl.ds(column, share.shape[1])], load.at[k]
        )
        for k, (share, (array, column)) in enumerate(zip(shares, spots))
    ]
    for copy in loads:
        copy.start()
    keep = [
        pltpu.make_async_copy(
            own, full.at[pl.ds(place.shard * own.shape[0], own.shape[0]), :], local.at[k]
        )
        for k, (own, full) in enumerate(zip(owns, fulls))
    ]
    greet(place)
    for copy in loads:
        copy.wait()
    swap = Swap(place, ins, outs, *refs[4:])
    swap.start()
    work = Gather(place, flows, owns, fulls, send, recv)
    for copy in keep:
        copy.start()
    for step in in_order(work.actions(), order):
        step()
    for copy in keep:
        copy.wait()
    swap.finish()


def gather_call(shares, spots, blocks, flows, shards, collective_id, order=None):
    labels = gather_labels(flows)
    count = max(array for array, _ in spots) + 1
    shapes = []
    for array in range(count):
        members = [share for share, spot in zip(shares, spots) if spot[0] == array]
        shapes.append((members[0].shape[0], sum(m.shape[1] for m in members)))
    far = pl.BlockSpec(memory_space=pl.ANY)
    return pl.pallas_call(
        functools.partial(gather_kernel, flows, spots, len(blocks), order),
        out_shape=[jax.ShapeDtypeStruct((shards * r, c), BF16) for r, c in shapes]
        + [jax.ShapeDtypeStruct(b.shape, b.dtype) for b in blocks],
        in_specs=[far] * (len(shares) + len(blocks)),
        out_specs=[far] * (count + len(blocks)),
        scratch_shapes=[pltpu.VMEM(shape, BF16) for shape in shapes]
        + [
            pltpu.SemaphoreType.DMA((len(labels.numbers),)),
            pltpu.SemaphoreType.DMA((len(labels.numbers),)),
            pltpu.SemaphoreType.DMA((count,)),
            pltpu.SemaphoreType.DMA((len(shares),)),
        ]
        + swap_scratch(len(blocks)),
        compiler_params=pltpu.CompilerParams(collective_id=collective_id, has_side_effects=True),
        name="gather_weights",
    )(*shares, *blocks)


def column_flows(array, shard_rows, columns, shared, early):
    half = columns // 2
    part = (half - shared) // 2
    flows = []
    if shared:
        flows.append(
            Flow(array, shard_rows, lambda core, side: (0, shard_rows, core * half, shared))
        )
    if early:
        flows.append(
            Flow(
                array,
                shard_rows,
                lambda core, side: (0, shard_rows, core * half + shared + side * part, early),
                sides=True,
            )
        )
    if part > early:
        flows.append(
            Flow(
                array,
                shard_rows,
                lambda core, side: (
                    0,
                    shard_rows,
                    core * half + shared + side * part + early,
                    part - early,
                ),
                order="pair",
                sides=True,
            )
        )
    return flows


def row_flows(array, shard_rows, columns, shared, early):
    half = shard_rows // 2
    part = (half - shared) // 2
    return [
        Flow(array, shard_rows, lambda core, side: (core * half, shared, 0, columns)),
        Flow(
            array,
            shard_rows,
            lambda core, side: (core * half + shared + side * part, early, 0, columns),
            sides=True,
        ),
        Flow(
            array,
            shard_rows,
            lambda core, side: (core * half + shared + side * part + early, part - early, 0, columns),
            order="pair",
            sides=True,
        ),
    ]


class Part:
    def __init__(self, rows, columns, along, flows, dtype=BF16):
        self.rows, self.columns, self.along, self.dtype = rows, columns, along, dtype
        self.flows = flows
        self.half_rows = rows // 2 if along == "rows" else rows
        self.half_columns = columns // 2 if along == "columns" else columns

    def half(self, ref, shard, core):
        base = 0 if shard is None else pl.multiple_of(shard * self.rows, 16)
        if self.along == "rows":
            row = core * self.half_rows + (0 if shard is None else shard * self.rows)
            return ref.at[pl.ds(pl.multiple_of(row, 16), self.half_rows), :]
        if self.along == "columns":
            column = pl.multiple_of(core * self.half_columns, 128)
            return ref.at[pl.ds(base, self.rows), pl.ds(column, self.half_columns)]
        return ref.at[pl.ds(base, self.rows), :]

    def inner(self, flow, side):
        first, extent = flow[0](side), flow[1]
        if self.along == "rows":
            start = first if isinstance(first, int) else pl.multiple_of(first, 16)
            return pl.ds(start, extent), slice(None)
        start = first if isinstance(first, int) else pl.multiple_of(first, 128)
        return slice(None), pl.ds(start, extent)

    def outer(self, flow, core, side):
        first, extent = flow[0](side), flow[1]
        if self.along == "rows":
            return pl.ds(pl.multiple_of(core * self.half_rows + first, 16), extent), slice(None)
        if self.along == "columns":
            return slice(None), pl.ds(
                pl.multiple_of(core * self.half_columns + first, 128), extent
            )
        return slice(None), slice(None)

    def extent(self, flow):
        if self.along == "rows":
            return flow[1], self.half_columns
        return self.half_rows, flow[1]


SPOTS = [(1, 3), (-1, 3), (1, 2), (-1, 2), (1, 1), (-1, 1), (1, 0)]


def reduce_scratch(parts):
    shapes = []
    for part in parts:
        half = (LINE * PAIR, part.half_rows, part.half_columns)
        shapes.append(pltpu.VMEM(half, part.dtype))
        shapes.append(pltpu.VMEM(half if part.along else half[1:], part.dtype))
        for flow in part.flows:
            rows, columns = part.extent(flow)
            shapes.append(
                pltpu.VMEM((LINE * PAIR if flow[3] else 1, rows, columns), part.dtype)
            )
            shapes.append(
                pltpu.VMEM((LINE if flow[2] == "line" else 1, rows, columns), part.dtype)
            )
            shapes.append(
                pltpu.VMEM(
                    ((LINE + 1) * (1 if flow[2] == "line" else PAIR), rows, columns), part.dtype
                )
            )
    return shapes


def reduce_labels(parts):
    labels = Labels()
    for n, part in enumerate(parts):
        for way, steps in SPOTS:
            for other in (False, True):
                labels((n, "twin", way, steps, other))
        labels((n, "twinend"))
        for k, flow in enumerate(part.flows):
            for way, steps in SPOTS:
                for other in (False, True):
                    if flow[3]:
                        labels((n, k, "side", way, steps, other))
                    if flow[2] == "pair" or not other:
                        labels((n, k, "line", way, steps, other))
                        if steps == 0:
                            labels((n, k, "line", -way, steps, other))
                if flow[2] == "line" or steps == 0:
                    labels((n, k, "pair", way, steps))
            labels((n, k, "sideend"))
            labels((n, k, "twinend"))
            labels((n, k, "twinsideend"))
    return labels


class Reduce:
    def __init__(self, place, parts, grads, outs, scratch, send, recv, load):
        self.place, self.parts, self.grads, self.outs = place, parts, grads, outs
        self.send, self.recv, self.load = send, recv, load
        self.labels = reduce_labels(parts)
        self.sent = []
        self.own, self.other, self.lanes = [], [], []
        at = 0
        for part in parts:
            self.own.append(scratch[at])
            self.other.append(scratch[at + 1])
            at += 2
            lanes = []
            for _ in part.flows:
                lanes.append(scratch[at : at + 3])
                at += 3
            self.lanes.append(lanes)

    def copy(self, source, target, key, peer):
        label = self.labels(key)
        return pltpu.make_async_remote_copy(
            source,
            target,
            self.send.at[label],
            self.recv.at[label],
            device_id=peer,
            device_id_type=MESH,
        )

    def start(self, conditions, copy):
        when(conditions, copy.start)
        self.sent.append((conditions, copy))

    def there(self, spot):
        return self.place.has(-spot[0], spot[1])

    def shard(self, spot, other):
        return self.place.shard_of(-spot[0], spot[1], other)

    def keep(self, n, spot, other):
        shard = self.shard(spot, other)
        label = SPOTS.index(spot) * 2 + int(other)
        return pltpu.make_async_copy(
            self.parts[n].half(self.grads[n], shard, self.place.core),
            self.own[n].at[shard],
            self.load.at[n * 2 * len(SPOTS) + label],
        )

    def twin(self, n, spot, other, core):
        shard = self.shard(spot, other)
        return self.copy(
            self.parts[n].half(self.grads[n], shard, core),
            self.other[n].at[shard],
            (n, "twin") + spot + (other,),
            self.place.twin(),
        )

    def begin(self, n, spot):
        there = self.there(spot)
        for other in (True, False):
            when([there], self.keep(n, spot, other).start)
            if self.parts[n].along:
                self.start([there], self.twin(n, spot, other, 1 - self.place.core))

    def piece(self, n, k, shard, side):
        part = self.parts[n]
        rows, columns = part.inner(part.flows[k], side)
        return self.own[n].at[shard, rows, columns]

    def side_copy(self, n, k, spot, other, side):
        shard = self.shard(spot, other)
        return self.copy(
            self.piece(n, k, shard, side),
            self.lanes[n][k][0].at[shard],
            (n, k, "side") + spot + (other,),
            self.place.beside(),
        )

    def add_cores(self, n, spot):
        there = self.there(spot)
        part = self.parts[n]
        for other in (True, False):

            def add(other=other):
                shard = self.shard(spot, other)
                self.keep(n, spot, other).wait()
                if part.along:
                    self.twin(n, spot, other, self.place.core).wait_recv()
                    self.own[n][shard] = self.own[n][shard] + self.other[n][shard]

            when([there], add)
        for other in (True, False):
            for k, flow in enumerate(part.flows):
                if flow[3]:
                    self.start([there], self.side_copy(n, k, spot, other, 1 - self.place.side))
                elif other:
                    self.start([there], self.pair_copy(n, k, spot, self.shard(spot, True)))

    def pair_copy(self, n, k, spot, shard):
        flow = self.parts[n].flows[k]
        slot = self.place.line + spot[0] * spot[1] if flow[2] == "line" else 0
        return self.copy(
            self.piece(n, k, shard, self.place.side),
            self.lanes[n][k][1].at[slot],
            (n, k, "pair") + spot,
            self.place.across(),
        )

    def add_sides(self, n, k, spot):
        there = self.there(spot)
        side = self.place.side
        for other in (True, False):

            def add(other=other):
                shard = self.shard(spot, other)
                self.side_copy(n, k, spot, other, side).wait_recv()
                piece = self.piece(n, k, shard, side)
                piece[...] = piece[...] + self.lanes[n][k][0][shard]

            when([there], add)
        if self.parts[n].flows[k][2] == "line":
            self.start([there], self.pair_copy(n, k, spot, self.shard(spot, True)))

    def line_slot(self, flow, way, steps, other, line):
        slot = line if (steps > 0 or way > 0) else LINE
        return slot + (LINE + 1) * int(other) if flow[2] == "pair" else slot

    def line_copy(self, n, k, spot, other, arriving):
        flow = self.parts[n].flows[k]
        way, steps = spot
        shard = self.shard(spot, other)
        line = self.place.line + way * steps
        left = steps if arriving else steps - 1
        return self.copy(
            self.piece(n, k, shard, self.place.side),
            self.lanes[n][k][2].at[self.line_slot(flow, way, left, other, line)],
            (n, k, "line", way, left, other),
            self.place.ahead(way),
        )

    def add_line(self, n, k, spot):
        place = self.place
        there = self.there(spot)
        way, steps = spot
        side = place.side
        flow = self.parts[n].flows[k]
        if flow[2] == "line":

            def add():
                shard = self.shard(spot, False)
                self.pair_copy(n, k, spot, shard).wait_recv()
                piece = self.piece(n, k, shard, side)
                piece[...] = piece[...] + self.lanes[n][k][1][place.line + way * steps]

            when([there], add)
        for other in (True, False) if flow[2] == "pair" else (False,):
            for direction in (1, -1) if steps == 0 else (way,):

                def add_line(other=other, here=(direction, steps)):
                    self.line_copy(n, k, here, other, True).wait_recv()
                    piece = self.piece(n, k, self.shard(here, other), side)
                    line = place.line + here[0] * here[1]
                    slot = self.line_slot(flow, here[0], here[1], other, line)
                    piece[...] = piece[...] + self.lanes[n][k][2][slot]

                when([there, place.can(-direction)], add_line)
            if steps > 0:
                self.start([there], self.line_copy(n, k, spot, other, False))

    def send_pair(self, n, k):
        self.start([], self.pair_copy(n, k, (1, 0), self.shard((1, 0), True)))

    def send_swap(self, n, k):
        self.start([], self.swap(n, k))

    def settle(self, n, k):
        place = self.place
        core, side, here = place.core, place.side, place.shard
        part = self.parts[n]
        flow = part.flows[k]
        piece = self.piece(n, k, here, side)
        out = self.out_view(n, k, core, side)
        if flow[3]:
            if flow[2] == "pair":
                self.pair_copy(n, k, (1, 0), here).wait_recv()
                out[...] = piece[...] + self.lanes[n][k][1][0]
            else:
                out[...] = piece[...]
            self.start([], self.out_copy(n, k, "sideend", place.beside(), core, side))
        else:
            self.swap(n, k).wait_recv()
            out[...] = piece[...] + self.lanes[n][k][0][0]
        if part.along:
            self.start([], self.out_copy(n, k, "twinend", place.twin(), core, side))
        else:
            self.start([], self.whole(n, k))

    def settle_side(self, n, k):
        place = self.place
        core, side = place.core, 1 - place.side
        self.out_copy(n, k, "sideend", place.beside(), core, side).wait_recv()
        self.start([], self.out_copy(n, k, "twinsideend", place.twin(), core, side))

    def swap(self, n, k):
        return self.copy(
            self.piece(n, k, self.place.shard, self.place.side),
            self.lanes[n][k][0].at[0],
            (n, k, "sideend"),
            self.place.beside(),
        )

    def out_view(self, n, k, core, side):
        part = self.parts[n]
        rows, columns = part.outer(part.flows[k], core, side)
        return self.outs[n].at[rows, columns]

    def out_copy(self, n, k, key, peer, core, side):
        view = self.out_view(n, k, core, side)
        return self.copy(view, view, (n, k, key), peer)

    def last(self):
        place = self.place
        core, side = place.core, place.side
        everything = [(n, k) for n, part in enumerate(self.parts) for k in range(len(part.flows))]
        for n, k in everything:
            if self.parts[n].along:
                self.out_copy(n, k, "twinend", place.twin(), 1 - core, side).wait_recv()
                if self.parts[n].flows[k][3]:
                    self.out_copy(
                        n, k, "twinsideend", place.twin(), 1 - core, 1 - side
                    ).wait_recv()
            else:
                self.whole(n, k).wait_recv()
        for conditions, copy in self.sent:
            when(conditions, copy.wait_send)
        for n, k in everything:
            if not self.parts[n].along:
                view = self.out_view(n, k, core, side)
                view[...] = view[...] + self.other[n][...]

    def whole(self, n, k):
        return self.copy(
            self.out_view(n, k, self.place.core, self.place.side),
            self.other[n],
            (n, k, "twinend"),
            self.place.twin(),
        )

    def actions(self):
        found = []
        for n, part in enumerate(self.parts):
            for spot in SPOTS:
                found.append((("begin", n, spot), lambda n=n, s=spot: self.begin(n, s)))
        for n, part in enumerate(self.parts):
            for spot in SPOTS:
                found.append((("cores", n, spot), lambda n=n, s=spot: self.add_cores(n, s)))
            for k, flow in enumerate(part.flows):
                at = (n, k)
                for spot in SPOTS:
                    if flow[3]:
                        found.append(
                            (("sides", n, k, spot), lambda at=at, s=spot: self.add_sides(*at, s))
                        )
                    found.append(
                        (("line", n, k, spot), lambda at=at, s=spot: self.add_line(*at, s))
                    )
                if flow[2] == "pair":
                    found.append((("pair", n, k), lambda at=at: self.send_pair(*at)))
                if not flow[3]:
                    found.append((("swap", n, k), lambda at=at: self.send_swap(*at)))
                found.append((("settle", n, k), lambda at=at: self.settle(*at)))
                if flow[3]:
                    found.append((("after", n, k), lambda at=at: self.settle_side(*at)))
        found.append((("last",), self.last))
        return found


def in_order(actions, order):
    if order is None:
        return [action for _, action in actions]
    assert sorted(order) == list(range(len(actions)))
    return [actions[i][1] for i in order]


def reduce_kernel(parts, blocks, order, *refs):
    count = len(parts)
    grads, refs = refs[:count], refs[count:]
    ins, refs = refs[:blocks], refs[blocks:]
    outs, refs = refs[:count], refs[count:]
    swapped, refs = refs[:blocks], refs[blocks:]
    scratch, (send, recv, load), sems = refs[:-6], refs[-6:-3], refs[-3:]
    place = Place()
    greet(place)
    swap = Swap(place, ins, swapped, *sems)
    swap.start()
    work = Reduce(place, parts, grads, outs, scratch, send, recv, load)
    for step in in_order(work.actions(), order):
        step()
    swap.finish()


def reduce_call(arrays, blocks, parts, collective_id, order=None):
    labels = reduce_labels(parts)
    count = len(arrays)
    return pl.pallas_call(
        functools.partial(reduce_kernel, parts, len(blocks), order),
        out_shape=[jax.ShapeDtypeStruct((p.rows, p.columns), p.dtype) for p in parts]
        + [jax.ShapeDtypeStruct(b.shape, b.dtype) for b in blocks],
        in_specs=[pl.BlockSpec(memory_space=pl.ANY)] * (count + len(blocks)),
        out_specs=[pl.BlockSpec(memory_space=pltpu.VMEM)] * count
        + [pl.BlockSpec(memory_space=pl.ANY)] * len(blocks),
        scratch_shapes=reduce_scratch(parts)
        + [
            pltpu.SemaphoreType.DMA((len(labels.numbers),)),
            pltpu.SemaphoreType.DMA((len(labels.numbers),)),
            pltpu.SemaphoreType.DMA((count * 2 * len(SPOTS),)),
        ]
        + swap_scratch(len(blocks)),
        compiler_params=pltpu.CompilerParams(
            collective_id=collective_id, has_side_effects=True, vmem_limit_bytes=63 << 20
        ),
        name="reduce_gradients",
    )(*arrays, *blocks)


def column_part(rows, columns, shared, early):
    half = columns // 2
    part = (half - shared) // 2
    flows = []
    if shared:
        flows.append((lambda side: 0, shared, "line", False))
    if early:
        flows.append((lambda side: shared + side * part, early, "line", True))
    if part > early:
        flows.append((lambda side: shared + side * part + early, part - early, "pair", True))
    return Part(rows, columns, "columns", flows)


def row_part(rows, columns, shared, early):
    half = rows // 2
    part = (half - shared) // 2
    return Part(
        rows,
        columns,
        "rows",
        [
            (lambda side: 0, shared, "line", False),
            (lambda side: shared + side * part, early, "line", True),
            (lambda side: shared + side * part + early, part - early, "pair", True),
        ],
    )


def vector_part(rows, columns):
    return Part(rows, columns, None, [(lambda side: 0, columns, "line", False)], F32)


ROW_QUERY, ROW_VALUE, ROW_OUTPUT, ROW_GAIN1, ROW_SHIFT1, ROW_INNER, INNER = 0, 1, 2, 3, 4, 5, 4
ROW_OUTER, ROW_GAIN2, ROW_SHIFT2 = 9, 10, 11
TABLE_ROWS = 16
LANES = 128
BAND = 32


def spread_table(table_ref, vec):
    for shard in range(table_ref.shape[0] // TABLE_ROWS):
        vec[:, pl.ds(shard * LANES, LANES)] = table_ref[
            pl.ds(shard * TABLE_ROWS, TABLE_ROWS), :
        ].astype(F32)


def fold_table(vec, table_ref, first, count):
    for shard in range(table_ref.shape[0] // TABLE_ROWS):
        table_ref[pl.ds(shard * TABLE_ROWS + first, count), :] = vec[
            pl.ds(first, count), pl.ds(shard * LANES, LANES)
        ]


def row_place(row, core, rows):
    half = rows // 2
    return jnp.where(row < half, row, row + half) + core * half


def total_rows(block):
    return jnp.sum(block.astype(F32), axis=0, keepdims=True)


def middle_kernel(
    rows_ref,
    context_ref,
    cot_ref,
    lengths_ref,
    table_ref,
    output_w,
    inner_w,
    outer_w,
    out_ref,
    first_grad_ref,
    context_grad_ref,
    sums_ref,
    output_g,
    inner_g,
    outer_g,
    output_v,
    inner_v,
    outer_v,
    vec,
    sums,
    active,
    slope,
    unit1,
    unit2,
    rate1,
    total,
    low,
    low_t,
    second,
    second_low,
    inner_b,
    outer_b,
    load,
    save,
):
    rows, width = rows_ref.shape
    tiles, _, tile = inner_v.shape
    ctx = lax.axis_index("ctx")
    side, core = lax.div(ctx, 2), lax.rem(ctx, 2)
    length = lengths_ref[side, 0]
    bands = rows // BAND

    def inner_load(t):
        return pltpu.make_async_copy(
            inner_w.at[:, pl.ds(pl.multiple_of(t * tile, tile), tile)], inner_v.at[t], load.at[0, t]
        )

    def outer_load(t):
        return pltpu.make_async_copy(
            outer_w.at[pl.ds(pl.multiple_of(t * tile, tile), tile), :], outer_v.at[t], load.at[1, t]
        )

    output_load = pltpu.make_async_copy(output_w, output_v, load.at[2, 0])
    output_load.start()
    for t in range(tiles):
        inner_load(t).start()
        outer_load(t).start()
    spread_table(table_ref, vec)
    sums[...] = jnp.zeros_like(sums)
    output_load.wait()
    total[...] = plain_product(context_ref[...], output_v[...])

    def band_of(b):
        return pl.ds(pl.multiple_of(b * BAND, BAND), BAND)

    def first_norm(b, carry):
        here = band_of(b)
        first_sum = (
            rows_ref[here, :].astype(F32) + total[here, :] + vec[pl.ds(ROW_OUTPUT, 1), :]
        )
        unit, rate = norm_parts(first_sum)
        unit1[here, :] = unit
        rate1[here, :] = jnp.broadcast_to(rate, (BAND, LANES))
        normed = unit * vec[pl.ds(ROW_GAIN1, 1), :] + vec[pl.ds(ROW_SHIFT1, 1), :]
        low[here, :] = normed.astype(BF16)
        total[here, :] = normed + vec[pl.ds(ROW_OUTER, 1), :]
        return carry

    lax.fori_loop(0, bands, first_norm, 0)
    low_t[...] = low[...].T

    def forward(t, carry):
        inner_load(t).wait()
        bias = jnp.concatenate(
            [
                vec[pl.ds(ROW_INNER + k, 1), pl.ds(pl.multiple_of(t * LANES, LANES), LANES)]
                for k in range(INNER)
            ],
            axis=1,
        )
        hidden = plain_product(low[...], inner_v[t]) + bias
        share = 0.5 + 0.5 * lax.erf(hidden * 0.7071067811865476)
        active[t] = (hidden * share).astype(BF16)
        slope[t] = share + hidden * (jnp.exp(-0.5 * hidden * hidden) * 0.3989422804014327)
        outer_load(t).wait()
        total[...] += plain_product(active[t], outer_v[t])
        return carry

    lax.fori_loop(0, tiles, forward, 0)

    def second_norm(b, carry):
        here = band_of(b)
        unit, rate = norm_parts(total[here, :])
        row = b * BAND + lax.broadcasted_iota(jnp.int32, (BAND, width), 0)
        mask = (row_place(row, core, rows) < length).astype(F32)
        gain = vec[pl.ds(ROW_GAIN2, 1), :]
        out_ref[here, :] = ((unit * gain + vec[pl.ds(ROW_SHIFT2, 1), :]) * mask).astype(BF16)
        out_grad = cot_ref[here, :].astype(F32) * mask
        grad = norm_back(unit, rate, out_grad * gain)
        second[here, :] = grad
        grad_low = grad.astype(BF16)
        second_low[here, :] = grad_low
        sums[pl.ds(ROW_GAIN2, 1), :] += total_rows(out_grad * unit)
        sums[pl.ds(ROW_SHIFT2, 1), :] += total_rows(out_grad)
        sums[pl.ds(ROW_OUTER, 1), :] += total_rows(grad_low)
        return carry

    lax.fori_loop(0, bands, second_norm, 0)

    def inner_save(t):
        slot = lax.rem(t, 2)
        return pltpu.make_async_copy(
            inner_b.at[slot],
            inner_g.at[:, pl.ds(pl.multiple_of(t * tile, tile), tile)],
            save.at[0, slot],
        )

    def outer_save(t):
        slot = lax.rem(t, 2)
        return pltpu.make_async_copy(
            outer_b.at[slot],
            outer_g.at[pl.ds(pl.multiple_of(t * tile, tile), tile), :],
            save.at[1, slot],
        )

    def backward(t, carry):
        slot = lax.rem(t, 2)
        hidden_grad = (right_product(second_low[...], outer_v[t]) * slope[t]).astype(BF16)
        summed = total_rows(hidden_grad)
        for k in range(INNER):
            sums[
                pl.ds(ROW_INNER + k, 1), pl.ds(pl.multiple_of(t * LANES, LANES), LANES)
            ] = summed[:, k * LANES : (k + 1) * LANES]

        @pl.when(t >= 2)
        def _():
            outer_save(t - 2).wait()
            inner_save(t - 2).wait()

        outer_b[slot] = left_product(active[t], second_low[...]).astype(BF16)
        inner_b[slot] = plain_product(low_t[...], hidden_grad).astype(BF16)
        outer_save(t).start()
        second[...] += right_product(hidden_grad, inner_v[t])
        inner_save(t).start()
        return carry

    lax.fori_loop(0, tiles, backward, 0)

    def first_back(b, carry):
        here = band_of(b)
        grad = second[here, :]
        unit = unit1[here, :]
        sums[pl.ds(ROW_GAIN1, 1), :] += total_rows(grad * unit)
        sums[pl.ds(ROW_SHIFT1, 1), :] += total_rows(grad)
        back = norm_back(unit, rate1[here, :1], grad * vec[pl.ds(ROW_GAIN1, 1), :])
        first_grad_ref[here, :] = back
        back_low = back.astype(BF16)
        second_low[here, :] = back_low
        sums[pl.ds(ROW_OUTPUT, 1), :] += total_rows(back_low)
        return carry

    lax.fori_loop(0, bands, first_back, 0)
    context_grad_ref[...] = right_product(second_low[...], output_v[...]).astype(BF16)
    output_g[...] = left_product(context_ref[...], second_low[...]).astype(BF16)
    fold_table(sums, sums_ref, 0, TABLE_ROWS)
    for t in range(tiles - 2, tiles):
        outer_save(t).wait()
        inner_save(t).wait()


def middle(rows, context, cot, lengths, table, output_w, inner_w, outer_w):
    count, width = rows.shape
    hidden = inner_w.shape[1]
    tile = INNER * LANES
    tiles = hidden // tile
    whole = pl.BlockSpec(memory_space=pltpu.VMEM)
    far = pl.BlockSpec(memory_space=pl.ANY)

    def space(dtype):
        return pltpu.VMEM((count, width), dtype)

    return pl.pallas_call(
        middle_kernel,
        out_shape=[
            jax.ShapeDtypeStruct((count, width), BF16),
            jax.ShapeDtypeStruct((count, width), F32),
            jax.ShapeDtypeStruct((count, width), BF16),
            jax.ShapeDtypeStruct(table.shape, F32),
            jax.ShapeDtypeStruct(output_w.shape, BF16),
            jax.ShapeDtypeStruct(inner_w.shape, BF16),
            jax.ShapeDtypeStruct(outer_w.shape, BF16),
        ],
        in_specs=[whole] * 3 + [pl.BlockSpec(memory_space=pltpu.SMEM), whole] + [far] * 3,
        out_specs=[whole] * 5 + [far] * 2,
        scratch_shapes=[
            pltpu.VMEM(output_w.shape, BF16),
            pltpu.VMEM((tiles, width, tile), BF16),
            pltpu.VMEM((tiles, tile, width), BF16),
            pltpu.VMEM((TABLE_ROWS, width), F32),
            pltpu.VMEM((TABLE_ROWS, width), F32),
            pltpu.VMEM((tiles, count, tile), BF16),
            pltpu.VMEM((tiles, count, tile), F32),
            space(F32),
            pltpu.VMEM((8, LANES), F32),
            pltpu.VMEM((count, LANES), F32),
            space(F32),
            space(BF16),
            pltpu.VMEM((width, count), BF16),
            space(F32),
            space(BF16),
            pltpu.VMEM((2, width, tile), BF16),
            pltpu.VMEM((2, tile, width), BF16),
            pltpu.SemaphoreType.DMA((3, tiles)),
            pltpu.SemaphoreType.DMA((2, 2)),
        ],
        compiler_params=pltpu.CompilerParams(vmem_limit_bytes=60 << 20),
        name="feed_forward",
    )(rows, context, cot, lengths, table, output_w, inner_w, outer_w)


def widen_kernel(splits, *refs):
    count = len(splits)
    ins, refs = refs[:count], refs[count:]
    outs = refs[: sum(splits)]
    wides, sems = refs[sum(splits) : -1], refs[-1]
    copies = []
    at = 0
    for source, parts in zip(ins, splits):
        columns = source.shape[-1] // parts
        for part in range(parts):
            wides[at][...] = source[..., part * columns : (part + 1) * columns].astype(F32)
            copies.append(pltpu.make_async_copy(wides[at], outs[at], sems.at[at]))
            copies[-1].start()
            at += 1
    for copy in copies:
        copy.wait()


def widen(arrays, splits):
    shapes = []
    for array, parts in zip(arrays, splits):
        shapes += [array.shape[:-1] + (array.shape[-1] // parts,)] * parts
    return pl.pallas_call(
        functools.partial(widen_kernel, splits),
        out_shape=[jax.ShapeDtypeStruct(shape, F32) for shape in shapes],
        in_specs=[pl.BlockSpec(memory_space=pltpu.VMEM)] * len(arrays),
        out_specs=[pl.BlockSpec(memory_space=pl.ANY)] * len(shapes),
        scratch_shapes=[pltpu.VMEM(shape, F32) for shape in shapes]
        + [pltpu.SemaphoreType.DMA((len(shapes),))],
        compiler_params=pltpu.CompilerParams(vmem_limit_bytes=40 << 20),
        name="widen_results",
    )(*arrays)


def greet_twin(place):
    barrier = pltpu.get_barrier_semaphore()
    pl.semaphore_signal(barrier, inc=1, device_id=place.twin(), device_id_type=MESH)
    pl.semaphore_wait(barrier, 1)


def stack_heads(block, lower):
    zero = jnp.zeros_like(block)
    return jnp.concatenate((jnp.where(lower, block, zero), jnp.where(lower, zero, block)), axis=0)


SPAN = 2 * HEAD_DIM


def span_of(section, pair, width):
    return pl.ds(pl.multiple_of(section * width + pair * SPAN, SPAN), SPAN)


class AttentionForward:
    def __init__(self, place, rows, weight, vec, bias, qkv, context, probs, away, tiles, send, recv, load):
        self.place, self.rows, self.weight, self.vec, self.bias = place, rows, weight, vec, bias
        self.qkv, self.context, self.probs, self.away = qkv, context, probs, away
        self.tiles, self.send, self.recv, self.load = tiles, send, recv, load
        self.count, self.width = context.shape
        self.pairs = self.width // SPAN
        self.tile = tiles.shape[2]

    def fetch_weight(self, t):
        return pltpu.make_async_copy(
            self.weight.at[:, pl.ds(t * self.tile, self.tile)], self.tiles.at[t], self.load.at[t]
        )

    def fetch(self, which, pair):
        return pltpu.make_async_remote_copy(
            self.qkv.at[:, span_of(which + 1, pair, self.width)],
            self.away.at[:, span_of(which, pair, self.width)],
            self.send.at[which, pair],
            self.recv.at[which, pair],
            device_id=self.place.twin(),
            device_id_type=MESH,
        )

    def project(self, t):
        columns = pl.ds(t * self.tile, self.tile)
        per = self.width // self.tile
        section = t // per
        self.fetch_weight(t).wait()
        product = plain_product(self.rows[...], self.tiles[t])
        if section != 1:
            row = ROW_QUERY if section == 0 else ROW_VALUE
            product = product + self.vec[pl.ds(row, 1), pl.ds((t % per) * self.tile, self.tile)]
        self.qkv[:, columns] = product.astype(BF16)

    def give(self, t):
        per = self.width // self.tile
        section = t // per
        if section:
            share = self.tile // SPAN
            for pair in range((t % per) * share, (t % per + 1) * share):
                self.fetch(section - 1, pair).start()

    def attend(self, pair):
        for which in range(2):
            self.fetch(which, pair).wait_recv()
        count = self.count
        lower = lax.broadcasted_iota(jnp.int32, (count, SPAN), 1) < HEAD_DIM

        def here(section):
            return self.qkv[:, span_of(section, pair, self.width)]

        def there(section):
            return self.away[:, span_of(section - 1, pair, self.width)]

        stacked = stack_heads(here(0) * HEAD_DIM**-0.5, lower)
        keys = jnp.concatenate((here(1), there(1)), axis=0)
        values = jnp.concatenate((here(2), there(2)), axis=0)
        scores = right_product(stacked, keys) + self.bias[:1, :]
        top = jnp.max(scores, axis=1, keepdims=True)
        weights = jnp.exp(scores - top)
        total = jnp.sum(weights, axis=1, keepdims=True)
        probs = (weights * (1.0 / total)).astype(BF16)
        self.probs[pair] = probs
        mixed = plain_product(probs, values)
        self.context[:, span_of(0, pair, self.width)] = jnp.where(
            lower, mixed[:count], mixed[count:]
        ).astype(BF16)

    def finish(self):
        for pair in range(self.pairs):
            for which in range(2):
                self.fetch(which, pair).wait_send()


def attend_kernel(
    rows_ref, lengths_ref, table_ref, weight, qkv, context, probs, away, bias_ref, tiles, vec, send, recv, load
):
    place = Place()
    rows = rows_ref.shape[0]
    length = lengths_ref[place.side, 0]
    row = lax.broadcasted_iota(jnp.int32, (8, rows), 1)
    for k, core in enumerate((place.core, 1 - place.core)):
        bias_ref[:, pl.ds(k * rows, rows)] = jnp.where(
            row_place(row, core, rows) < length, 0.0, -1e30
        )
    work = AttentionForward(
        place, rows_ref, weight, vec, bias_ref, qkv, context, probs, away, tiles, send, recv, load
    )
    count = tiles.shape[0]
    order = list(range(count // 3, count)) + list(range(count // 3))
    for t in order:
        work.fetch_weight(t).start()
    greet_twin(place)
    spread_table(table_ref, vec)
    for before, t in zip([None] + order, order):
        work.project(t)
        if before is not None:
            work.give(before)

    def step(pair, carry):
        work.attend(pair)
        return carry

    lax.fori_loop(0, work.pairs, step, 0)
    work.finish()


def attend(rows, lengths, table, weight, collective_id):
    count, width = rows.shape
    pairs = width // SPAN
    tile = 512
    tiles = weight.shape[1] // tile
    whole = pl.BlockSpec(memory_space=pltpu.VMEM)
    return pl.pallas_call(
        attend_kernel,
        out_shape=[
            jax.ShapeDtypeStruct((count, 3 * width), BF16),
            jax.ShapeDtypeStruct((count, width), BF16),
            jax.ShapeDtypeStruct((pairs, 2 * count, 2 * count), BF16),
            jax.ShapeDtypeStruct((count, 2 * width), BF16),
        ],
        in_specs=[
            whole,
            pl.BlockSpec(memory_space=pltpu.SMEM),
            whole,
            pl.BlockSpec(memory_space=pl.ANY),
        ],
        out_specs=[whole] * 4,
        scratch_shapes=[
            pltpu.VMEM((8, 2 * count), F32),
            pltpu.VMEM((tiles, width, tile), BF16),
            pltpu.VMEM((TABLE_ROWS, width), F32),
            pltpu.SemaphoreType.DMA((2, pairs)),
            pltpu.SemaphoreType.DMA((2, pairs)),
            pltpu.SemaphoreType.DMA((tiles,)),
        ],
        compiler_params=pltpu.CompilerParams(
            collective_id=collective_id, has_side_effects=True, vmem_limit_bytes=40 << 20
        ),
        name="attention_forward",
    )(rows, lengths, table, weight)


class AttentionBackward:
    def __init__(
        self, place, rows, qkv, away, probs, grad, weight, out, weight_grad, tiles, blocks, keep, leave, come, send, recv, load, save
    ):
        self.place, self.rows, self.qkv, self.away, self.probs = place, rows, qkv, away, probs
        self.grad, self.weight, self.out, self.weight_grad = grad, weight, out, weight_grad
        self.tiles, self.blocks, self.keep, self.leave, self.come = tiles, blocks, keep, leave, come
        self.send, self.recv, self.load, self.save = send, recv, load, save
        self.count, self.width = grad.shape
        self.pairs = self.width // SPAN
        self.tile = tiles.shape[2]

    def fetch_weight(self, t):
        return pltpu.make_async_copy(
            self.weight.at[:, pl.ds(t * self.tile, self.tile)], self.tiles.at[t], self.load.at[t]
        )

    def give(self, which, pair):
        return pltpu.make_async_remote_copy(
            self.leave.at[:, span_of(which, pair, self.width)],
            self.come.at[:, span_of(which, pair, self.width)],
            self.send.at[which, pair],
            self.recv.at[which, pair],
            device_id=self.place.twin(),
            device_id_type=MESH,
        )

    def attend(self, pair):
        count = self.count
        lower = lax.broadcasted_iota(jnp.int32, (count, SPAN), 1) < HEAD_DIM
        scale = HEAD_DIM**-0.5

        def here(section):
            return self.qkv[:, span_of(section, pair, self.width)]

        def there(section):
            return self.away[:, span_of(section - 1, pair, self.width)]

        first = span_of(0, pair, self.width)
        second = span_of(1, pair, self.width)
        stacked = stack_heads(here(0) * scale, lower)
        keys = jnp.concatenate((here(1), there(1)), axis=0)
        values = jnp.concatenate((here(2), there(2)), axis=0)
        grad = stack_heads(self.grad[:, first], lower)
        probs = self.probs[pair]
        value_part = left_product(probs, grad)
        probs_grad = right_product(grad, values)
        wide = probs.astype(F32)
        inner = jnp.sum(wide * probs_grad, axis=1, keepdims=True)
        scores_grad = (wide * (probs_grad - inner)).astype(BF16)
        key_part = left_product(scores_grad, stacked)
        self.leave[:, first] = key_part[count:].astype(BF16)
        self.leave[:, second] = value_part[count:].astype(BF16)
        self.keep[:, first] = key_part[:count]
        self.keep[:, second] = value_part[:count]
        mixed = plain_product(scores_grad, keys) * scale
        self.out[:, first] = jnp.where(lower, mixed[:count], mixed[count:]).astype(BF16)
        for which in range(2):
            self.give(which, pair).start()

    def settle(self, pair):
        for which in range(2):
            self.give(which, pair).wait_recv()
            here = span_of(which, pair, self.width)
            self.out[:, span_of(which + 1, pair, self.width)] = (
                self.keep[:, here] + self.come[:, here].astype(F32)
            ).astype(BF16)

    def weigh(self, t, rows_t):
        columns = pl.ds(t * self.tile, self.tile)
        self.blocks[t] = plain_product(rows_t, self.out[:, columns]).astype(BF16)

    def save_weight(self, t):
        return pltpu.make_async_copy(
            self.blocks.at[t], self.weight_grad.at[:, pl.ds(t * self.tile, self.tile)], self.save.at[t]
        )

    def spread(self, t):
        columns = pl.ds(t * self.tile, self.tile)
        self.fetch_weight(t).wait()
        return right_product(self.out[:, columns], self.tiles[t])

    def bias_sums(self, sums):
        sums[pl.ds(ROW_QUERY, 1), :] = total_rows(self.out[:, : self.width])
        sums[pl.ds(ROW_VALUE, 1), :] = total_rows(self.out[:, 2 * self.width :])

    def finish(self):
        for pair in range(self.pairs):
            for which in range(2):
                self.give(which, pair).wait_send()


def attend_back_kernel(
    rows_ref, qkv, away, probs, grad, first_grad, table_ref, weight,
    weight_grad, input_grad, sums_ref,
    out, tiles, blocks, keep, leave, come, total, sums, rows_t, send, recv, load, save,
):
    place = Place()
    work = AttentionBackward(
        place, rows_ref, qkv, away, probs, grad, weight, out, weight_grad, tiles, blocks,
        keep, leave, come, send, recv, load, save,
    )
    count = tiles.shape[0]
    for t in range(count):
        work.fetch_weight(t).start()
    greet_twin(place)

    def step(pair, carry):
        work.attend(pair)
        return carry

    lax.fori_loop(0, work.pairs, step, 0)
    rows_t[...] = rows_ref[...].T
    total[...] = first_grad[...]
    for t in range(count):
        if t == count // 3:

            def settle(pair, carry):
                work.settle(pair)
                return carry

            lax.fori_loop(0, work.pairs, settle, 0)
        work.weigh(t, rows_t[...])
        if t:
            work.save_weight(t - 1).start()
        total[...] += work.spread(t)
    work.save_weight(count - 1).start()
    input_grad[...] = total[...].astype(BF16)
    work.bias_sums(sums)
    sums_ref[...] = table_ref[...]
    fold_table(sums, sums_ref, ROW_QUERY, 2)
    for t in range(count):
        work.save_weight(t).wait()
    work.finish()


def attend_back(rows, saved, grad, first_grad, table, weight, collective_id):
    qkv, away, probs = saved
    count, width = rows.shape
    pairs = width // SPAN
    tile = 512
    tiles = weight.shape[1] // tile
    whole = pl.BlockSpec(memory_space=pltpu.VMEM)
    far = pl.BlockSpec(memory_space=pl.ANY)
    return pl.pallas_call(
        attend_back_kernel,
        out_shape=[
            jax.ShapeDtypeStruct(weight.shape, BF16),
            jax.ShapeDtypeStruct((count, width), BF16),
            jax.ShapeDtypeStruct(table.shape, F32),
        ],
        in_specs=[whole] * 7 + [far],
        out_specs=[far, whole, whole],
        scratch_shapes=[
            pltpu.VMEM((count, 3 * width), BF16),
            pltpu.VMEM((tiles, width, tile), BF16),
            pltpu.VMEM((tiles, width, tile), BF16),
            pltpu.VMEM((count, 2 * width), F32),
            pltpu.VMEM((count, 2 * width), BF16),
            pltpu.VMEM((count, 2 * width), BF16),
            pltpu.VMEM((count, width), F32),
            pltpu.VMEM((TABLE_ROWS, width), F32),
            pltpu.VMEM((width, count), BF16),
            pltpu.SemaphoreType.DMA((2, pairs)),
            pltpu.SemaphoreType.DMA((2, pairs)),
            pltpu.SemaphoreType.DMA((tiles,)),
            pltpu.SemaphoreType.DMA((tiles,)),
        ],
        compiler_params=pltpu.CompilerParams(
            collective_id=collective_id, has_side_effects=True, vmem_limit_bytes=60 << 20
        ),
        name="attention_backward",
    )(rows, qkv, away, probs, grad, first_grad, table, weight)


def exact_gelu(hidden):
    return jax.nn.gelu(hidden, approximate=False)


def plain_product(left, right):
    return jnp.dot(left, right, preferred_element_type=F32)


def left_product(left, right):
    return lax.dot_general(left, right, (((0,), (0,)), ((), ())), preferred_element_type=F32)


def right_product(left, right):
    return lax.dot_general(left, right, (((1,), (1,)), ((), ())), preferred_element_type=F32)


def column_sums(rows):
    return jnp.sum(rows.astype(F32), axis=0)


def norm_parts(total):
    average = jnp.mean(total, axis=-1, keepdims=True)
    centered = total - average
    variance = jnp.mean(centered * centered, axis=-1, keepdims=True)
    rate = lax.rsqrt(variance + EPSILON)
    return centered * rate, rate


def norm_back(unit, rate, grad):
    return rate * (
        grad
        - jnp.mean(grad, axis=-1, keepdims=True)
        - unit * jnp.mean(grad * unit, axis=-1, keepdims=True)
    )


def split_columns(packed, widths):
    pieces = []
    start = 0
    for width in widths:
        pieces.append(packed[..., start : start + width])
        start += width
    return pieces


def native_forward(queries, keys_all, values_all, key_valid, heads):
    shape = queries.shape[:2] + (heads, HEAD_DIM)
    key_shape = keys_all.shape[:2] + (heads, HEAD_DIM)
    scores = jnp.einsum(
        "sqhd,skhd->shqk",
        queries.reshape(shape),
        keys_all.reshape(key_shape),
        preferred_element_type=F32,
    ) * (HEAD_DIM**-0.5)
    scores = jnp.where(key_valid[:, None, None, :], scores, -1e30)
    top = jnp.max(scores, axis=-1, keepdims=True)
    weights = jnp.exp(scores - top)
    probs = (weights / jnp.sum(weights, axis=-1, keepdims=True)).astype(BF16)
    context = jnp.einsum(
        "shqk,skhd->sqhd", probs, values_all.reshape(key_shape), preferred_element_type=F32
    )
    return context.reshape(queries.shape).astype(BF16), probs


def native_backward(queries, keys_all, values_all, probs, context_grad, heads):
    shape = queries.shape[:2] + (heads, HEAD_DIM)
    key_shape = keys_all.shape[:2] + (heads, HEAD_DIM)
    scale = HEAD_DIM**-0.5
    grad_heads = context_grad.reshape(shape)
    wide = probs.astype(F32)
    probs_grad = jnp.einsum(
        "sqhd,skhd->shqk", grad_heads, values_all.reshape(key_shape), preferred_element_type=F32
    )
    inner_total = jnp.sum(wide * probs_grad, axis=-1, keepdims=True)
    scores_grad = (wide * (probs_grad - inner_total)).astype(BF16)
    query_grad = jnp.einsum(
        "shqk,skhd->sqhd", scores_grad, keys_all.reshape(key_shape), preferred_element_type=F32
    )
    key_part = jnp.einsum(
        "shqk,sqhd->skhd", scores_grad, queries.reshape(shape), preferred_element_type=F32
    )
    value_part = jnp.einsum("shqk,sqhd->skhd", probs, grad_heads, preferred_element_type=F32)
    return (
        (query_grad * scale).astype(BF16).reshape(queries.shape),
        (key_part * scale).astype(BF16).reshape(keys_all.shape),
        value_part.astype(BF16).reshape(values_all.shape),
    )


def gather_rows(part):
    return lax.all_gather(part, "fsdp", axis=0, tiled=True)


def reduce_rows(part):
    share = lax.psum_scatter(part.astype(BF16), "fsdp", scatter_dimension=0, tiled=True)
    return lax.psum(share, "ctx").astype(F32)


def layer(flat_rows, cot_rows, row_mask, packed, widths, weights, forward, backward):
    full_qkv, full_output, full_inner, full_outer = weights
    rows, width = flat_rows.shape
    shards = packed.shape[0]
    (
        bias_query,
        bias_value,
        bias_output,
        gain_first,
        shift_first,
        bias_inner,
        bias_outer,
        gain_second,
        shift_second,
    ) = [piece.reshape(-1).astype(F32) for piece in split_columns(packed, widths)]
    bias_qkv = jnp.concatenate((bias_query, jnp.zeros_like(bias_query), bias_value))
    qkv = (plain_product(flat_rows, full_qkv) + bias_qkv).astype(BF16)
    context, saved = forward(qkv)

    first_sum = flat_rows.astype(F32) + plain_product(context, full_output) + bias_output
    first_unit, first_rate = norm_parts(first_sum)
    normed = first_unit * gain_first + shift_first
    normed_low = normed.astype(BF16)
    hidden = plain_product(normed_low, full_inner) + bias_inner
    active, gelu_back = jax.vjp(exact_gelu, hidden)
    active_low = active.astype(BF16)
    second_sum = normed + plain_product(active_low, full_outer) + bias_outer
    second_unit, second_rate = norm_parts(second_sum)
    output = ((second_unit * gain_second + shift_second) * row_mask).astype(BF16)

    out_grad = cot_rows.astype(F32) * row_mask
    second_gain_part = jnp.sum(out_grad * second_unit, axis=0)
    second_shift_part = jnp.sum(out_grad, axis=0)
    second_grad = norm_back(second_unit, second_rate, out_grad * gain_second)
    second_low = second_grad.astype(BF16)
    outer_weight_part = left_product(active_low, second_low).astype(BF16)
    outer_bias_part = column_sums(second_low)
    (hidden_grad,) = gelu_back(right_product(second_low, full_outer))
    hidden_low = hidden_grad.astype(BF16)
    inner_weight_part = left_product(normed_low, hidden_low).astype(BF16)
    inner_bias_part = column_sums(hidden_low)
    normed_grad = second_grad + right_product(hidden_low, full_inner)
    first_gain_part = jnp.sum(normed_grad * first_unit, axis=0)
    first_shift_part = jnp.sum(normed_grad, axis=0)
    first_grad = norm_back(first_unit, first_rate, normed_grad * gain_first)
    branch_low = first_grad.astype(BF16)
    output_weight_part = left_product(context, branch_low).astype(BF16)
    output_bias_part = column_sums(branch_low)
    context_grad = right_product(branch_low, full_output).astype(BF16)
    qkv_grad = backward(saved, context_grad)
    qkv_weight_part = left_product(flat_rows, qkv_grad).astype(BF16)
    query_bias_part = column_sums(qkv_grad[:, :width])
    value_bias_part = column_sums(qkv_grad[:, 2 * width :])
    input_grad = first_grad + right_product(qkv_grad, full_qkv)
    vector_parts = (
        query_bias_part,
        value_bias_part,
        output_bias_part,
        first_gain_part,
        first_shift_part,
        inner_bias_part,
        outer_bias_part,
        second_gain_part,
        second_shift_part,
    )
    packed_parts = jnp.concatenate([part.reshape(shards, -1) for part in vector_parts], axis=1)
    return (
        output,
        input_grad,
        packed_parts,
        (qkv_weight_part, output_weight_part, inner_weight_part, outer_weight_part),
    )


def native_body(inputs, cotangent, lengths, vectors, weights):
    widths = [member.shape[0] for member in vectors]
    packed = lax.all_gather(jnp.concatenate(vectors), "fsdp", axis=0, tiled=False)
    joined = (jnp.concatenate(weights[:3], axis=1),) + weights[3:]
    full = tuple(gather_rows(part) for part in joined)
    micro, seqs, block_len, width = inputs.shape
    heads = width // HEAD_DIM
    total_slots = block_len * lax.axis_size("ctx")
    group = micro * seqs
    rows = group * block_len
    flat_len = lengths.reshape(group)
    local_pos = lax.axis_index("ctx") * block_len + jnp.arange(block_len, dtype=jnp.int32)
    row_mask = (local_pos[None, :] < flat_len[:, None]).astype(F32).reshape(rows, 1)
    key_valid = jnp.arange(total_slots, dtype=jnp.int32)[None, :] < flat_len[:, None]

    def forward(qkv):
        queries = qkv[:, :width].reshape(group, block_len, width)
        keys_values = lax.all_gather(
            qkv[:, width:].reshape(group, block_len, 2 * width), "ctx", axis=1, tiled=True
        )
        keys, values = keys_values[:, :, :width], keys_values[:, :, width:]
        context, probs = native_forward(queries, keys, values, key_valid, heads)
        return context.reshape(rows, width), (queries, keys, values, probs)

    def backward(saved, context_grad):
        query_grad, key_part, value_part = native_backward(
            *saved, context_grad.reshape(group, block_len, width), heads
        )
        keys_values_grad = lax.psum_scatter(
            jnp.concatenate((key_part, value_part), axis=2), "ctx", scatter_dimension=1, tiled=True
        )
        return jnp.concatenate(
            (query_grad.reshape(rows, width), keys_values_grad.reshape(rows, 2 * width)), axis=1
        )

    output, input_grad, packed_parts, parts = layer(
        inputs.reshape(rows, width),
        cotangent.reshape(rows, width),
        row_mask,
        packed,
        widths,
        full,
        forward,
        backward,
    )
    share = lax.psum_scatter(packed_parts, "fsdp", scatter_dimension=0, tiled=True)
    return (
        output.reshape(inputs.shape),
        input_grad.reshape(inputs.shape),
        lax.psum(share, "ctx")[0],
        tuple(split_columns(reduce_rows(parts[0]), [width] * 3))
        + tuple(reduce_rows(part) for part in parts[1:]),
    )


def direct_body(inputs, cotangent, lengths, vectors, weights):
    micro, seqs, block_len, width = inputs.shape
    shards = LINE * PAIR
    rows = 2 * block_len
    table = jnp.zeros((TABLE_ROWS, LANES), F32)
    row = 0
    for vector in vectors:
        lines = vector.shape[0] // LANES
        filled = ((row, TABLE_ROWS - row - lines), (0, 0))
        table += jnp.pad(vector.astype(F32).reshape(lines, LANES), filled)
        row += lines
    query_weight, key_weight, value_weight, output_weight, inner_weight, outer_weight = weights
    blocks = (inputs.reshape(micro, block_len, width), cotangent.reshape(micro, block_len, width))
    shard_rows, hidden = inner_weight.shape
    flows = [Flow(0, TABLE_ROWS, lambda core, side: (0, TABLE_ROWS, 0, LANES), cores=False)]
    flows += column_flows(1, shard_rows, 3 * width, *GATHER_SPLIT[0])
    flows += column_flows(2, shard_rows, width, *GATHER_SPLIT[1])
    flows += column_flows(3, shard_rows, hidden, *GATHER_SPLIT[2])
    flows += row_flows(4, hidden // shards, width, *GATHER_SPLIT[3])
    tables, full_qkv, full_output, full_inner, full_outer, in_rows, cot_rows = gather_call(
        (table.astype(BF16),) + weights,
        ((0, 0), (1, 0), (1, width), (1, 2 * width), (2, 0), (3, 0), (4, 0)),
        blocks,
        flows,
        shards,
        1,
        GATHER_ORDER,
    )
    in_rows = in_rows.reshape(rows, width)
    cot_rows = cot_rows.reshape(rows, width)
    qkv, context, probs, away = attend(in_rows, lengths, tables, full_qkv, 3)
    output, first_grad, context_grad, table_grad, output_part, inner_part, outer_part = middle(
        in_rows, context, cot_rows, lengths, tables, full_output, full_inner, full_outer
    )
    qkv_part, input_grad, table_grad = attend_back(
        in_rows, (qkv, away, probs), context_grad, first_grad, table_grad, full_qkv, 4
    )
    sums = reduce_call(
        (inner_part, outer_part, output_part, qkv_part, table_grad),
        (
            output.reshape(micro, block_len, width),
            input_grad.reshape(micro, block_len, width),
        ),
        [
            column_part(shard_rows, hidden, *REDUCE_SPLIT[0]),
            row_part(hidden // shards, width, *REDUCE_SPLIT[1]),
            column_part(shard_rows, width, *REDUCE_SPLIT[2]),
            column_part(shard_rows, 3 * width, *REDUCE_SPLIT[3]),
            vector_part(TABLE_ROWS, LANES),
        ],
        2,
        REDUCE_ORDER,
    )
    inner_share, outer_share, output_share, qkv_share, table_share, outs, grads = sums
    wide = widen((qkv_share, output_share, inner_share, outer_share, grads), (3, 1, 1, 1, 1))
    return (
        outs.reshape(inputs.shape),
        wide[6].reshape(inputs.shape),
        table_share.reshape(-1),
        tuple(wide[:6]),
    )


def body(
    inputs,
    cotangent,
    lengths,
    query_weight,
    key_weight,
    value_weight,
    output_weight,
    query_bias,
    value_bias,
    output_bias,
    first_gain,
    first_shift,
    inner_weight,
    inner_bias,
    outer_weight,
    outer_bias,
    second_gain,
    second_shift,
):
    vectors = (
        query_bias,
        value_bias,
        output_bias,
        first_gain,
        first_shift,
        inner_bias,
        outer_bias,
        second_gain,
        second_shift,
    )
    widths = [member.shape[0] for member in vectors]
    weights = (
        query_weight,
        key_weight,
        value_weight,
        output_weight,
        inner_weight,
        outer_weight,
    )
    laid_out = lax.axis_size("fsdp") == LINE * PAIR and lax.axis_size("ctx") == 4
    whole_lines = all(extent % LANES == 0 for extent in widths)
    direct = laid_out and inputs.shape[:2] == (2, 1) and whole_lines
    run = direct_body if direct else native_body
    output, input_grad, vector_share, weight_shares = run(
        inputs, cotangent, lengths, vectors, weights
    )
    shares = split_columns(vector_share, widths)
    query_share, key_share, value_share, output_share, inner_share, outer_share = weight_shares
    return (
        output,
        input_grad,
        query_share,
        key_share,
        value_share,
        output_share,
        shares[0],
        shares[1],
        shares[2],
        shares[3],
        shares[4],
        inner_share,
        shares[5],
        outer_share,
        shares[6],
        shares[7],
        shares[8],
    )


def solution(mesh):
    data = P(None, "fsdp", "ctx", None)
    matrix = P("fsdp", None)
    vector = P("fsdp")
    return jax.shard_map(
        body,
        mesh=mesh,
        in_specs=(data, data, P(None, "fsdp"))
        + (matrix,) * 4
        + (vector,) * 5
        + (matrix, vector, matrix, vector, vector, vector),
        out_specs=(data, data)
        + (matrix,) * 4
        + (vector,) * 5
        + (matrix, vector, matrix, vector, vector, vector),
        check_vma=False,
    )
```

profile of v0, /device:TPU:1, one launch (start us, length us, event | category | flops | bytes accessed | tf_op | source)
XLA Modules:
  0.0 322.4 jit_solution(4203545920196380669)
XLA Ops:
  0.7 0.7 copy.35.lengths_ref
  1.4 0.0 copy-start.12
  1.4 1.4 add_convert_fusion.refs_0_
  2.8 107.0 %gather_weights.1 = (bf16[128,128]{1,0:T(8,128)(2,1)}, bf16[1024,3072]{1,0:T(8,128)(2,1)}, bf16[1024,1024]{1,0:T(8,128)(2,1)}, bf16[1024,4096]{1,0:T(8,128)(2,1)...) custom-call(bf16[16,128]{1,0:T(8,128)(2,1)} %add_convert_fusion.refs_0_, ...), custom_call_target="tpu_custom_call" | custom-call | tf_op jit(solution)/shard_map/gather_weights/pallas_call | solution.py:384
  109.8 0.0 copy-start
  109.8 2.8 copy-done
  112.6 0.0 copy-start.1
  112.6 1.0 copy-done.1
  113.6 0.0 copy-start.11
  113.6 0.8 copy-done.11
  114.4 12.6 %attention_forward.1 = (bf16[256,3072]{1,0:T(8,128)(2,1)S(1)}, bf16[256,1024]{1,0:T(8,128)(2,1)S(1)}, bf16[8,512,512]{2,1,0:T(8,128)(2,1)S(1)}, bf16[256,2048]{1,0:T(8,128)(2,1)S(1)}) custom-call(bf16[256,1024]{1,0:T(8,128)(2,1)S(1)} %bitcast.41, s32[2,1]{1,0:T(2,128)S(1)} %copy.35.lengths_ref, bf16[128,128]{1,0:T(8,128)(2,1)S(1)} %copy-done.11, ...), custom_call_target="tpu_custom_call" | custom-call | tf_op jit(solution)/shard_map/attention_forward/pallas_call | solution.py:1333
  127.0 0.0 copy-start.2
  127.1 2.0 copy-done.2
  129.1 0.0 copy-start.3
  129.1 1.1 copy-done.3
  130.2 0.0 copy-start.6
  130.2 1.0 copy-done.6
  131.2 0.0 copy-start.9
  131.2 0.8 copy-done.9
  132.0 0.0 copy-done.12
  132.0 33.3 %feed_forward.1 = (bf16[256,1024]{1,0:T(8,128)(2,1)}, f32[256,1024]{1,0:T(8,128)}, bf16[256,1024]{1,0:T(8,128)(2,1)}, f32[128,128]{1,0:T(8,128)}, bf16[1024,1024...) custom-call(bf16[256,1024]{1,0:T(8,128)(2,1)} %bitcast.39, bf16[256,1024]{1,0:T(8,128)(2,1)} %copy-done.9, ...), custom_call_target="tpu_custom_call" | custom-call | tf_op jit(solution)/shard_map/feed_forward/pallas_call | solution.py:1128
  165.4 19.0 %attention_backward.1 = (bf16[1024,3072]{1,0:T(8,128)(2,1)}, bf16[256,1024]{1,0:T(8,128)(2,1)}, f32[128,128]{1,0:T(8,128)}) custom-call(bf16[256,1024]{1,0:T(8,128)(2,1)} %bitcast.40, bf16[256,3072]{1,0:T(8,128)(2,1)} %copy-done.3, bf16[256,2048]{1,0:T(8,128)(2,1)} %copy-done.6, bf16[8,512,512]{2,1,0:T(8,128)(2,1)} %copy-done.2, ...), custom_call_target="tpu_custom_call" | custom-call | tf_op jit(solution)/shard_map/attention_backward/pallas_call | solution.py:1507
  184.4 124.8 %reduce_gradients.1 = (bf16[128,4096]{1,0:T(8,128)(2,1)}, bf16[512,1024]{1,0:T(8,128)(2,1)}, bf16[128,1024]{1,0:T(8,128)(2,1)}, bf16[128,3072]{1,0:T(8,128)(2,1)...) custom-call(bf16[1024,4096]{1,0:T(8,128)(2,1)} %get-tuple-element.60.refs_0_, ...), custom_call_target="tpu_custom_call" | custom-call | tf_op jit(solution)/shard_map/reduce_gradients/pallas_call | solution.py:853
  309.2 1.3 slice_bitcast_fusion
  310.5 1.4 slice_bitcast_fusion.1
  311.9 1.2 copy-done.4
  313.1 1.2 copy-done.5
  314.4 1.1 copy-done.7
  315.5 1.0 copy-done.8
  316.5 0.9 copy-done.10
  317.5 3.1 widen_results.1
  320.6 1.9 copy.40
  (5 shorter events, 0.0 us)
Async XLA Ops:
  1.4 130.6 %copy-start.12 = (s32[2,1]{1,0:T(2,128)}, s32[2,1]{1,0:T(2,128)S(1)}, u32[]{:S(2)}) copy-start(s32[2,1]{1,0:T(2,128)S(1)} %copy.35.lengths_ref) | copy-start | bytes 28
  109.8 2.8 copy-start
  112.6 1.0 copy-start.1
  113.6 0.8 copy-start.11
  127.0 2.0 copy-start.2
  129.1 1.1 copy-start.3
  130.2 1.0 copy-start.6
  131.2 0.8 copy-start.9
  311.9 1.2 copy-start.4
  313.1 1.2 copy-start.5
  314.4 1.1 copy-start.7
  315.5 1.0 copy-start.8
  316.5 0.9 copy-start.10
where the time goes:
time: 323 us; the launch traced here: 322 us
  Pallas kernels  300 us (93%)
  local copies, waits for them, and re-layouts  20.4 us (6%)
    pallas_call x1, Pallas kernels, reduce_call(): pl.pallas_call(functools.partial(reduce_kernel, parts, len(blocks), order...  125 us
    pallas_call x1, Pallas kernels, gather_call(): pl.pallas_call(functools.partial(gather_kernel, flows, spots, len(blocks)...  107 us
    pallas_call x1, Pallas kernels, middle(): pl.pallas_call(middle_kernel, out_shape=[jax.ShapeDtypeStruct((count, wid...  33.3 us
    pallas_call x1, Pallas kernels, attend_back(): pl.pallas_call(attend_back_kernel, out_shape=[jax.ShapeDtypeStruct(weight...  19 us
    unnamed x28, local copies, waits for them, and re-layouts  17.7 us
    pallas_call x1, Pallas kernels, attend(): pl.pallas_call(attend_kernel, out_shape=[jax.ShapeDtypeStruct((count, 3 *...  12.6 us

commit v1 on v0

--- a/solution.py
+++ b/solution.py
@@ -12,36 +12,35 @@
 F32 = jnp.float32
 BF16 = jnp.bfloat16
 
-GATHER_SPLIT = ((256, 384), (256, 128), (512, 384), (160, 32))
-REDUCE_SPLIT = ((768, 256), (128, 48), (256, 128), (1024, 128))
+GATHER_SPLIT = ((512, 0), (256, 0), (256, 384), (128, 32))
+REDUCE_SPLIT = ((768, 512), (128, 32), (256, 128), (768, 256))
 GATHER_ORDER = (
-    0, 1, 9, 2, 3, 4, 13, 5, 6, 7, 10, 8, 11, 70, 32, 71, 69, 18, 35, 75, 33, 31, 76, 14, 16, 38,
-    34, 41, 48, 37, 40, 12, 73, 22, 21, 17, 46, 78, 74, 24, 89, 43, 19, 81, 79, 107, 15, 27, 20,
-    39, 45, 83, 72, 50, 23, 77, 86, 88, 36, 42, 29, 145, 108, 57, 146, 26, 84, 109, 147, 92, 54,
-    111, 94, 30, 44, 80, 25, 55, 149, 114, 60, 62, 51, 113, 90, 95, 82, 152, 151, 116, 52, 110,
-    47, 154, 97, 56, 87, 100, 117, 96, 155, 119, 49, 157, 150, 105, 59, 148, 85, 67, 121, 124,
-    221, 93, 126, 28, 98, 159, 222, 112, 115, 53, 160, 102, 153, 162, 156, 183, 122, 184, 223, 63,
-    165, 185, 58, 168, 130, 225, 187, 120, 158, 91, 127, 65, 164, 101, 103, 132, 227, 190, 128,
-    228, 138, 166, 171, 189, 61, 186, 224, 133, 240, 99, 64, 241, 176, 230, 191, 188, 170, 231,
-    118, 226, 229, 106, 202, 242, 204, 131, 161, 136, 247, 192, 66, 169, 193, 232, 141, 181, 123,
-    172, 143, 174, 173, 209, 129, 68, 194, 163, 125, 246, 212, 233, 167, 135, 211, 248, 250, 178,
-    205, 203, 195, 210, 235, 140, 249, 104, 200, 198, 179, 134, 234, 208, 182, 238, 244, 213, 137,
-    206, 139, 177, 197, 243, 144, 180, 252, 257, 142, 236, 219, 239, 217, 201, 196, 254, 207, 214,
-    199, 245, 251, 215, 255, 258, 175, 237, 253, 216, 256, 218, 220, 259,
+    5, 6, 2, 0, 1, 3, 9, 13, 64, 29, 10, 4, 81, 30, 26, 62, 36, 7, 47, 149, 75, 70, 53, 94, 14,
+    104, 11, 32, 82, 27, 79, 217, 143, 46, 33, 218, 35, 24, 49, 28, 162, 16, 160, 63, 71, 38, 132,
+    131, 67, 34, 115, 200, 60, 172, 41, 8, 98, 21, 96, 201, 101, 58, 84, 66, 138, 68, 189, 100,
+    69, 109, 50, 103, 135, 113, 80, 106, 97, 164, 163, 130, 40, 211, 54, 120, 45, 22, 152, 169,
+    166, 126, 23, 31, 74, 116, 72, 83, 144, 89, 61, 212, 148, 183, 198, 76, 171, 174, 139, 147,
+    114, 12, 153, 137, 177, 118, 77, 168, 161, 206, 203, 173, 136, 199, 154, 55, 215, 65, 121,
+    155, 91, 110, 230, 99, 142, 134, 228, 216, 39, 181, 95, 105, 78, 184, 48, 37, 165, 73, 150,
+    223, 178, 188, 229, 19, 102, 167, 17, 182, 85, 128, 140, 87, 186, 15, 51, 25, 170, 156, 108,
+    133, 205, 207, 145, 119, 175, 220, 59, 57, 194, 86, 52, 204, 43, 157, 56, 151, 232, 122, 233,
+    234, 90, 210, 129, 185, 20, 123, 42, 127, 141, 196, 125, 190, 235, 18, 159, 221, 44, 202, 117,
+    176, 92, 224, 236, 107, 111, 208, 237, 222, 213, 88, 179, 197, 158, 231, 191, 225, 238, 193,
+    214, 209, 112, 124, 219, 187, 180, 239, 226, 195, 192, 146, 93, 227, 240,
 )
 REDUCE_ORDER = (
-    0, 1, 9, 2, 3, 4, 5, 6, 7, 8, 10, 11, 32, 34, 220, 30, 218, 12, 14, 216, 13, 18, 28, 25, 15,
-    17, 214, 16, 19, 20, 23, 21, 22, 31, 217, 24, 221, 29, 215, 33, 219, 222, 35, 36, 37, 27, 38,
-    42, 223, 224, 226, 40, 43, 39, 225, 227, 85, 228, 41, 87, 84, 45, 86, 51, 44, 47, 88, 53, 89,
-    90, 69, 70, 67, 68, 133, 46, 137, 26, 135, 136, 73, 74, 138, 57, 55, 165, 134, 71, 72, 166,
-    168, 167, 139, 170, 171, 169, 59, 92, 91, 118, 119, 48, 94, 77, 49, 93, 75, 76, 63, 78, 54,
-    79, 80, 81, 229, 61, 100, 116, 117, 95, 102, 96, 141, 140, 52, 122, 110, 123, 58, 120, 121,
-    106, 126, 97, 143, 56, 142, 124, 125, 112, 173, 104, 172, 108, 128, 98, 127, 145, 144, 174,
-    151, 157, 153, 199, 175, 129, 155, 161, 130, 197, 159, 203, 146, 183, 147, 198, 60, 149, 177,
-    181, 185, 201, 189, 200, 202, 193, 176, 187, 62, 204, 101, 50, 64, 207, 208, 65, 205, 82, 103,
-    178, 179, 206, 105, 152, 148, 150, 209, 107, 210, 211, 109, 131, 191, 156, 111, 154, 182, 83,
-    184, 160, 158, 188, 113, 114, 99, 186, 192, 180, 190, 212, 162, 163, 194, 195, 66, 213, 115,
-    164, 132, 196, 230,
+    30, 232, 8, 29, 7, 84, 33, 15, 0, 6, 231, 9, 10, 18, 85, 14, 233, 1, 35, 2, 41, 134, 234, 235,
+    118, 87, 86, 91, 92, 119, 12, 236, 51, 137, 42, 34, 36, 89, 28, 237, 31, 11, 19, 133, 3, 240,
+    215, 52, 37, 238, 27, 21, 93, 88, 141, 122, 214, 94, 140, 22, 20, 106, 219, 23, 43, 100, 53,
+    38, 239, 166, 44, 17, 69, 4, 165, 116, 13, 120, 138, 167, 95, 26, 39, 110, 104, 101, 123, 221,
+    217, 149, 25, 157, 222, 108, 45, 67, 173, 68, 90, 32, 172, 96, 136, 16, 135, 117, 54, 24, 71,
+    46, 183, 124, 126, 197, 5, 220, 199, 200, 169, 224, 102, 241, 40, 103, 57, 121, 216, 170, 198,
+    184, 151, 143, 242, 75, 72, 70, 105, 174, 55, 47, 63, 168, 243, 58, 73, 187, 74, 153, 223,
+    139, 127, 61, 125, 181, 185, 150, 48, 218, 76, 49, 109, 175, 128, 59, 154, 159, 205, 171, 56,
+    226, 97, 107, 145, 225, 201, 177, 202, 176, 142, 152, 182, 98, 50, 62, 227, 189, 155, 111, 77,
+    203, 60, 191, 207, 193, 178, 206, 179, 129, 158, 130, 79, 161, 204, 78, 228, 112, 156, 144,
+    188, 131, 209, 186, 64, 99, 65, 160, 180, 113, 208, 114, 132, 192, 190, 162, 163, 80, 81, 146,
+    147, 210, 66, 211, 229, 194, 82, 164, 195, 148, 212, 115, 83, 196, 213, 230,
 )
 
 MESH = pl.DeviceIdType.MESH
@@ -292,13 +291,16 @@
                     found.append(
                         (("side", n, spot), lambda n=n, spot=spot: self.arrive_side(n, spot))
                     )
-        found.append((("last",), self.finish))
         return found
 
-    def finish(self):
+    def wait_twins(self, arrays):
         for number, flow in enumerate(self.flows):
-            for spot in positions(flow.order):
-                self.arrive_twin(number, spot)
+            if flow.array in arrays:
+                for spot in positions(flow.order):
+                    self.arrive_twin(number, spot)
+
+    def finish(self, arrays):
+        self.wait_twins(arrays)
         for conditions, copy in self.sent:
             when(conditions, copy.wait_send)
 
@@ -333,71 +335,6 @@
 
 def swap_scratch(count):
     return [pltpu.SemaphoreType.DMA((count,))] * 3
-
-
-def gather_kernel(flows, spots, blocks, order, *refs):
-    count = max(array for array, _ in spots) + 1
-    shares, refs = refs[: len(spots)], refs[len(spots) :]
-    ins, refs = refs[:blocks], refs[blocks:]
-    fulls, refs = refs[:count], refs[count:]
-    outs, refs = refs[:blocks], refs[blocks:]
-    owns, refs = refs[:count], refs[count:]
-    send, recv, local, load = refs[:4]
-    place = Place()
-    loads = [
-        pltpu.make_async_copy(
-            share, owns[array].at[:, pl.ds(column, share.shape[1])], load.at[k]
-        )
-        for k, (share, (array, column)) in enumerate(zip(shares, spots))
-    ]
-    for copy in loads:
-        copy.start()
-    keep = [
-        pltpu.make_async_copy(
-            own, full.at[pl.ds(place.shard * own.shape[0], own.shape[0]), :], local.at[k]
-        )
-        for k, (own, full) in enumerate(zip(owns, fulls))
-    ]
-    greet(place)
-    for copy in loads:
-        copy.wait()
-    swap = Swap(place, ins, outs, *refs[4:])
-    swap.start()
-    work = Gather(place, flows, owns, fulls, send, recv)
-    for copy in keep:
-        copy.start()
-    for step in in_order(work.actions(), order):
-        step()
-    for copy in keep:
-        copy.wait()
-    swap.finish()
-
-
-def gather_call(shares, spots, blocks, flows, shards, collective_id, order=None):
-    labels = gather_labels(flows)
-    count = max(array for array, _ in spots) + 1
-    shapes = []
-    for array in range(count):
-        members = [share for share, spot in zip(shares, spots) if spot[0] == array]
-        shapes.append((members[0].shape[0], sum(m.shape[1] for m in members)))
-    far = pl.BlockSpec(memory_space=pl.ANY)
-    return pl.pallas_call(
-        functools.partial(gather_kernel, flows, spots, len(blocks), order),
-        out_shape=[jax.ShapeDtypeStruct((shards * r, c), BF16) for r, c in shapes]
-        + [jax.ShapeDtypeStruct(b.shape, b.dtype) for b in blocks],
-        in_specs=[far] * (len(shares) + len(blocks)),
-        out_specs=[far] * (count + len(blocks)),
-        scratch_shapes=[pltpu.VMEM(shape, BF16) for shape in shapes]
-        + [
-            pltpu.SemaphoreType.DMA((len(labels.numbers),)),
-            pltpu.SemaphoreType.DMA((len(labels.numbers),)),
-            pltpu.SemaphoreType.DMA((count,)),
-            pltpu.SemaphoreType.DMA((len(shares),)),
-        ]
-        + swap_scratch(len(blocks)),
-        compiler_params=pltpu.CompilerParams(collective_id=collective_id, has_side_effects=True),
-        name="gather_weights",
-    )(*shares, *blocks)
 
 
 def column_flows(array, shard_rows, columns, shared, early):
@@ -457,8 +394,9 @@
 
 
 class Part:
-    def __init__(self, rows, columns, along, flows, dtype=BF16):
+    def __init__(self, rows, columns, along, flows, dtype=BF16, inside=False):
         self.rows, self.columns, self.along, self.dtype = rows, columns, along, dtype
+        self.inside = inside
         self.flows = flows
         self.half_rows = rows // 2 if along == "rows" else rows
         self.half_columns = columns // 2 if along == "columns" else columns
@@ -596,8 +534,9 @@
 
     def twin(self, n, spot, other, core):
         shard = self.shard(spot, other)
+        part = self.parts[n]
         return self.copy(
-            self.parts[n].half(self.grads[n], shard, core),
+            self.grads[n].at[shard] if part.inside else part.half(self.grads[n], shard, core),
             self.other[n].at[shard],
             (n, "twin") + spot + (other,),
             self.place.twin(),
@@ -606,7 +545,8 @@
     def begin(self, n, spot):
         there = self.there(spot)
         for other in (True, False):
-            when([there], self.keep(n, spot, other).start)
+            if not self.parts[n].inside:
+                when([there], self.keep(n, spot, other).start)
             if self.parts[n].along:
                 self.start([there], self.twin(n, spot, other, 1 - self.place.core))
 
@@ -631,7 +571,8 @@
 
             def add(other=other):
                 shard = self.shard(spot, other)
-                self.keep(n, spot, other).wait()
+                if not part.inside:
+                    self.keep(n, spot, other).wait()
                 if part.along:
                     self.twin(n, spot, other, self.place.core).wait_recv()
                     self.own[n][shard] = self.own[n][shard] + self.other[n][shard]
@@ -854,9 +795,9 @@
         functools.partial(reduce_kernel, parts, len(blocks), order),
         out_shape=[jax.ShapeDtypeStruct((p.rows, p.columns), p.dtype) for p in parts]
         + [jax.ShapeDtypeStruct(b.shape, b.dtype) for b in blocks],
-        in_specs=[pl.BlockSpec(memory_space=pl.ANY)] * (count + len(blocks)),
+        in_specs=[pl.BlockSpec(memory_space=pltpu.HBM)] * (count + len(blocks)),
         out_specs=[pl.BlockSpec(memory_space=pltpu.VMEM)] * count
-        + [pl.BlockSpec(memory_space=pl.ANY)] * len(blocks),
+        + [pl.BlockSpec(memory_space=pltpu.HBM)] * len(blocks),
         scratch_shapes=reduce_scratch(parts)
         + [
             pltpu.SemaphoreType.DMA((len(labels.numbers),)),
@@ -871,7 +812,7 @@
     )(*arrays, *blocks)
 
 
-def column_part(rows, columns, shared, early):
+def column_part(rows, columns, shared, early, inside=False):
     half = columns // 2
     part = (half - shared) // 2
     flows = []
@@ -881,7 +822,7 @@
         flows.append((lambda side: shared + side * part, early, "line", True))
     if part > early:
         flows.append((lambda side: shared + side * part + early, part - early, "pair", True))
-    return Part(rows, columns, "columns", flows)
+    return Part(rows, columns, "columns", flows, inside=inside)
 
 
 def row_part(rows, columns, shared, early):
@@ -899,8 +840,8 @@
     )
 
 
-def vector_part(rows, columns):
-    return Part(rows, columns, None, [(lambda side: 0, columns, "line", False)], F32)
+def vector_part(rows, columns, inside=False):
+    return Part(rows, columns, None, [(lambda side: 0, columns, "line", False)], F32, inside)
 
 
 ROW_QUERY, ROW_VALUE, ROW_OUTPUT, ROW_GAIN1, ROW_SHIFT1, ROW_INNER, INNER = 0, 1, 2, 3, 4, 5, 4
@@ -1120,7 +1061,7 @@
     tile = INNER * LANES
     tiles = hidden // tile
     whole = pl.BlockSpec(memory_space=pltpu.VMEM)
-    far = pl.BlockSpec(memory_space=pl.ANY)
+    far = pl.BlockSpec(memory_space=pltpu.HBM)
 
     def space(dtype):
         return pltpu.VMEM((count, width), dtype)
@@ -1164,44 +1105,67 @@
     )(rows, context, cot, lengths, table, output_w, inner_w, outer_w)
 
 
-def widen_kernel(splits, *refs):
+def widen_kernel(splits, lines, *refs):
     count = len(splits)
-    ins, refs = refs[:count], refs[count:]
-    outs = refs[: sum(splits)]
-    wides, sems = refs[sum(splits) : -1], refs[-1]
+    many = sum(splits)
+    ins, table, outs = refs[:count], refs[count], refs[count + 1 : count + 1 + many]
+    vectors = refs[count + 1 + many : count + 1 + many + len(lines)]
+    rest = refs[count + 1 + many + len(lines) :]
+    narrow, held, wides = rest[:count], rest[count], rest[count + 1 : count + 1 + many]
+    load, save = rest[-2:]
+    loads = [
+        pltpu.make_async_copy(here, there, load.at[k])
+        for k, (here, there) in enumerate(zip(ins + (table,), narrow + (held,)))
+    ]
+    for copy in loads:
+        copy.start()
     copies = []
     at = 0
-    for source, parts in zip(ins, splits):
-        columns = source.shape[-1] // parts
+    for k, parts in enumerate(splits):
+        loads[k].wait()
+        columns = narrow[k].shape[-1] // parts
         for part in range(parts):
-            wides[at][...] = source[..., part * columns : (part + 1) * columns].astype(F32)
-            copies.append(pltpu.make_async_copy(wides[at], outs[at], sems.at[at]))
+            wides[at][...] = narrow[k][..., part * columns : (part + 1) * columns].astype(
+                wides[at].dtype
+            )
+            copies.append(pltpu.make_async_copy(wides[at], outs[at], save.at[at]))
             copies[-1].start()
             at += 1
+    loads[count].wait()
+    row = 0
+    for vector, extent in zip(vectors, lines):
+        for line in range(extent):
+            copies.append(
+                pltpu.make_async_copy(
+                    held.at[row], vector.at[pl.ds(line * LANES, LANES)], save.at[many + row]
+                )
+            )
+            copies[-1].start()
+            row += 1
     for copy in copies:
         copy.wait()
 
 
-def widen(arrays, splits):
+def widen(arrays, splits, types, table, lines):
     shapes = []
-    for array, parts in zip(arrays, splits):
-        shapes += [array.shape[:-1] + (array.shape[-1] // parts,)] * parts
+    for array, parts, kind in zip(arrays, splits, types):
+        shape = array.shape[:-1] + (array.shape[-1] // parts,)
+        shapes += [jax.ShapeDtypeStruct(shape, kind)] * parts
+    far = pl.BlockSpec(memory_space=pltpu.HBM)
     return pl.pallas_call(
-        functools.partial(widen_kernel, splits),
-        out_shape=[jax.ShapeDtypeStruct(shape, F32) for shape in shapes],
-        in_specs=[pl.BlockSpec(memory_space=pltpu.VMEM)] * len(arrays),
-        out_specs=[pl.BlockSpec(memory_space=pl.ANY)] * len(shapes),
-        scratch_shapes=[pltpu.VMEM(shape, F32) for shape in shapes]
-        + [pltpu.SemaphoreType.DMA((len(shapes),))],
+        functools.partial(widen_kernel, splits, lines),
+        out_shape=shapes + [jax.ShapeDtypeStruct((k * LANES,), F32) for k in lines],
+        in_specs=[far] * (len(arrays) + 1),
+        out_specs=[far] * (len(shapes) + len(lines)),
+        scratch_shapes=[pltpu.VMEM(array.shape, array.dtype) for array in arrays + (table,)]
+        + [pltpu.VMEM(shape.shape, shape.dtype) for shape in shapes]
+        + [
+            pltpu.SemaphoreType.DMA((len(arrays) + 1,)),
+            pltpu.SemaphoreType.DMA((len(shapes) + sum(lines),)),
+        ],
         compiler_params=pltpu.CompilerParams(vmem_limit_bytes=40 << 20),
         name="widen_results",
-    )(*arrays)
-
-
-def greet_twin(place):
-    barrier = pltpu.get_barrier_semaphore()
-    pl.semaphore_signal(barrier, inc=1, device_id=place.twin(), device_id_type=MESH)
-    pl.semaphore_wait(barrier, 1)
+    )(*arrays, table)
 
 
 def stack_heads(block, lower):
@@ -1209,6 +1173,18 @@
     return jnp.concatenate((jnp.where(lower, block, zero), jnp.where(lower, zero, block)), axis=0)
 
 
+def repeat(first, stop, action):
+    def step(i, carry):
+        action(i)
+        return carry
+
+    lax.fori_loop(first, stop, step, 0)
+
+
+GROUPS = 4
+HALVES = 2
+
+
 SPAN = 2 * HEAD_DIM
 
 
@@ -1217,18 +1193,15 @@
 
 
 class AttentionForward:
-    def __init__(self, place, rows, weight, vec, bias, qkv, context, probs, away, tiles, send, recv, load):
+    def __init__(self, place, rows, weight, vec, bias, qkv, context, probs, held, away, send, recv, save):
         self.place, self.rows, self.weight, self.vec, self.bias = place, rows, weight, vec, bias
-        self.qkv, self.context, self.probs, self.away = qkv, context, probs, away
-        self.tiles, self.send, self.recv, self.load = tiles, send, recv, load
+        self.qkv, self.context, self.probs, self.held, self.away = qkv, context, probs, held, away
+        self.send, self.recv, self.save = send, recv, save
         self.count, self.width = context.shape
         self.pairs = self.width // SPAN
-        self.tile = tiles.shape[2]
-
-    def fetch_weight(self, t):
-        return pltpu.make_async_copy(
-            self.weight.at[:, pl.ds(t * self.tile, self.tile)], self.tiles.at[t], self.load.at[t]
-        )
+
+    def save_probs(self, pair):
+        return pltpu.make_async_copy(self.held.at[pair], self.probs.at[pair], self.save.at[pair])
 
     def fetch(self, which, pair):
         return pltpu.make_async_remote_copy(
@@ -1240,24 +1213,25 @@
             device_id_type=MESH,
         )
 
-    def project(self, t):
-        columns = pl.ds(t * self.tile, self.tile)
-        per = self.width // self.tile
-        section = t // per
-        self.fetch_weight(t).wait()
-        product = plain_product(self.rows[...], self.tiles[t])
-        if section != 1:
-            row = ROW_QUERY if section == 0 else ROW_VALUE
-            product = product + self.vec[pl.ds(row, 1), pl.ds((t % per) * self.tile, self.tile)]
-        self.qkv[:, columns] = product.astype(BF16)
-
-    def give(self, t):
-        per = self.width // self.tile
-        section = t // per
-        if section:
-            share = self.tile // SPAN
-            for pair in range((t % per) * share, (t % per + 1) * share):
-                self.fetch(section - 1, pair).start()
+    def project(self, section):
+        tile = 512
+        rows = self.rows[...].reshape(self.count, self.width)
+
+        def one(t):
+            columns = pl.ds(pl.multiple_of(section * self.width + t * tile, tile), tile)
+            product = plain_product(rows, self.weight[:, columns])
+            if section != 1:
+                row = ROW_QUERY if section == 0 else ROW_VALUE
+                product = product + self.vec[
+                    pl.ds(row, 1), pl.ds(pl.multiple_of(t * tile, tile), tile)
+                ]
+            self.qkv[:, columns] = product.astype(BF16)
+
+        repeat(0, self.width // tile, one)
+
+    def give(self, which):
+        for pair in range(self.pairs):
+            self.fetch(which, pair).start()
 
     def attend(self, pair):
         for which in range(2):
@@ -1279,103 +1253,174 @@
         weights = jnp.exp(scores - top)
         total = jnp.sum(weights, axis=1, keepdims=True)
         probs = (weights * (1.0 / total)).astype(BF16)
-        self.probs[pair] = probs
+        self.held[pair] = probs
+        self.save_probs(pair).start()
         mixed = plain_product(probs, values)
         self.context[:, span_of(0, pair, self.width)] = jnp.where(
             lower, mixed[:count], mixed[count:]
         ).astype(BF16)
 
+    def attend_group(self, group):
+        each = self.pairs // GROUPS
+        repeat(group * each, (group + 1) * each, self.attend)
+
     def finish(self):
         for pair in range(self.pairs):
             for which in range(2):
                 self.fetch(which, pair).wait_send()
-
-
-def attend_kernel(
-    rows_ref, lengths_ref, table_ref, weight, qkv, context, probs, away, bias_ref, tiles, vec, send, recv, load
-):
+            self.save_probs(pair).wait()
+
+
+TABLE, QUERIES = 0, 1
+
+
+def start_actions(gather, work, keep, swaps, save, table_ref):
+    found = gather.actions()
+    others = [k for k in range(len(keep)) if k not in (TABLE, QUERIES)]
+
+    def ready():
+        gather.wait_twins((TABLE, QUERIES))
+        for k in (TABLE, QUERIES):
+            keep[k].wait()
+        swaps[0].finish()
+        spread_table(table_ref, work.vec)
+        save.start()
+
+    def values():
+        work.project(2)
+        work.give(0)
+
+    def queries():
+        work.give(1)
+        work.project(0)
+
+    found.append((("ready",), ready))
+    found.append((("project", 0), lambda: work.project(1)))
+    found.append((("project", 1), values))
+    found.append((("project", 2), queries))
+    for group in range(GROUPS):
+        found.append((("pa", group), lambda group=group: work.attend_group(group)))
+
+    def last():
+        gather.finish(others)
+        work.finish()
+        for k in others:
+            keep[k].wait()
+        swaps[1].finish()
+        save.wait()
+
+    found.append((("last",), last))
+    return found
+
+
+def start_kernel(flows, spots, order, *refs):
+    count = max(array for array, _ in spots) + 1
+    shares, refs = refs[: len(spots)], refs[len(spots) :]
+    (in_block, cot_block, lengths_ref), refs = refs[:3], refs[3:]
+    table_ref, refs = refs[0], refs[1:]
+    far, refs = refs[: count - 1], refs[count - 1 :]
+    rows, cots, qkv, context, probs, away = refs[:6]
+    owns, refs = refs[6 : 6 + count], refs[6 + count :]
+    weight, held, vec, bias = refs[:4]
+    send, recv, local, load, send2, recv2, save2, saveq = refs[4:12]
+    fulls = (table_ref, weight) + tuple(far[1:])
     place = Place()
-    rows = rows_ref.shape[0]
+    loads = [
+        pltpu.make_async_copy(
+            share, owns[array].at[:, pl.ds(column, share.shape[1])], load.at[k]
+        )
+        for k, (share, (array, column)) in enumerate(zip(shares, spots))
+    ]
+    for copy in loads:
+        copy.start()
+    keep = [
+        pltpu.make_async_copy(
+            own, full.at[pl.ds(pl.multiple_of(place.shard * own.shape[0], 16), own.shape[0]), :], local.at[k]
+        )
+        for k, (own, full) in enumerate(zip(owns, fulls))
+    ]
+    greet(place)
+    rows_count = context.shape[0]
     length = lengths_ref[place.side, 0]
-    row = lax.broadcasted_iota(jnp.int32, (8, rows), 1)
+    row = lax.broadcasted_iota(jnp.int32, (8, rows_count), 1)
     for k, core in enumerate((place.core, 1 - place.core)):
-        bias_ref[:, pl.ds(k * rows, rows)] = jnp.where(
-            row_place(row, core, rows) < length, 0.0, -1e30
-        )
+        bias[:, pl.ds(k * rows_count, rows_count)] = jnp.where(
+            row_place(row, core, rows_count) < length, 0.0, -1e30
+        )
+    for copy in loads:
+        copy.wait()
+    swaps = [
+        Swap(place, [in_block], [rows], *refs[12:15]),
+        Swap(place, [cot_block], [cots], *refs[15:18]),
+    ]
+    for swap in swaps:
+        swap.start()
+    gather = Gather(place, flows, owns, fulls, send, recv)
+    for copy in keep:
+        copy.start()
     work = AttentionForward(
-        place, rows_ref, weight, vec, bias_ref, qkv, context, probs, away, tiles, send, recv, load
-    )
-    count = tiles.shape[0]
-    order = list(range(count // 3, count)) + list(range(count // 3))
-    for t in order:
-        work.fetch_weight(t).start()
-    greet_twin(place)
-    spread_table(table_ref, vec)
-    for before, t in zip([None] + order, order):
-        work.project(t)
-        if before is not None:
-            work.give(before)
-
-    def step(pair, carry):
-        work.attend(pair)
-        return carry
-
-    lax.fori_loop(0, work.pairs, step, 0)
-    work.finish()
-
-
-def attend(rows, lengths, table, weight, collective_id):
-    count, width = rows.shape
+        place, rows, weight, vec, bias, qkv, context, probs, held, away, send2, recv2, save2
+    )
+    save = pltpu.make_async_copy(weight, far[0], saveq.at[0])
+    for step in in_order(start_actions(gather, work, keep, swaps, save, table_ref), order):
+        step()
+
+
+def start(shares, spots, blocks, lengths, flows, shards, collective_id, order):
+    labels = gather_labels(flows)
+    count = max(array for array, _ in spots) + 1
+    shapes = []
+    for array in range(count):
+        members = [share for share, spot in zip(shares, spots) if spot[0] == array]
+        shapes.append((members[0].shape[0], sum(m.shape[1] for m in members)))
+    _, block_len, width = blocks[0].shape
+    rows = 2 * block_len
     pairs = width // SPAN
-    tile = 512
-    tiles = weight.shape[1] // tile
+    far = pl.BlockSpec(memory_space=pltpu.HBM)
     whole = pl.BlockSpec(memory_space=pltpu.VMEM)
+    probs_shape = (pairs, 2 * rows, 2 * rows)
     return pl.pallas_call(
-        attend_kernel,
-        out_shape=[
-            jax.ShapeDtypeStruct((count, 3 * width), BF16),
-            jax.ShapeDtypeStruct((count, width), BF16),
-            jax.ShapeDtypeStruct((pairs, 2 * count, 2 * count), BF16),
-            jax.ShapeDtypeStruct((count, 2 * width), BF16),
+        functools.partial(start_kernel, flows, spots, order),
+        out_shape=[jax.ShapeDtypeStruct((shards * r, c), BF16) for r, c in shapes]
+        + [jax.ShapeDtypeStruct(block.shape, BF16) for block in blocks]
+        + [
+            jax.ShapeDtypeStruct((rows, 3 * width), BF16),
+            jax.ShapeDtypeStruct((rows, width), BF16),
+            jax.ShapeDtypeStruct(probs_shape, BF16),
+            jax.ShapeDtypeStruct((rows, 2 * width), BF16),
         ],
-        in_specs=[
-            whole,
-            pl.BlockSpec(memory_space=pltpu.SMEM),
-            whole,
-            pl.BlockSpec(memory_space=pl.ANY),
-        ],
-        out_specs=[whole] * 4,
-        scratch_shapes=[
-            pltpu.VMEM((8, 2 * count), F32),
-            pltpu.VMEM((tiles, width, tile), BF16),
+        in_specs=[far] * (len(shares) + 2) + [pl.BlockSpec(memory_space=pltpu.SMEM)],
+        out_specs=[whole] + [far] * (count - 1) + [whole, far] + [whole, whole, far, whole],
+        scratch_shapes=[pltpu.VMEM(shape, BF16) for shape in shapes]
+        + [
+            pltpu.VMEM((shards * shapes[QUERIES][0], shapes[QUERIES][1]), BF16),
+            pltpu.VMEM(probs_shape, BF16),
             pltpu.VMEM((TABLE_ROWS, width), F32),
+            pltpu.VMEM((8, 2 * rows), F32),
+            pltpu.SemaphoreType.DMA((len(labels.numbers),)),
+            pltpu.SemaphoreType.DMA((len(labels.numbers),)),
+            pltpu.SemaphoreType.DMA((count,)),
+            pltpu.SemaphoreType.DMA((len(shares),)),
             pltpu.SemaphoreType.DMA((2, pairs)),
             pltpu.SemaphoreType.DMA((2, pairs)),
-            pltpu.SemaphoreType.DMA((tiles,)),
-        ],
+            pltpu.SemaphoreType.DMA((pairs,)),
+            pltpu.SemaphoreType.DMA((1,)),
+        ]
+        + swap_scratch(1) * 2,
         compiler_params=pltpu.CompilerParams(
-            collective_id=collective_id, has_side_effects=True, vmem_limit_bytes=40 << 20
+            collective_id=collective_id, has_side_effects=True, vmem_limit_bytes=48 << 20
         ),
-        name="attention_forward",
-    )(rows, lengths, table, weight)
+        name="gather_attention_forward",
+    )(*shares, *blocks, lengths)
 
 
 class AttentionBackward:
-    def __init__(
-        self, place, rows, qkv, away, probs, grad, weight, out, weight_grad, tiles, blocks, keep, leave, come, send, recv, load, save
-    ):
-        self.place, self.rows, self.qkv, self.away, self.probs = place, rows, qkv, away, probs
-        self.grad, self.weight, self.out, self.weight_grad = grad, weight, out, weight_grad
-        self.tiles, self.blocks, self.keep, self.leave, self.come = tiles, blocks, keep, leave, come
-        self.send, self.recv, self.load, self.save = send, recv, load, save
+    def __init__(self, place, qkv, away, grad, out, keep, leave, come, send, recv):
+        self.place, self.qkv, self.away, self.grad = place, qkv, away, grad
+        self.out, self.keep, self.leave, self.come = out, keep, leave, come
+        self.send, self.recv = send, recv
         self.count, self.width = grad.shape
         self.pairs = self.width // SPAN
-        self.tile = tiles.shape[2]
-
-    def fetch_weight(self, t):
-        return pltpu.make_async_copy(
-            self.weight.at[:, pl.ds(t * self.tile, self.tile)], self.tiles.at[t], self.load.at[t]
-        )
 
     def give(self, which, pair):
         return pltpu.make_async_remote_copy(
@@ -1387,7 +1432,7 @@
             device_id_type=MESH,
         )
 
-    def attend(self, pair):
+    def attend(self, pair, probs):
         count = self.count
         lower = lax.broadcasted_iota(jnp.int32, (count, SPAN), 1) < HEAD_DIM
         scale = HEAD_DIM**-0.5
@@ -1404,7 +1449,6 @@
         keys = jnp.concatenate((here(1), there(1)), axis=0)
         values = jnp.concatenate((here(2), there(2)), axis=0)
         grad = stack_heads(self.grad[:, first], lower)
-        probs = self.probs[pair]
         value_part = left_product(probs, grad)
         probs_grad = right_product(grad, values)
         wide = probs.astype(F32)
@@ -1428,111 +1472,197 @@
                 self.keep[:, here] + self.come[:, here].astype(F32)
             ).astype(BF16)
 
-    def weigh(self, t, rows_t):
-        columns = pl.ds(t * self.tile, self.tile)
-        self.blocks[t] = plain_product(rows_t, self.out[:, columns]).astype(BF16)
-
-    def save_weight(self, t):
-        return pltpu.make_async_copy(
-            self.blocks.at[t], self.weight_grad.at[:, pl.ds(t * self.tile, self.tile)], self.save.at[t]
-        )
-
-    def spread(self, t):
-        columns = pl.ds(t * self.tile, self.tile)
-        self.fetch_weight(t).wait()
-        return right_product(self.out[:, columns], self.tiles[t])
-
-    def bias_sums(self, sums):
-        sums[pl.ds(ROW_QUERY, 1), :] = total_rows(self.out[:, : self.width])
-        sums[pl.ds(ROW_VALUE, 1), :] = total_rows(self.out[:, 2 * self.width :])
-
     def finish(self):
         for pair in range(self.pairs):
             for which in range(2):
                 self.give(which, pair).wait_send()
 
 
-def attend_back_kernel(
-    rows_ref, qkv, away, probs, grad, first_grad, table_ref, weight,
-    weight_grad, input_grad, sums_ref,
-    out, tiles, blocks, keep, leave, come, total, sums, rows_t, send, recv, load, save,
-):
+class Finish:
+    def __init__(self, work, tiles, weight, rows_ref, rows_t, first_grad, total, block, sums, held, probs, load, sems):
+        self.work, self.tiles, self.weight, self.rows_ref, self.rows_t = work, tiles, weight, rows_ref, rows_t
+        self.total, self.block, self.sums = total, block, sums
+        self.held, self.probs, self.load, self.sems = held, probs, load, sems
+        self.grad_load = pltpu.make_async_copy(first_grad, total, sems.at[held.shape[0]])
+        self.count, self.width = total.shape
+        self.tile = tiles.shape[2]
+
+    def weight_load(self, t):
+        columns = pl.ds(pl.multiple_of(t * self.tile, self.tile), self.tile)
+        slot = lax.rem(t, self.tiles.shape[0])
+        return pltpu.make_async_copy(
+            self.weight.at[:, columns], self.tiles.at[slot], self.load.at[slot]
+        )
+
+    def probs_load(self, pair):
+        slot = lax.rem(pair, self.held.shape[0])
+        return pltpu.make_async_copy(
+            self.probs.at[pair], self.held.at[slot], self.sems.at[slot]
+        )
+
+    def begin(self):
+        for pair in range(self.held.shape[0]):
+            self.probs_load(pair).start()
+        for t in range(self.tiles.shape[0]):
+            self.weight_load(t).start()
+        self.grad_load.start()
+
+    def attend(self, group):
+        each = self.work.pairs // GROUPS
+
+        slots = self.held.shape[0]
+
+        def one(pair):
+            self.probs_load(pair).wait()
+            self.work.attend(pair, self.held[lax.rem(pair, slots)])
+            pl.when(pair + slots < self.work.pairs)(self.probs_load(pair + slots).start)
+
+        repeat(group * each, (group + 1) * each, one)
+
+    def settle(self):
+        repeat(0, self.work.pairs, self.work.settle)
+
+    def weigh(self, core, target):
+        shards, rows, columns = target.shape
+        tile = self.tile
+
+        def one(j):
+            start = pl.multiple_of(core * columns + j * tile, tile)
+            product = plain_product(self.rows_t[...], self.work.out[:, pl.ds(start, tile)])
+            low = product.astype(BF16)
+            for shard in range(shards):
+                target[shard, :, pl.ds(pl.multiple_of(j * tile, tile), tile)] = low[
+                    shard * rows : (shard + 1) * rows
+                ]
+
+        repeat(0, columns // tile, one)
+
+    def turn(self):
+        self.rows_t[...] = self.rows_ref[...].T
+
+    def bias_sums(self, target):
+        self.sums[pl.ds(0, 1), :] = total_rows(self.work.out[:, : self.width])
+        self.sums[pl.ds(1, 1), :] = total_rows(self.work.out[:, 2 * self.width :])
+        for shard in range(target.shape[0]):
+            target[shard, pl.ds(ROW_QUERY, 2), :] = self.sums[
+                pl.ds(0, 2), pl.ds(shard * LANES, LANES)
+            ]
+
+    def spread(self, half):
+        count = self.weight.shape[1] // self.tile
+        each = count // HALVES
+        slots = self.tiles.shape[0]
+        if half == 0:
+            self.grad_load.wait()
+
+        def one(t):
+            self.weight_load(t).wait()
+            columns = pl.ds(pl.multiple_of(t * self.tile, self.tile), self.tile)
+            tile = self.tiles[lax.rem(t, slots)]
+            self.total[...] += right_product(self.work.out[:, columns], tile)
+            pl.when(t + slots < count)(self.weight_load(t + slots).start)
+
+        repeat(half * each, (half + 1) * each, one)
+        if half == HALVES - 1:
+            rows = self.block.shape[1]
+            for part in range(2):
+                self.block[part] = self.total[pl.ds(part * rows, rows), :].astype(BF16)
+
+
+def finish_actions(reduce, finish, swaps):
+    queries, vectors = 3, 4
+    place = reduce.place
+    found = reduce.actions()
+
+    def load():
+        finish.begin()
+        finish.turn()
+
+    found.append((("load",), load))
+    found.append((("swapout",), swaps[0].start))
+    for group in range(GROUPS):
+        found.append((("att", group), lambda group=group: finish.attend(group)))
+    found.append((("settleatt",), finish.settle))
+    found.append((("leave",), lambda: finish.weigh(1 - place.core, reduce.grads[queries])))
+    found.append((("own",), lambda: finish.weigh(place.core, reduce.own[queries])))
+    found.append((("sums",), lambda: finish.bias_sums(reduce.own[vectors])))
+    for half in range(HALVES):
+        found.append((("dx", half), lambda half=half: finish.spread(half)))
+    found.append((("swapin",), swaps[1].start))
+    return found
+
+
+def finish_kernel(parts, order, *refs):
+    rows_ref, qkv, away, grad, table_ref, first_grad, probs, weight = refs[:8]
+    grads, out_block = list(refs[8:11]), refs[11]
+    outs, swapped, refs = refs[12:17], refs[17:19], refs[19:]
+    leave_q, tiles, held, out, keep, leave, come, total, sums, rows_t, block = refs[:11]
+    send2, recv2, load2, sems = refs[11:15]
+    scratch, rest = refs[15:-9], refs[-9:]
     place = Place()
-    work = AttentionBackward(
-        place, rows_ref, qkv, away, probs, grad, weight, out, weight_grad, tiles, blocks,
-        keep, leave, come, send, recv, load, save,
-    )
-    count = tiles.shape[0]
-    for t in range(count):
-        work.fetch_weight(t).start()
-    greet_twin(place)
-
-    def step(pair, carry):
-        work.attend(pair)
-        return carry
-
-    lax.fori_loop(0, work.pairs, step, 0)
-    rows_t[...] = rows_ref[...].T
-    total[...] = first_grad[...]
-    for t in range(count):
-        if t == count // 3:
-
-            def settle(pair, carry):
-                work.settle(pair)
-                return carry
-
-            lax.fori_loop(0, work.pairs, settle, 0)
-        work.weigh(t, rows_t[...])
-        if t:
-            work.save_weight(t - 1).start()
-        total[...] += work.spread(t)
-    work.save_weight(count - 1).start()
-    input_grad[...] = total[...].astype(BF16)
-    work.bias_sums(sums)
-    sums_ref[...] = table_ref[...]
-    fold_table(sums, sums_ref, ROW_QUERY, 2)
-    for t in range(count):
-        work.save_weight(t).wait()
+    work = AttentionBackward(place, qkv, away, grad, out, keep, leave, come, send2, recv2)
+    finish = Finish(
+        work, tiles, weight, rows_ref, rows_t, first_grad, total, block, sums, held, probs, load2, sems
+    )
+    reduce = Reduce(place, parts, grads + [leave_q, None], outs, scratch, *rest[:3])
+    swaps = [
+        Swap(place, [out_block], [swapped[0]], *rest[3:6]),
+        Swap(place, [block], [swapped[1]], *rest[6:9]),
+    ]
+    for shard in range(LINE * PAIR):
+        reduce.own[4][shard] = table_ref[pl.ds(shard * TABLE_ROWS, TABLE_ROWS), :]
+    greet(place)
+    for step in in_order(finish_actions(reduce, finish, swaps), order):
+        step()
     work.finish()
-
-
-def attend_back(rows, saved, grad, first_grad, table, weight, collective_id):
+    for swap in swaps:
+        swap.finish()
+
+
+def finish(rows, saved, grad, first_grad, table, weight, grads, block, parts, collective_id, order):
     qkv, away, probs = saved
     count, width = rows.shape
     pairs = width // SPAN
     tile = 512
-    tiles = weight.shape[1] // tile
+    labels = reduce_labels(parts)
     whole = pl.BlockSpec(memory_space=pltpu.VMEM)
-    far = pl.BlockSpec(memory_space=pl.ANY)
+    far = pl.BlockSpec(memory_space=pltpu.HBM)
+    queries = parts[3]
     return pl.pallas_call(
-        attend_back_kernel,
-        out_shape=[
-            jax.ShapeDtypeStruct(weight.shape, BF16),
-            jax.ShapeDtypeStruct((count, width), BF16),
-            jax.ShapeDtypeStruct(table.shape, F32),
-        ],
-        in_specs=[whole] * 7 + [far],
-        out_specs=[far, whole, whole],
+        functools.partial(finish_kernel, parts, order),
+        out_shape=[jax.ShapeDtypeStruct((p.rows, p.columns), p.dtype) for p in parts]
+        + [jax.ShapeDtypeStruct(block.shape, BF16)] * 2,
+        in_specs=[whole] * 5 + [far] * 7,
+        out_specs=[whole] * len(parts) + [far] * 2,
         scratch_shapes=[
+            pltpu.VMEM((LINE * PAIR, queries.half_rows, queries.half_columns), BF16),
+            pltpu.VMEM((2, width, tile), BF16),
+            pltpu.VMEM((pairs // 2,) + probs.shape[1:], BF16),
             pltpu.VMEM((count, 3 * width), BF16),
-            pltpu.VMEM((tiles, width, tile), BF16),
-            pltpu.VMEM((tiles, width, tile), BF16),
             pltpu.VMEM((count, 2 * width), F32),
             pltpu.VMEM((count, 2 * width), BF16),
             pltpu.VMEM((count, 2 * width), BF16),
             pltpu.VMEM((count, width), F32),
-            pltpu.VMEM((TABLE_ROWS, width), F32),
+            pltpu.VMEM((8, width), F32),
             pltpu.VMEM((width, count), BF16),
+            pltpu.VMEM(block.shape, BF16),
             pltpu.SemaphoreType.DMA((2, pairs)),
             pltpu.SemaphoreType.DMA((2, pairs)),
-            pltpu.SemaphoreType.DMA((tiles,)),
-            pltpu.SemaphoreType.DMA((tiles,)),
-        ],
+            pltpu.SemaphoreType.DMA((2,)),
+            pltpu.SemaphoreType.DMA((pairs // 2 + 1,)),
+        ]
+        + reduce_scratch(parts)
+        + [
+            pltpu.SemaphoreType.DMA((len(labels.numbers),)),
+            pltpu.SemaphoreType.DMA((len(labels.numbers),)),
+            pltpu.SemaphoreType.DMA((len(parts) * 2 * len(SPOTS),)),
+        ]
+        + swap_scratch(1) * 2,
         compiler_params=pltpu.CompilerParams(
-            collective_id=collective_id, has_side_effects=True, vmem_limit_bytes=60 << 20
+            collective_id=collective_id, has_side_effects=True, vmem_limit_bytes=63 << 20
         ),
-        name="attention_backward",
-    )(rows, qkv, away, probs, grad, first_grad, table, weight)
+        name="attention_backward_reduce",
+    )(rows, qkv, away, grad, table, first_grad, probs, weight, *grads, block)
 
 
 def exact_gelu(hidden):
@@ -1756,7 +1886,7 @@
     return (
         output.reshape(inputs.shape),
         input_grad.reshape(inputs.shape),
-        lax.psum(share, "ctx")[0],
+        split_columns(lax.psum(share, "ctx")[0], widths),
         tuple(split_columns(reduce_rows(parts[0]), [width] * 3))
         + tuple(reduce_rows(part) for part in parts[1:]),
     )
@@ -1781,10 +1911,23 @@
     flows += column_flows(2, shard_rows, width, *GATHER_SPLIT[1])
     flows += column_flows(3, shard_rows, hidden, *GATHER_SPLIT[2])
     flows += row_flows(4, hidden // shards, width, *GATHER_SPLIT[3])
-    tables, full_qkv, full_output, full_inner, full_outer, in_rows, cot_rows = gather_call(
+    (
+        tables,
+        full_qkv,
+        full_output,
+        full_inner,
+        full_outer,
+        in_rows,
+        cot_rows,
+        qkv,
+        context,
+        probs,
+        away,
+    ) = start(
         (table.astype(BF16),) + weights,
         ((0, 0), (1, 0), (1, width), (1, 2 * width), (2, 0), (3, 0), (4, 0)),
         blocks,
+        lengths,
         flows,
         shards,
         1,
@@ -1792,35 +1935,41 @@
     )
     in_rows = in_rows.reshape(rows, width)
     cot_rows = cot_rows.reshape(rows, width)
-    qkv, context, probs, away = attend(in_rows, lengths, tables, full_qkv, 3)
     output, first_grad, context_grad, table_grad, output_part, inner_part, outer_part = middle(
         in_rows, context, cot_rows, lengths, tables, full_output, full_inner, full_outer
     )
-    qkv_part, input_grad, table_grad = attend_back(
-        in_rows, (qkv, away, probs), context_grad, first_grad, table_grad, full_qkv, 4
-    )
-    sums = reduce_call(
-        (inner_part, outer_part, output_part, qkv_part, table_grad),
-        (
-            output.reshape(micro, block_len, width),
-            input_grad.reshape(micro, block_len, width),
-        ),
+    sums = finish(
+        in_rows,
+        (qkv, away, probs),
+        context_grad,
+        first_grad,
+        table_grad,
+        full_qkv,
+        (inner_part, outer_part, output_part),
+        output.reshape(micro, block_len, width),
         [
             column_part(shard_rows, hidden, *REDUCE_SPLIT[0]),
             row_part(hidden // shards, width, *REDUCE_SPLIT[1]),
             column_part(shard_rows, width, *REDUCE_SPLIT[2]),
-            column_part(shard_rows, 3 * width, *REDUCE_SPLIT[3]),
-            vector_part(TABLE_ROWS, LANES),
+            column_part(shard_rows, 3 * width, *REDUCE_SPLIT[3], inside=True),
+            vector_part(TABLE_ROWS, LANES, inside=True),
         ],
         2,
         REDUCE_ORDER,
     )
     inner_share, outer_share, output_share, qkv_share, table_share, outs, grads = sums
-    wide = widen((qkv_share, output_share, inner_share, outer_share, grads), (3, 1, 1, 1, 1))
+    lines = tuple(vector.shape[0] // LANES for vector in vectors)
+    wide = widen(
+        (qkv_share, output_share, inner_share, outer_share, grads, outs),
+        (3, 1, 1, 1, 1, 1),
+        (F32,) * 5 + (BF16,),
+        table_share,
+        lines,
+    )
     return (
-        outs.reshape(inputs.shape),
+        wide[7].reshape(inputs.shape),
         wide[6].reshape(inputs.shape),
-        table_share.reshape(-1),
+        tuple(wide[8:]),
         tuple(wide[:6]),
     )
 
@@ -1869,10 +2018,7 @@
     whole_lines = all(extent % LANES == 0 for extent in widths)
     direct = laid_out and inputs.shape[:2] == (2, 1) and whole_lines
     run = direct_body if direct else native_body
-    output, input_grad, vector_share, weight_shares = run(
-        inputs, cotangent, lengths, vectors, weights
-    )
-    shares = split_columns(vector_share, widths)
+    output, input_grad, shares, weight_shares = run(inputs, cotangent, lengths, vectors, weights)
     query_share, key_share, value_share, output_share, inner_share, outer_share = weight_shares
     return (
         output,

time: 323 us -> 300 us (0.929)
  Pallas kernels: 300 us -> 278 us
    pallas_call x5 -> x3, Pallas kernels: 267 us -> 245 us  [the longest x1 126 us: finish(): pl.pallas_call(functools.partial(finish_kernel, parts, order), out_shape=...]
    unnamed x28 -> x41, local copies, waits for them, and re-layouts: 17.7 us -> 19.1 us
where the time goes in v1:
time: 300 us; the launch traced here: 299 us
  Pallas kernels  278 us (93%)
  local copies, waits for them, and re-layouts  19.1 us (6%)
    pallas_call x1, Pallas kernels, finish(): pl.pallas_call(functools.partial(finish_kernel, parts, order), out_shape=...  126 us
    pallas_call x1, Pallas kernels, start(): pl.pallas_call(functools.partial(start_kernel, flows, spots, order), out_...  115 us
    pallas_call x1, Pallas kernels, middle(): pl.pallas_call(middle_kernel, out_shape=[jax.ShapeDtypeStruct((count, wid...  33.5 us
    unnamed x41, local copies, waits for them, and re-layouts  19.1 us

profile of v1, /device:TPU:1, one launch (start us, length us, event | category | flops | bytes accessed | tf_op | source)
XLA Modules:
  0.0 299.1 jit_solution(8947445243242806613)
XLA Ops:
  0.7 0.7 copy.35.refs_9_.lengths_ref
  1.4 0.8 add_convert_fusion.refs_0_
  2.2 0.0 copy-start.2
  2.2 1.2 copy-done.2
  3.4 0.0 copy-start.8
  3.4 1.0 copy-done.8
  4.5 0.0 copy-start.9
  4.5 1.0 copy-done.9
  5.5 0.0 copy-start.13
  5.5 0.9 copy-done.13
  6.5 0.9 copy-done.14
  7.4 0.9 copy-done.15
  8.4 0.9 copy-done.16
  9.3 115.2 %gather_attention_forward.1 = (bf16[128,128]{1,0:T(8,128)(2,1)S(1)}, bf16[1024,3072]{1,0:T(8,128)(2,1)}, bf16[1024,1024]{1,0:T(8,128)(2,1)}, bf16[1024,4096]{1,0...) custom-call(bf16[16,128]{1,0:T(8,128)(2,1)S(1)} %add_convert_fusion., ...), custom_call_target="tpu_custom_call" | custom-call | tf_op jit(solution)/shard_map/gather_attention_forward/pallas_call | solution.py:1382
  124.5 0.0 copy-start
  124.5 0.8 copy-done
  125.3 1.0 copy-done.1
  126.3 0.8 copy-done.6
  127.1 0.8 copy-done.7
  127.9 0.6 copy-done.17
  128.5 0.0 copy-done.19
  128.5 33.5 %feed_forward.1 = (bf16[256,1024]{1,0:T(8,128)(2,1)}, f32[256,1024]{1,0:T(8,128)}, bf16[256,1024]{1,0:T(8,128)(2,1)}, f32[128,128]{1,0:T(8,128)}, bf16[1024,1024...) custom-call(bf16[256,1024]{1,0:T(8,128)(2,1)} %bitcast.20, bf16[256,1024]{1,0:T(8,128)(2,1)} %copy-done.7, ...), custom_call_target="tpu_custom_call" | custom-call | tf_op jit(solution)/shard_map/feed_forward/pallas_call | solution.py:1069
  162.0 125.9 %attention_backward_reduce.1 = (bf16[128,4096]{1,0:T(8,128)(2,1)}, bf16[512,1024]{1,0:T(8,128)(2,1)}, bf16[128,1024]{1,0:T(8,128)(2,1)}, bf16[128,3072]{1,0:T(8,...) custom-call(bf16[256,1024]{1,0:T(8,128)(2,1)} %bitcast.21, ...), custom_call_target="tpu_custom_call" | custom-call | tf_op jit(solution)/shard_map/attention_backward_reduce/pallas_call | solution.py:1631
  287.9 0.0 copy-start.3
  287.9 1.2 copy-done.3
  289.1 1.2 copy-done.4
  290.3 1.1 copy-done.5
  291.5 1.0 copy-done.10
  292.5 1.0 copy-done.11
  293.5 0.9 copy-done.12
  294.5 0.7 copy-done.18
  295.2 3.7 %widen_results.1 = (f32[128,1024]{1,0:T(8,128)}, f32[128,1024]{1,0:T(8,128)}, f32[128,1024]{1,0:T(8,128)}, f32[128,1024]{1,0:T(8,128)}, f32[128,4096]{1,0:T(8,12...) custom-call(bf16[128,3072]{1,0:T(8,128)(2,1)S(1)} %copy-done.5, ...), custom_call_target="tpu_custom_call" | custom-call | tf_op jit(solution)/shard_map/widen_results/pallas_call | solution.py:1155
  (14 shorter events, 0.0 us)
Async XLA Ops:
  1.4 127.1 %copy-start.19 = (s32[2,1]{1,0:T(2,128)}, s32[2,1]{1,0:T(2,128)S(1)}, u32[]{:S(2)}) copy-start(s32[2,1]{1,0:T(2,128)S(1)} %copy.35.refs_9_.lengths_ref) | copy-start | bytes 28
  2.2 1.2 copy-start.2
  3.4 1.0 copy-start.8
  4.5 1.0 copy-start.9
  5.5 0.9 copy-start.13
  6.5 0.9 copy-start.14
  7.4 0.9 copy-start.15
  8.4 0.9 copy-start.16
  124.5 0.8 copy-start
  125.3 1.0 copy-start.1
  126.3 0.8 copy-start.6
  127.1 0.8 copy-start.7
  127.9 0.6 copy-start.17
  287.9 1.2 copy-start.3
  289.1 1.2 copy-start.4
  290.3 1.1 copy-start.5
  291.5 1.0 copy-start.10
  292.5 1.0 copy-start.11
  293.5 0.9 copy-start.12
  294.5 0.7 copy-start.18

commit v2 on v1

--- a/solution.py
+++ b/solution.py
@@ -12,35 +12,36 @@
 F32 = jnp.float32
 BF16 = jnp.bfloat16
 
-GATHER_SPLIT = ((512, 0), (256, 0), (256, 384), (128, 32))
-REDUCE_SPLIT = ((768, 512), (128, 32), (256, 128), (768, 256))
+GATHER_SPLIT = ((256, 384), (256, 128), (1024, 128), (128, 64))
+REDUCE_SPLIT = ((512, 512), (128, 48), (256, 128), (1024, 256))
 GATHER_ORDER = (
-    5, 6, 2, 0, 1, 3, 9, 13, 64, 29, 10, 4, 81, 30, 26, 62, 36, 7, 47, 149, 75, 70, 53, 94, 14,
-    104, 11, 32, 82, 27, 79, 217, 143, 46, 33, 218, 35, 24, 49, 28, 162, 16, 160, 63, 71, 38, 132,
-    131, 67, 34, 115, 200, 60, 172, 41, 8, 98, 21, 96, 201, 101, 58, 84, 66, 138, 68, 189, 100,
-    69, 109, 50, 103, 135, 113, 80, 106, 97, 164, 163, 130, 40, 211, 54, 120, 45, 22, 152, 169,
-    166, 126, 23, 31, 74, 116, 72, 83, 144, 89, 61, 212, 148, 183, 198, 76, 171, 174, 139, 147,
-    114, 12, 153, 137, 177, 118, 77, 168, 161, 206, 203, 173, 136, 199, 154, 55, 215, 65, 121,
-    155, 91, 110, 230, 99, 142, 134, 228, 216, 39, 181, 95, 105, 78, 184, 48, 37, 165, 73, 150,
-    223, 178, 188, 229, 19, 102, 167, 17, 182, 85, 128, 140, 87, 186, 15, 51, 25, 170, 156, 108,
-    133, 205, 207, 145, 119, 175, 220, 59, 57, 194, 86, 52, 204, 43, 157, 56, 151, 232, 122, 233,
-    234, 90, 210, 129, 185, 20, 123, 42, 127, 141, 196, 125, 190, 235, 18, 159, 221, 44, 202, 117,
-    176, 92, 224, 236, 107, 111, 208, 237, 222, 213, 88, 179, 197, 158, 231, 191, 225, 238, 193,
-    214, 209, 112, 124, 219, 187, 180, 239, 226, 195, 192, 146, 93, 227, 240,
+    7, 3, 5, 0, 1, 2, 10, 73, 71, 33, 8, 16, 27, 32, 69, 11, 14, 81, 147, 12, 70, 6, 185, 31, 86,
+    35, 223, 109, 40, 76, 79, 34, 9, 48, 19, 41, 111, 15, 4, 29, 128, 38, 92, 152, 110, 54, 43,
+    74, 145, 108, 93, 24, 242, 67, 107, 90, 37, 204, 84, 60, 130, 168, 75, 59, 52, 46, 146, 224,
+    13, 129, 100, 17, 21, 155, 143, 83, 116, 62, 187, 36, 114, 117, 222, 26, 22, 112, 113, 206,
+    157, 105, 184, 82, 53, 88, 151, 166, 228, 25, 124, 65, 57, 94, 169, 45, 244, 85, 63, 207, 205,
+    78, 20, 42, 119, 87, 149, 219, 164, 160, 50, 153, 68, 23, 122, 138, 91, 183, 101, 51, 231,
+    102, 221, 135, 193, 47, 132, 18, 192, 133, 120, 233, 106, 171, 131, 243, 55, 49, 126, 176,
+    121, 227, 127, 154, 170, 250, 150, 165, 159, 186, 28, 95, 172, 162, 203, 188, 39, 136, 245,
+    202, 89, 115, 167, 161, 66, 123, 58, 225, 189, 240, 226, 174, 139, 64, 148, 72, 195, 125, 247,
+    30, 96, 56, 200, 241, 179, 259, 260, 261, 181, 196, 252, 97, 236, 180, 175, 194, 198, 80, 158,
+    44, 251, 163, 214, 98, 156, 230, 103, 220, 182, 173, 262, 263, 141, 255, 264, 215, 257, 199,
+    190, 208, 235, 212, 232, 177, 197, 77, 246, 140, 217, 229, 178, 265, 237, 248, 249, 256, 211,
+    201, 209, 134, 238, 258, 104, 137, 142, 118, 191, 213, 234, 61, 266, 218, 239, 144, 254, 210,
+    216, 253, 99, 267,
 )
 REDUCE_ORDER = (
-    30, 232, 8, 29, 7, 84, 33, 15, 0, 6, 231, 9, 10, 18, 85, 14, 233, 1, 35, 2, 41, 134, 234, 235,
-    118, 87, 86, 91, 92, 119, 12, 236, 51, 137, 42, 34, 36, 89, 28, 237, 31, 11, 19, 133, 3, 240,
-    215, 52, 37, 238, 27, 21, 93, 88, 141, 122, 214, 94, 140, 22, 20, 106, 219, 23, 43, 100, 53,
-    38, 239, 166, 44, 17, 69, 4, 165, 116, 13, 120, 138, 167, 95, 26, 39, 110, 104, 101, 123, 221,
-    217, 149, 25, 157, 222, 108, 45, 67, 173, 68, 90, 32, 172, 96, 136, 16, 135, 117, 54, 24, 71,
-    46, 183, 124, 126, 197, 5, 220, 199, 200, 169, 224, 102, 241, 40, 103, 57, 121, 216, 170, 198,
-    184, 151, 143, 242, 75, 72, 70, 105, 174, 55, 47, 63, 168, 243, 58, 73, 187, 74, 153, 223,
-    139, 127, 61, 125, 181, 185, 150, 48, 218, 76, 49, 109, 175, 128, 59, 154, 159, 205, 171, 56,
-    226, 97, 107, 145, 225, 201, 177, 202, 176, 142, 152, 182, 98, 50, 62, 227, 189, 155, 111, 77,
-    203, 60, 191, 207, 193, 178, 206, 179, 129, 158, 130, 79, 161, 204, 78, 228, 112, 156, 144,
-    188, 131, 209, 186, 64, 99, 65, 160, 180, 113, 208, 114, 132, 192, 190, 162, 163, 80, 81, 146,
-    147, 210, 66, 211, 229, 194, 82, 164, 195, 148, 212, 115, 83, 196, 213, 230,
+    215, 14, 3, 7, 2, 0, 8, 214, 216, 38, 1, 10, 84, 133, 85, 37, 9, 33, 11, 217, 36, 218, 28, 86,
+    87, 35, 29, 12, 219, 4, 5, 92, 17, 89, 57, 91, 220, 221, 21, 88, 24, 26, 34, 40, 42, 94, 222,
+    16, 23, 22, 136, 44, 165, 223, 168, 93, 15, 197, 39, 20, 43, 202, 51, 134, 135, 166, 53, 167,
+    45, 67, 6, 19, 68, 102, 170, 204, 47, 141, 126, 198, 143, 96, 18, 25, 172, 173, 95, 71, 54,
+    116, 52, 30, 103, 118, 119, 151, 41, 55, 46, 149, 117, 138, 106, 174, 59, 199, 181, 175, 27,
+    75, 31, 200, 13, 169, 61, 205, 69, 58, 139, 70, 150, 206, 185, 108, 140, 224, 90, 77, 183,
+    120, 121, 48, 203, 137, 49, 72, 189, 100, 225, 226, 56, 63, 177, 191, 171, 124, 76, 142, 122,
+    60, 104, 187, 97, 123, 32, 201, 73, 98, 145, 74, 144, 155, 110, 153, 79, 182, 128, 176, 127,
+    146, 62, 125, 152, 78, 159, 184, 101, 107, 157, 147, 186, 207, 64, 65, 80, 178, 179, 105, 148,
+    193, 188, 208, 99, 154, 66, 190, 81, 129, 130, 109, 112, 156, 209, 111, 161, 82, 192, 158,
+    210, 160, 211, 131, 180, 113, 114, 162, 163, 50, 194, 195, 83, 212, 132, 164, 115, 196, 213,
 )
 
 MESH = pl.DeviceIdType.MESH
@@ -771,47 +772,6 @@
     return [actions[i][1] for i in order]
 
 
-def reduce_kernel(parts, blocks, order, *refs):
-    count = len(parts)
-    grads, refs = refs[:count], refs[count:]
-    ins, refs = refs[:blocks], refs[blocks:]
-    outs, refs = refs[:count], refs[count:]
-    swapped, refs = refs[:blocks], refs[blocks:]
-    scratch, (send, recv, load), sems = refs[:-6], refs[-6:-3], refs[-3:]
-    place = Place()
-    greet(place)
-    swap = Swap(place, ins, swapped, *sems)
-    swap.start()
-    work = Reduce(place, parts, grads, outs, scratch, send, recv, load)
-    for step in in_order(work.actions(), order):
-        step()
-    swap.finish()
-
-
-def reduce_call(arrays, blocks, parts, collective_id, order=None):
-    labels = reduce_labels(parts)
-    count = len(arrays)
-    return pl.pallas_call(
-        functools.partial(reduce_kernel, parts, len(blocks), order),
-        out_shape=[jax.ShapeDtypeStruct((p.rows, p.columns), p.dtype) for p in parts]
-        + [jax.ShapeDtypeStruct(b.shape, b.dtype) for b in blocks],
-        in_specs=[pl.BlockSpec(memory_space=pltpu.HBM)] * (count + len(blocks)),
-        out_specs=[pl.BlockSpec(memory_space=pltpu.VMEM)] * count
-        + [pl.BlockSpec(memory_space=pltpu.HBM)] * len(blocks),
-        scratch_shapes=reduce_scratch(parts)
-        + [
-            pltpu.SemaphoreType.DMA((len(labels.numbers),)),
-            pltpu.SemaphoreType.DMA((len(labels.numbers),)),
-            pltpu.SemaphoreType.DMA((count * 2 * len(SPOTS),)),
-        ]
-        + swap_scratch(len(blocks)),
-        compiler_params=pltpu.CompilerParams(
-            collective_id=collective_id, has_side_effects=True, vmem_limit_bytes=63 << 20
-        ),
-        name="reduce_gradients",
-    )(*arrays, *blocks)
-
-
 def column_part(rows, columns, shared, early, inside=False):
     half = columns // 2
     part = (half - shared) // 2
@@ -847,8 +807,9 @@
 ROW_QUERY, ROW_VALUE, ROW_OUTPUT, ROW_GAIN1, ROW_SHIFT1, ROW_INNER, INNER = 0, 1, 2, 3, 4, 5, 4
 ROW_OUTER, ROW_GAIN2, ROW_SHIFT2 = 9, 10, 11
 TABLE_ROWS = 16
+VMEM = 67043328
 LANES = 128
-BAND = 32
+BAND = 128
 
 
 def spread_table(table_ref, vec):
@@ -1100,7 +1061,7 @@
             pltpu.SemaphoreType.DMA((3, tiles)),
             pltpu.SemaphoreType.DMA((2, 2)),
         ],
-        compiler_params=pltpu.CompilerParams(vmem_limit_bytes=60 << 20),
+        compiler_params=pltpu.CompilerParams(vmem_limit_bytes=VMEM),
         name="feed_forward",
     )(rows, context, cot, lengths, table, output_w, inner_w, outer_w)
 
@@ -1163,7 +1124,7 @@
             pltpu.SemaphoreType.DMA((len(arrays) + 1,)),
             pltpu.SemaphoreType.DMA((len(shapes) + sum(lines),)),
         ],
-        compiler_params=pltpu.CompilerParams(vmem_limit_bytes=40 << 20),
+        compiler_params=pltpu.CompilerParams(vmem_limit_bytes=VMEM),
         name="widen_results",
     )(*arrays, table)
 
@@ -1408,7 +1369,7 @@
         ]
         + swap_scratch(1) * 2,
         compiler_params=pltpu.CompilerParams(
-            collective_id=collective_id, has_side_effects=True, vmem_limit_bytes=48 << 20
+            collective_id=collective_id, has_side_effects=True, vmem_limit_bytes=VMEM
         ),
         name="gather_attention_forward",
     )(*shares, *blocks, lengths)
@@ -1659,7 +1620,7 @@
         ]
         + swap_scratch(1) * 2,
         compiler_params=pltpu.CompilerParams(
-            collective_id=collective_id, has_side_effects=True, vmem_limit_bytes=63 << 20
+            collective_id=collective_id, has_side_effects=True, vmem_limit_bytes=VMEM
         ),
         name="attention_backward_reduce",
     )(rows, qkv, away, grad, table, first_grad, probs, weight, *grads, block)

time: 300 us -> 276 us (0.920)
  local copies, waits for them, and re-layouts: 19.1 us -> 1.3 us
  Pallas kernels: 278 us -> 272 us
    unnamed x41 -> x1, local copies, waits for them, and re-layouts: 19.1 us -> 1.3 us
    pallas_call x1, Pallas kernels: 33.5 us -> 30.3 us  [middle(): pl.pallas_call(middle_kernel, out_shape=[jax.ShapeDtypeStruct((count, wid...]
where the time goes in v2:
time: 276 us
  Pallas kernels  272 us (99%)
    pallas_call x1, Pallas kernels, finish(): pl.pallas_call(functools.partial(finish_kernel, parts, order), out_shape=...  125 us
    pallas_call x1, Pallas kernels, start(): pl.pallas_call(functools.partial(start_kernel, flows, spots, order), out_...  112 us
    pallas_call x1, Pallas kernels, middle(): pl.pallas_call(middle_kernel, out_shape=[jax.ShapeDtypeStruct((count, wid...  30.3 us

profile of v2, /device:TPU:1, one launch (start us, length us, event | category | flops | bytes accessed | tf_op | source)
XLA Modules:
  0.0 275.7 jit_solution(14171308044424517287)
XLA Ops:
  0.7 1.3 copy.35.refs_9_.lengths_ref
  2.0 1.4 add_convert_fusion.refs_0_
  3.3 112.4 %gather_attention_forward.1 = (bf16[128,128]{1,0:T(8,128)(2,1)}, bf16[1024,3072]{1,0:T(8,128)(2,1)}, bf16[1024,1024]{1,0:T(8,128)(2,1)}, bf16[1024,4096]{1,0:T(8...) custom-call(bf16[16,128]{1,0:T(8,128)(2,1)} %add_convert_fusion.refs, ...), custom_call_target="tpu_custom_call" | custom-call | tf_op jit(solution)/shard_map/gather_attention_forward/pallas_call | solution.py:1343
  115.8 30.3 %feed_forward.1 = (bf16[256,1024]{1,0:T(8,128)(2,1)}, f32[256,1024]{1,0:T(8,128)}, bf16[256,1024]{1,0:T(8,128)(2,1)}, f32[128,128]{1,0:T(8,128)}, bf16[1024,1024...) custom-call(bf16[256,1024]{1,0:T(8,128)(2,1)} %bitcast.20, ...), custom_call_target="tpu_custom_call" | custom-call | tf_op jit(solution)/shard_map/feed_forward/pallas_call | solution.py:1030
  146.1 124.8 %attention_backward_reduce.1 = (bf16[128,4096]{1,0:T(8,128)(2,1)}, bf16[512,1024]{1,0:T(8,128)(2,1)}, bf16[128,1024]{1,0:T(8,128)(2,1)}, bf16[128,3072]{1,0:T(8,...) custom-call(bf16[256,1024]{1,0:T(8,128)(2,1)} %bitcast.21, ...), custom_call_target="tpu_custom_call" | custom-call | tf_op jit(solution)/shard_map/attention_backward_reduce/pallas_call | solution.py:1592
  270.9 4.6 %widen_results.1 = (f32[128,1024]{1,0:T(8,128)}, f32[128,1024]{1,0:T(8,128)}, f32[128,1024]{1,0:T(8,128)}, f32[128,1024]{1,0:T(8,128)}, f32[128,4096]{1,0:T(8,12...) custom-call(bf16[128,3072]{1,0:T(8,128)(2,1)} %get-tuple-element.77., ...), custom_call_target="tpu_custom_call" | custom-call | tf_op jit(solution)/shard_map/widen_results/pallas_call | solution.py:1116

commit v3 on v2

--- a/solution.py
+++ b/solution.py
@@ -13,35 +13,33 @@
 BF16 = jnp.bfloat16
 
 GATHER_SPLIT = ((256, 384), (256, 128), (1024, 128), (128, 64))
-REDUCE_SPLIT = ((512, 512), (128, 48), (256, 128), (1024, 256))
+REDUCE_SPLIT = ((1024, 512), (160, 0), (256, 128), (768, 256))
 GATHER_ORDER = (
-    7, 3, 5, 0, 1, 2, 10, 73, 71, 33, 8, 16, 27, 32, 69, 11, 14, 81, 147, 12, 70, 6, 185, 31, 86,
-    35, 223, 109, 40, 76, 79, 34, 9, 48, 19, 41, 111, 15, 4, 29, 128, 38, 92, 152, 110, 54, 43,
-    74, 145, 108, 93, 24, 242, 67, 107, 90, 37, 204, 84, 60, 130, 168, 75, 59, 52, 46, 146, 224,
-    13, 129, 100, 17, 21, 155, 143, 83, 116, 62, 187, 36, 114, 117, 222, 26, 22, 112, 113, 206,
-    157, 105, 184, 82, 53, 88, 151, 166, 228, 25, 124, 65, 57, 94, 169, 45, 244, 85, 63, 207, 205,
-    78, 20, 42, 119, 87, 149, 219, 164, 160, 50, 153, 68, 23, 122, 138, 91, 183, 101, 51, 231,
-    102, 221, 135, 193, 47, 132, 18, 192, 133, 120, 233, 106, 171, 131, 243, 55, 49, 126, 176,
-    121, 227, 127, 154, 170, 250, 150, 165, 159, 186, 28, 95, 172, 162, 203, 188, 39, 136, 245,
-    202, 89, 115, 167, 161, 66, 123, 58, 225, 189, 240, 226, 174, 139, 64, 148, 72, 195, 125, 247,
-    30, 96, 56, 200, 241, 179, 259, 260, 261, 181, 196, 252, 97, 236, 180, 175, 194, 198, 80, 158,
-    44, 251, 163, 214, 98, 156, 230, 103, 220, 182, 173, 262, 263, 141, 255, 264, 215, 257, 199,
-    190, 208, 235, 212, 232, 177, 197, 77, 246, 140, 217, 229, 178, 265, 237, 248, 249, 256, 211,
-    201, 209, 134, 238, 258, 104, 137, 142, 118, 191, 213, 234, 61, 266, 218, 239, 144, 254, 210,
-    216, 253, 99, 267,
+    3, 4, 7, 10, 0, 2, 32, 66, 1, 38, 17, 100, 8, 29, 63, 5, 68, 30, 64, 106, 35, 62, 98, 97, 168,
+    72, 174, 103, 77, 69, 136, 191, 43, 34, 74, 13, 81, 96, 132, 79, 12, 28, 47, 111, 142, 134,
+    15, 164, 204, 131, 153, 137, 102, 49, 145, 210, 140, 9, 165, 213, 14, 117, 208, 40, 200, 83,
+    46, 76, 166, 99, 42, 31, 171, 18, 70, 78, 179, 170, 135, 221, 175, 183, 101, 217, 118, 185,
+    151, 48, 65, 123, 169, 130, 199, 50, 11, 108, 36, 112, 6, 143, 218, 23, 55, 21, 86, 198, 157,
+    115, 149, 216, 82, 202, 59, 209, 180, 205, 196, 110, 138, 24, 141, 148, 167, 182, 184, 144,
+    152, 52, 37, 162, 150, 128, 25, 188, 197, 91, 71, 41, 133, 33, 214, 219, 154, 116, 186, 230,
+    222, 22, 53, 44, 57, 67, 114, 109, 89, 73, 16, 120, 113, 201, 172, 85, 51, 215, 220, 20, 178,
+    87, 211, 104, 80, 84, 158, 225, 45, 26, 181, 155, 19, 187, 75, 203, 163, 94, 192, 159, 212,
+    147, 232, 233, 39, 231, 161, 206, 90, 124, 119, 223, 234, 60, 92, 121, 93, 105, 235, 146, 139,
+    125, 56, 176, 236, 237, 207, 195, 226, 229, 107, 58, 95, 173, 129, 189, 126, 227, 127, 54,
+    193, 238, 88, 156, 177, 160, 27, 122, 228, 194, 61, 239, 224, 190, 240,
 )
 REDUCE_ORDER = (
-    215, 14, 3, 7, 2, 0, 8, 214, 216, 38, 1, 10, 84, 133, 85, 37, 9, 33, 11, 217, 36, 218, 28, 86,
-    87, 35, 29, 12, 219, 4, 5, 92, 17, 89, 57, 91, 220, 221, 21, 88, 24, 26, 34, 40, 42, 94, 222,
-    16, 23, 22, 136, 44, 165, 223, 168, 93, 15, 197, 39, 20, 43, 202, 51, 134, 135, 166, 53, 167,
-    45, 67, 6, 19, 68, 102, 170, 204, 47, 141, 126, 198, 143, 96, 18, 25, 172, 173, 95, 71, 54,
-    116, 52, 30, 103, 118, 119, 151, 41, 55, 46, 149, 117, 138, 106, 174, 59, 199, 181, 175, 27,
-    75, 31, 200, 13, 169, 61, 205, 69, 58, 139, 70, 150, 206, 185, 108, 140, 224, 90, 77, 183,
-    120, 121, 48, 203, 137, 49, 72, 189, 100, 225, 226, 56, 63, 177, 191, 171, 124, 76, 142, 122,
-    60, 104, 187, 97, 123, 32, 201, 73, 98, 145, 74, 144, 155, 110, 153, 79, 182, 128, 176, 127,
-    146, 62, 125, 152, 78, 159, 184, 101, 107, 157, 147, 186, 207, 64, 65, 80, 178, 179, 105, 148,
-    193, 188, 208, 99, 154, 66, 190, 81, 129, 130, 109, 112, 156, 209, 111, 161, 82, 192, 158,
-    210, 160, 211, 131, 180, 113, 114, 162, 163, 50, 194, 195, 83, 212, 132, 164, 115, 196, 213,
+    7, 8, 10, 3, 198, 14, 68, 9, 0, 67, 200, 70, 69, 85, 86, 12, 199, 11, 201, 2, 1, 74, 28, 5,
+    75, 35, 72, 15, 4, 83, 84, 89, 202, 71, 203, 77, 16, 34, 38, 29, 13, 42, 36, 100, 40, 204, 39,
+    76, 90, 207, 205, 17, 18, 21, 24, 107, 22, 23, 206, 132, 135, 25, 43, 104, 87, 88, 134, 78,
+    37, 133, 91, 93, 94, 6, 136, 164, 30, 165, 33, 32, 139, 45, 185, 148, 182, 208, 26, 79, 102,
+    73, 31, 184, 209, 210, 44, 53, 140, 154, 47, 150, 20, 141, 181, 137, 27, 101, 41, 116, 166,
+    55, 51, 19, 168, 57, 92, 143, 158, 174, 120, 156, 183, 138, 170, 189, 167, 103, 118, 188, 151,
+    152, 54, 95, 155, 109, 172, 80, 81, 142, 46, 176, 186, 96, 61, 108, 149, 191, 52, 59, 122,
+    159, 105, 97, 106, 48, 144, 190, 169, 49, 82, 119, 117, 56, 110, 187, 193, 145, 146, 58, 111,
+    153, 124, 63, 60, 123, 121, 112, 62, 98, 192, 126, 160, 50, 157, 113, 114, 171, 125, 173, 194,
+    195, 99, 64, 65, 175, 128, 127, 161, 162, 177, 178, 129, 130, 115, 196, 147, 179, 66, 131,
+    163, 180, 197,
 )
 
 MESH = pl.DeviceIdType.MESH
@@ -376,7 +374,7 @@
 def row_flows(array, shard_rows, columns, shared, early):
     half = shard_rows // 2
     part = (half - shared) // 2
-    return [
+    flows = [
         Flow(array, shard_rows, lambda core, side: (core * half, shared, 0, columns)),
         Flow(
             array,
@@ -392,6 +390,7 @@
             sides=True,
         ),
     ]
+    return [flow for flow in flows if flow.region(0, 0)[1]]
 
 
 class Part:
@@ -788,16 +787,12 @@
 def row_part(rows, columns, shared, early):
     half = rows // 2
     part = (half - shared) // 2
-    return Part(
-        rows,
-        columns,
-        "rows",
-        [
-            (lambda side: 0, shared, "line", False),
-            (lambda side: shared + side * part, early, "line", True),
-            (lambda side: shared + side * part + early, part - early, "pair", True),
-        ],
-    )
+    flows = [
+        (lambda side: 0, shared, "line", False),
+        (lambda side: shared + side * part, early, "line", True),
+        (lambda side: shared + side * part + early, part - early, "pair", True),
+    ]
+    return Part(rows, columns, "rows", [flow for flow in flows if flow[1]])
 
 
 def vector_part(rows, columns, inside=False):
@@ -836,21 +831,28 @@
 
 
 def middle_kernel(
-    rows_ref,
-    context_ref,
-    cot_ref,
+    rows_far,
+    context_far,
+    cot_far,
     lengths_ref,
     table_ref,
     output_w,
     inner_w,
     outer_w,
+    out_far,
+    first_grad_far,
+    context_grad_far,
+    sums_ref,
+    output_far,
+    inner_g,
+    outer_g,
+    rows_ref,
+    context_ref,
+    cot_ref,
     out_ref,
     first_grad_ref,
     context_grad_ref,
-    sums_ref,
     output_g,
-    inner_g,
-    outer_g,
     output_v,
     inner_v,
     outer_v,
@@ -859,7 +861,6 @@
     active,
     slope,
     unit1,
-    unit2,
     rate1,
     total,
     low,
@@ -870,12 +871,13 @@
     outer_b,
     load,
     save,
+    few,
 ):
     rows, width = rows_ref.shape
     tiles, _, tile = inner_v.shape
     ctx = lax.axis_index("ctx")
     side, core = lax.div(ctx, 2), lax.rem(ctx, 2)
-    length = lengths_ref[side, 0]
+    length = lengths_ref[side]
     bands = rows // BAND
 
     def inner_load(t):
@@ -888,15 +890,26 @@
             outer_w.at[pl.ds(pl.multiple_of(t * tile, tile), tile), :], outer_v.at[t], load.at[1, t]
         )
 
-    output_load = pltpu.make_async_copy(output_w, output_v, load.at[2, 0])
-    output_load.start()
-    for t in range(tiles):
+    output_load = pltpu.make_async_copy(output_w, output_v, few.at[0])
+    context_load = pltpu.make_async_copy(context_far, context_ref, few.at[1])
+    rows_load = pltpu.make_async_copy(rows_far, rows_ref, few.at[2])
+    cot_load = pltpu.make_async_copy(cot_far, cot_ref, few.at[3])
+    out_save = pltpu.make_async_copy(out_ref, out_far, few.at[4])
+    first_save = pltpu.make_async_copy(first_grad_ref, first_grad_far, few.at[5])
+    context_save = pltpu.make_async_copy(context_grad_ref, context_grad_far, few.at[6])
+    output_save = pltpu.make_async_copy(output_g, output_far, few.at[7])
+    for copy in (context_load, output_load, rows_load):
+        copy.start()
+    spread_table(table_ref, vec)
+    sums[...] = jnp.zeros_like(sums)
+    context_load.wait()
+    output_load.wait()
+    ahead = 3
+    for t in range(ahead):
         inner_load(t).start()
         outer_load(t).start()
-    spread_table(table_ref, vec)
-    sums[...] = jnp.zeros_like(sums)
-    output_load.wait()
     total[...] = plain_product(context_ref[...], output_v[...])
+    rows_load.wait()
 
     def band_of(b):
         return pl.ds(pl.multiple_of(b * BAND, BAND), BAND)
@@ -917,8 +930,16 @@
     lax.fori_loop(0, bands, first_norm, 0)
     low_t[...] = low[...].T
 
+    cot_load.start()
+
     def forward(t, carry):
         inner_load(t).wait()
+
+        @pl.when(t + ahead < tiles)
+        def _():
+            inner_load(t + ahead).start()
+            outer_load(t + ahead).start()
+
         bias = jnp.concatenate(
             [
                 vec[pl.ds(ROW_INNER + k, 1), pl.ds(pl.multiple_of(t * LANES, LANES), LANES)]
@@ -935,6 +956,8 @@
         return carry
 
     lax.fori_loop(0, tiles, forward, 0)
+
+    cot_load.wait()
 
     def second_norm(b, carry):
         here = band_of(b)
@@ -954,6 +977,7 @@
         return carry
 
     lax.fori_loop(0, bands, second_norm, 0)
+    out_save.start()
 
     def inner_save(t):
         slot = lax.rem(t, 2)
@@ -1008,12 +1032,17 @@
         return carry
 
     lax.fori_loop(0, bands, first_back, 0)
+    output_g[...] = left_product(context_ref[...], second_low[...]).astype(BF16)
+    first_save.start()
     context_grad_ref[...] = right_product(second_low[...], output_v[...]).astype(BF16)
-    output_g[...] = left_product(context_ref[...], second_low[...]).astype(BF16)
+    output_save.start()
     fold_table(sums, sums_ref, 0, TABLE_ROWS)
+    context_save.start()
     for t in range(tiles - 2, tiles):
         outer_save(t).wait()
         inner_save(t).wait()
+    for copy in (out_save, first_save, output_save, context_save):
+        copy.wait()
 
 
 def middle(rows, context, cot, lengths, table, output_w, inner_w, outer_w):
@@ -1038,9 +1067,16 @@
             jax.ShapeDtypeStruct(inner_w.shape, BF16),
             jax.ShapeDtypeStruct(outer_w.shape, BF16),
         ],
-        in_specs=[whole] * 3 + [pl.BlockSpec(memory_space=pltpu.SMEM), whole] + [far] * 3,
-        out_specs=[whole] * 5 + [far] * 2,
+        in_specs=[far] * 3 + [pl.BlockSpec(memory_space=pltpu.SMEM), whole] + [far] * 3,
+        out_specs=[far] * 3 + [whole] + [far] * 3,
         scratch_shapes=[
+            space(BF16),
+            space(BF16),
+            space(BF16),
+            space(BF16),
+            space(F32),
+            space(BF16),
+            pltpu.VMEM(output_w.shape, BF16),
             pltpu.VMEM(output_w.shape, BF16),
             pltpu.VMEM((tiles, width, tile), BF16),
             pltpu.VMEM((tiles, tile, width), BF16),
@@ -1049,7 +1085,6 @@
             pltpu.VMEM((tiles, count, tile), BF16),
             pltpu.VMEM((tiles, count, tile), F32),
             space(F32),
-            pltpu.VMEM((8, LANES), F32),
             pltpu.VMEM((count, LANES), F32),
             space(F32),
             space(BF16),
@@ -1058,8 +1093,9 @@
             space(BF16),
             pltpu.VMEM((2, width, tile), BF16),
             pltpu.VMEM((2, tile, width), BF16),
-            pltpu.SemaphoreType.DMA((3, tiles)),
+            pltpu.SemaphoreType.DMA((2, tiles)),
             pltpu.SemaphoreType.DMA((2, 2)),
+            pltpu.SemaphoreType.DMA((8,)),
         ],
         compiler_params=pltpu.CompilerParams(vmem_limit_bytes=VMEM),
         name="feed_forward",
@@ -1302,7 +1338,7 @@
     ]
     greet(place)
     rows_count = context.shape[0]
-    length = lengths_ref[place.side, 0]
+    length = lengths_ref[place.side]
     row = lax.broadcasted_iota(jnp.int32, (8, rows_count), 1)
     for k, core in enumerate((place.core, 1 - place.core)):
         bias[:, pl.ds(k * rows_count, rows_count)] = jnp.where(
@@ -1856,6 +1892,7 @@
 def direct_body(inputs, cotangent, lengths, vectors, weights):
     micro, seqs, block_len, width = inputs.shape
     shards = LINE * PAIR
+    lengths = lengths.reshape(micro)
     rows = 2 * block_len
     table = jnp.zeros((TABLE_ROWS, LANES), F32)
     row = 0

time: 276 us -> 269 us (0.975)
  Pallas kernels: 272 us -> 267 us
    pallas_call x1, Pallas kernels: 112 us -> 109 us  [start(): pl.pallas_call(functools.partial(start_kernel, flows, spots, order), out_...]
where the time goes in v3:
time: 269 us
  Pallas kernels  267 us (99%)
    pallas_call x1, Pallas kernels, finish(): pl.pallas_call(functools.partial(finish_kernel, parts, order), out_shape=...  123 us
    pallas_call x1, Pallas kernels, start(): pl.pallas_call(functools.partial(start_kernel, flows, spots, order), out_...  109 us
    pallas_call x1, Pallas kernels, middle(): pl.pallas_call(middle_kernel, out_shape=[jax.ShapeDtypeStruct((count, wid...  29.6 us

profile of v3, /device:TPU:1, one launch (start us, length us, event | category | flops | bytes accessed | tf_op | source)
XLA Modules:
  0.0 269.0 jit_solution(18387460499204108024)
XLA Ops:
  0.7 1.4 add_convert_fusion.refs_0_
  2.1 109.2 %gather_attention_forward.1 = (bf16[128,128]{1,0:T(8,128)(2,1)}, bf16[1024,3072]{1,0:T(8,128)(2,1)}, bf16[1024,1024]{1,0:T(8,128)(2,1)}, bf16[1024,4096]{1,0:T(8...) custom-call(bf16[16,128]{1,0:T(8,128)(2,1)} %add_convert_fusion.refs, ...), custom_call_target="tpu_custom_call" | custom-call | tf_op jit(solution)/shard_map/gather_attention_forward/pallas_call | solution.py:1379
  111.3 29.6 %feed_forward.1 = (bf16[256,1024]{1,0:T(8,128)(2,1)}, f32[256,1024]{1,0:T(8,128)}, bf16[256,1024]{1,0:T(8,128)(2,1)}, f32[128,128]{1,0:T(8,128)}, bf16[1024,1024...) custom-call(bf16[256,1024]{1,0:T(8,128)(2,1)} %bitcast.21, ...), custom_call_target="tpu_custom_call" | custom-call | tf_op jit(solution)/shard_map/feed_forward/pallas_call | solution.py:1059
  140.9 123.3 %attention_backward_reduce.1 = (bf16[128,4096]{1,0:T(8,128)(2,1)}, bf16[512,1024]{1,0:T(8,128)(2,1)}, bf16[128,1024]{1,0:T(8,128)(2,1)}, bf16[128,3072]{1,0:T(8,...) custom-call(bf16[256,1024]{1,0:T(8,128)(2,1)} %bitcast.22, ...), custom_call_target="tpu_custom_call" | custom-call | tf_op jit(solution)/shard_map/attention_backward_reduce/pallas_call | solution.py:1628
  264.3 4.6 %widen_results.1 = (f32[128,1024]{1,0:T(8,128)}, f32[128,1024]{1,0:T(8,128)}, f32[128,1024]{1,0:T(8,128)}, f32[128,1024]{1,0:T(8,128)}, f32[128,4096]{1,0:T(8,12...) custom-call(bf16[128,3072]{1,0:T(8,128)(2,1)} %get-tuple-element.77., ...), custom_call_target="tpu_custom_call" | custom-call | tf_op jit(solution)/shard_map/widen_results/pallas_call | solution.py:1152

commit v4 on v3

--- a/solution.py
+++ b/solution.py
@@ -13,33 +13,33 @@
 BF16 = jnp.bfloat16
 
 GATHER_SPLIT = ((256, 384), (256, 128), (1024, 128), (128, 64))
-REDUCE_SPLIT = ((1024, 512), (160, 0), (256, 128), (768, 256))
+REDUCE_SPLIT = ((768, 256), (160, 48), (256, 128), (1024, 256))
 GATHER_ORDER = (
-    3, 4, 7, 10, 0, 2, 32, 66, 1, 38, 17, 100, 8, 29, 63, 5, 68, 30, 64, 106, 35, 62, 98, 97, 168,
-    72, 174, 103, 77, 69, 136, 191, 43, 34, 74, 13, 81, 96, 132, 79, 12, 28, 47, 111, 142, 134,
-    15, 164, 204, 131, 153, 137, 102, 49, 145, 210, 140, 9, 165, 213, 14, 117, 208, 40, 200, 83,
-    46, 76, 166, 99, 42, 31, 171, 18, 70, 78, 179, 170, 135, 221, 175, 183, 101, 217, 118, 185,
-    151, 48, 65, 123, 169, 130, 199, 50, 11, 108, 36, 112, 6, 143, 218, 23, 55, 21, 86, 198, 157,
-    115, 149, 216, 82, 202, 59, 209, 180, 205, 196, 110, 138, 24, 141, 148, 167, 182, 184, 144,
-    152, 52, 37, 162, 150, 128, 25, 188, 197, 91, 71, 41, 133, 33, 214, 219, 154, 116, 186, 230,
-    222, 22, 53, 44, 57, 67, 114, 109, 89, 73, 16, 120, 113, 201, 172, 85, 51, 215, 220, 20, 178,
-    87, 211, 104, 80, 84, 158, 225, 45, 26, 181, 155, 19, 187, 75, 203, 163, 94, 192, 159, 212,
-    147, 232, 233, 39, 231, 161, 206, 90, 124, 119, 223, 234, 60, 92, 121, 93, 105, 235, 146, 139,
-    125, 56, 176, 236, 237, 207, 195, 226, 229, 107, 58, 95, 173, 129, 189, 126, 227, 127, 54,
-    193, 238, 88, 156, 177, 160, 27, 122, 228, 194, 61, 239, 224, 190, 240,
+    10, 3, 2, 7, 4, 0, 8, 66, 64, 30, 5, 28, 1, 38, 43, 77, 72, 132, 15, 134, 98, 47, 111, 35,
+    166, 69, 140, 200, 145, 29, 103, 32, 97, 9, 183, 162, 74, 89, 128, 36, 100, 179, 114, 60, 63,
+    81, 106, 213, 67, 96, 180, 115, 34, 102, 68, 49, 12, 217, 94, 65, 201, 62, 149, 142, 141, 18,
+    164, 13, 208, 184, 99, 146, 31, 40, 168, 137, 76, 129, 78, 131, 16, 42, 83, 50, 136, 6, 61,
+    48, 51, 101, 209, 112, 174, 107, 151, 93, 117, 110, 225, 82, 171, 33, 14, 170, 123, 45, 214,
+    205, 130, 153, 144, 118, 52, 21, 19, 55, 202, 165, 119, 181, 169, 53, 175, 73, 113, 90, 218,
+    185, 152, 135, 116, 198, 133, 124, 199, 196, 150, 23, 120, 46, 85, 219, 59, 172, 167, 204,
+    203, 37, 108, 222, 22, 84, 148, 80, 188, 86, 71, 138, 79, 221, 220, 216, 20, 230, 212, 39, 11,
+    75, 210, 186, 178, 215, 154, 191, 182, 147, 232, 233, 70, 91, 234, 235, 17, 24, 104, 139, 105,
+    26, 121, 157, 236, 155, 176, 195, 163, 109, 143, 57, 226, 54, 159, 161, 92, 95, 211, 27, 25,
+    237, 197, 173, 56, 41, 177, 125, 127, 58, 231, 207, 238, 223, 160, 189, 193, 227, 44, 229,
+    126, 87, 88, 206, 122, 158, 187, 156, 239, 228, 190, 192, 194, 224, 240,
 )
 REDUCE_ORDER = (
-    7, 8, 10, 3, 198, 14, 68, 9, 0, 67, 200, 70, 69, 85, 86, 12, 199, 11, 201, 2, 1, 74, 28, 5,
-    75, 35, 72, 15, 4, 83, 84, 89, 202, 71, 203, 77, 16, 34, 38, 29, 13, 42, 36, 100, 40, 204, 39,
-    76, 90, 207, 205, 17, 18, 21, 24, 107, 22, 23, 206, 132, 135, 25, 43, 104, 87, 88, 134, 78,
-    37, 133, 91, 93, 94, 6, 136, 164, 30, 165, 33, 32, 139, 45, 185, 148, 182, 208, 26, 79, 102,
-    73, 31, 184, 209, 210, 44, 53, 140, 154, 47, 150, 20, 141, 181, 137, 27, 101, 41, 116, 166,
-    55, 51, 19, 168, 57, 92, 143, 158, 174, 120, 156, 183, 138, 170, 189, 167, 103, 118, 188, 151,
-    152, 54, 95, 155, 109, 172, 80, 81, 142, 46, 176, 186, 96, 61, 108, 149, 191, 52, 59, 122,
-    159, 105, 97, 106, 48, 144, 190, 169, 49, 82, 119, 117, 56, 110, 187, 193, 145, 146, 58, 111,
-    153, 124, 63, 60, 123, 121, 112, 62, 98, 192, 126, 160, 50, 157, 113, 114, 171, 125, 173, 194,
-    195, 99, 64, 65, 175, 128, 127, 161, 162, 177, 178, 129, 130, 115, 196, 147, 179, 66, 131,
-    163, 180, 197,
+    14, 8, 4, 7, 0, 116, 5, 10, 197, 9, 2, 1, 85, 39, 84, 198, 40, 123, 12, 35, 3, 15, 86, 87,
+    199, 92, 91, 200, 37, 36, 42, 89, 11, 94, 38, 201, 43, 32, 31, 69, 93, 29, 13, 88, 67, 68,
+    202, 203, 23, 70, 102, 205, 181, 18, 51, 117, 90, 61, 28, 19, 180, 24, 183, 22, 96, 95, 16,
+    132, 44, 100, 134, 118, 204, 104, 121, 17, 21, 148, 33, 110, 45, 124, 71, 72, 120, 34, 125,
+    77, 6, 101, 188, 20, 73, 74, 150, 119, 149, 47, 46, 151, 41, 57, 97, 190, 75, 136, 76, 103,
+    26, 156, 187, 133, 184, 126, 153, 168, 78, 164, 25, 185, 155, 106, 30, 127, 98, 182, 206, 152,
+    207, 105, 208, 158, 128, 79, 157, 122, 165, 189, 55, 53, 27, 52, 48, 108, 166, 80, 81, 154,
+    186, 135, 107, 172, 49, 170, 174, 54, 138, 160, 167, 129, 99, 159, 112, 169, 192, 56, 142,
+    191, 82, 59, 111, 130, 140, 161, 162, 109, 171, 176, 58, 63, 137, 173, 175, 139, 193, 194,
+    113, 114, 144, 62, 60, 131, 143, 177, 178, 141, 83, 50, 64, 65, 163, 145, 146, 115, 66, 179,
+    195, 147, 196,
 )
 
 MESH = pl.DeviceIdType.MESH
@@ -323,13 +323,24 @@
             for k, (here, there) in enumerate(zip(ins, outs))
         ]
 
-    def start(self):
-        for copy in self.away + self.stay:
-            copy.start()
+    def start(self, k=0):
+        self.away[k].start()
+        self.stay[k].start()
+
+    def wait_here(self, k):
+        self.away[k].wait_recv()
+        self.stay[k].wait()
+        self.held = k
+
+    held = None
 
     def finish(self):
-        for copy in self.away + self.stay:
-            copy.wait()
+        for k, (away, stay) in enumerate(zip(self.away, self.stay)):
+            if k == self.held:
+                away.wait_send()
+            else:
+                away.wait()
+                stay.wait()
 
 
 def swap_scratch(count):
@@ -872,13 +883,19 @@
     load,
     save,
     few,
+    swap_send,
+    swap_recv,
+    swap_local,
 ):
     rows, width = rows_ref.shape
     tiles, _, tile = inner_v.shape
-    ctx = lax.axis_index("ctx")
-    side, core = lax.div(ctx, 2), lax.rem(ctx, 2)
+    place = Place()
+    side, core = place.side, place.core
     length = lengths_ref[side]
     bands = rows // BAND
+    assert BAND == cot_ref.shape[1]
+    barrier = pltpu.get_barrier_semaphore()
+    pl.semaphore_signal(barrier, inc=1, device_id=place.beside(), device_id_type=MESH)
 
     def inner_load(t):
         return pltpu.make_async_copy(
@@ -893,8 +910,9 @@
     output_load = pltpu.make_async_copy(output_w, output_v, few.at[0])
     context_load = pltpu.make_async_copy(context_far, context_ref, few.at[1])
     rows_load = pltpu.make_async_copy(rows_far, rows_ref, few.at[2])
-    cot_load = pltpu.make_async_copy(cot_far, cot_ref, few.at[3])
-    out_save = pltpu.make_async_copy(out_ref, out_far, few.at[4])
+    turn = Swap(
+        place, [cot_far, out_ref], [cot_ref, out_far], swap_send, swap_recv, swap_local
+    )
     first_save = pltpu.make_async_copy(first_grad_ref, first_grad_far, few.at[5])
     context_save = pltpu.make_async_copy(context_grad_ref, context_grad_far, few.at[6])
     output_save = pltpu.make_async_copy(output_g, output_far, few.at[7])
@@ -904,6 +922,8 @@
     sums[...] = jnp.zeros_like(sums)
     context_load.wait()
     output_load.wait()
+    pl.semaphore_wait(barrier, 1)
+    turn.start(0)
     ahead = 3
     for t in range(ahead):
         inner_load(t).start()
@@ -930,7 +950,6 @@
     lax.fori_loop(0, bands, first_norm, 0)
     low_t[...] = low[...].T
 
-    cot_load.start()
 
     def forward(t, carry):
         inner_load(t).wait()
@@ -957,7 +976,7 @@
 
     lax.fori_loop(0, tiles, forward, 0)
 
-    cot_load.wait()
+    turn.wait_here(0)
 
     def second_norm(b, carry):
         here = band_of(b)
@@ -965,8 +984,8 @@
         row = b * BAND + lax.broadcasted_iota(jnp.int32, (BAND, width), 0)
         mask = (row_place(row, core, rows) < length).astype(F32)
         gain = vec[pl.ds(ROW_GAIN2, 1), :]
-        out_ref[here, :] = ((unit * gain + vec[pl.ds(ROW_SHIFT2, 1), :]) * mask).astype(BF16)
-        out_grad = cot_ref[here, :].astype(F32) * mask
+        out_ref[b] = ((unit * gain + vec[pl.ds(ROW_SHIFT2, 1), :]) * mask).astype(BF16)
+        out_grad = cot_ref[b].astype(F32) * mask
         grad = norm_back(unit, rate, out_grad * gain)
         second[here, :] = grad
         grad_low = grad.astype(BF16)
@@ -977,7 +996,7 @@
         return carry
 
     lax.fori_loop(0, bands, second_norm, 0)
-    out_save.start()
+    turn.start(1)
 
     def inner_save(t):
         slot = lax.rem(t, 2)
@@ -1041,11 +1060,12 @@
     for t in range(tiles - 2, tiles):
         outer_save(t).wait()
         inner_save(t).wait()
-    for copy in (out_save, first_save, output_save, context_save):
+    for copy in (first_save, output_save, context_save):
         copy.wait()
-
-
-def middle(rows, context, cot, lengths, table, output_w, inner_w, outer_w):
+    turn.finish()
+
+
+def middle(collective_id, rows, context, cot, lengths, table, output_w, inner_w, outer_w):
     count, width = rows.shape
     hidden = inner_w.shape[1]
     tile = INNER * LANES
@@ -1059,7 +1079,7 @@
     return pl.pallas_call(
         middle_kernel,
         out_shape=[
-            jax.ShapeDtypeStruct((count, width), BF16),
+            jax.ShapeDtypeStruct(cot.shape, BF16),
             jax.ShapeDtypeStruct((count, width), F32),
             jax.ShapeDtypeStruct((count, width), BF16),
             jax.ShapeDtypeStruct(table.shape, F32),
@@ -1072,8 +1092,8 @@
         scratch_shapes=[
             space(BF16),
             space(BF16),
-            space(BF16),
-            space(BF16),
+            pltpu.VMEM(cot.shape, BF16),
+            pltpu.VMEM(cot.shape, BF16),
             space(F32),
             space(BF16),
             pltpu.VMEM(output_w.shape, BF16),
@@ -1096,8 +1116,11 @@
             pltpu.SemaphoreType.DMA((2, tiles)),
             pltpu.SemaphoreType.DMA((2, 2)),
             pltpu.SemaphoreType.DMA((8,)),
-        ],
-        compiler_params=pltpu.CompilerParams(vmem_limit_bytes=VMEM),
+        ]
+        + swap_scratch(2),
+        compiler_params=pltpu.CompilerParams(
+            collective_id=collective_id, has_side_effects=True, vmem_limit_bytes=VMEM
+        ),
         name="feed_forward",
     )(rows, context, cot, lengths, table, output_w, inner_w, outer_w)
 
@@ -1271,7 +1294,7 @@
 TABLE, QUERIES = 0, 1
 
 
-def start_actions(gather, work, keep, swaps, save, table_ref):
+def start_actions(gather, work, keep, swap, save, table_ref):
     found = gather.actions()
     others = [k for k in range(len(keep)) if k not in (TABLE, QUERIES)]
 
@@ -1279,7 +1302,7 @@
         gather.wait_twins((TABLE, QUERIES))
         for k in (TABLE, QUERIES):
             keep[k].wait()
-        swaps[0].finish()
+        swap.finish()
         spread_table(table_ref, work.vec)
         save.start()
 
@@ -1303,7 +1326,6 @@
         work.finish()
         for k in others:
             keep[k].wait()
-        swaps[1].finish()
         save.wait()
 
     found.append((("last",), last))
@@ -1313,11 +1335,11 @@
 def start_kernel(flows, spots, order, *refs):
     count = max(array for array, _ in spots) + 1
     shares, refs = refs[: len(spots)], refs[len(spots) :]
-    (in_block, cot_block, lengths_ref), refs = refs[:3], refs[3:]
+    (in_block, lengths_ref), refs = refs[:2], refs[2:]
     table_ref, refs = refs[0], refs[1:]
     far, refs = refs[: count - 1], refs[count - 1 :]
-    rows, cots, qkv, context, probs, away = refs[:6]
-    owns, refs = refs[6 : 6 + count], refs[6 + count :]
+    rows, qkv, context, probs, away = refs[:5]
+    owns, refs = refs[5 : 5 + count], refs[5 + count :]
     weight, held, vec, bias = refs[:4]
     send, recv, local, load, send2, recv2, save2, saveq = refs[4:12]
     fulls = (table_ref, weight) + tuple(far[1:])
@@ -1346,12 +1368,8 @@
         )
     for copy in loads:
         copy.wait()
-    swaps = [
-        Swap(place, [in_block], [rows], *refs[12:15]),
-        Swap(place, [cot_block], [cots], *refs[15:18]),
-    ]
-    for swap in swaps:
-        swap.start()
+    swap = Swap(place, [in_block], [rows], *refs[12:15])
+    swap.start()
     gather = Gather(place, flows, owns, fulls, send, recv)
     for copy in keep:
         copy.start()
@@ -1359,18 +1377,18 @@
         place, rows, weight, vec, bias, qkv, context, probs, held, away, send2, recv2, save2
     )
     save = pltpu.make_async_copy(weight, far[0], saveq.at[0])
-    for step in in_order(start_actions(gather, work, keep, swaps, save, table_ref), order):
+    for step in in_order(start_actions(gather, work, keep, swap, save, table_ref), order):
         step()
 
 
-def start(shares, spots, blocks, lengths, flows, shards, collective_id, order):
+def start(shares, spots, block, lengths, flows, shards, collective_id, order):
     labels = gather_labels(flows)
     count = max(array for array, _ in spots) + 1
     shapes = []
     for array in range(count):
         members = [share for share, spot in zip(shares, spots) if spot[0] == array]
         shapes.append((members[0].shape[0], sum(m.shape[1] for m in members)))
-    _, block_len, width = blocks[0].shape
+    _, block_len, width = block.shape
     rows = 2 * block_len
     pairs = width // SPAN
     far = pl.BlockSpec(memory_space=pltpu.HBM)
@@ -1379,15 +1397,15 @@
     return pl.pallas_call(
         functools.partial(start_kernel, flows, spots, order),
         out_shape=[jax.ShapeDtypeStruct((shards * r, c), BF16) for r, c in shapes]
-        + [jax.ShapeDtypeStruct(block.shape, BF16) for block in blocks]
         + [
+            jax.ShapeDtypeStruct(block.shape, BF16),
             jax.ShapeDtypeStruct((rows, 3 * width), BF16),
             jax.ShapeDtypeStruct((rows, width), BF16),
             jax.ShapeDtypeStruct(probs_shape, BF16),
             jax.ShapeDtypeStruct((rows, 2 * width), BF16),
         ],
-        in_specs=[far] * (len(shares) + 2) + [pl.BlockSpec(memory_space=pltpu.SMEM)],
-        out_specs=[whole] + [far] * (count - 1) + [whole, far] + [whole, whole, far, whole],
+        in_specs=[far] * (len(shares) + 1) + [pl.BlockSpec(memory_space=pltpu.SMEM)],
+        out_specs=[whole] + [far] * (count - 1) + [whole, whole, whole, far, whole],
         scratch_shapes=[pltpu.VMEM(shape, BF16) for shape in shapes]
         + [
             pltpu.VMEM((shards * shapes[QUERIES][0], shapes[QUERIES][1]), BF16),
@@ -1403,12 +1421,12 @@
             pltpu.SemaphoreType.DMA((pairs,)),
             pltpu.SemaphoreType.DMA((1,)),
         ]
-        + swap_scratch(1) * 2,
+        + swap_scratch(1),
         compiler_params=pltpu.CompilerParams(
             collective_id=collective_id, has_side_effects=True, vmem_limit_bytes=VMEM
         ),
         name="gather_attention_forward",
-    )(*shares, *blocks, lengths)
+    )(*shares, block, lengths)
 
 
 class AttentionBackward:
@@ -1566,7 +1584,7 @@
                 self.block[part] = self.total[pl.ds(part * rows, rows), :].astype(BF16)
 
 
-def finish_actions(reduce, finish, swaps):
+def finish_actions(reduce, finish, swap):
     queries, vectors = 3, 4
     place = reduce.place
     found = reduce.actions()
@@ -1576,7 +1594,6 @@
         finish.turn()
 
     found.append((("load",), load))
-    found.append((("swapout",), swaps[0].start))
     for group in range(GROUPS):
         found.append((("att", group), lambda group=group: finish.attend(group)))
     found.append((("settleatt",), finish.settle))
@@ -1585,38 +1602,34 @@
     found.append((("sums",), lambda: finish.bias_sums(reduce.own[vectors])))
     for half in range(HALVES):
         found.append((("dx", half), lambda half=half: finish.spread(half)))
-    found.append((("swapin",), swaps[1].start))
+    found.append((("swapin",), swap.start))
     return found
 
 
 def finish_kernel(parts, order, *refs):
     rows_ref, qkv, away, grad, table_ref, first_grad, probs, weight = refs[:8]
-    grads, out_block = list(refs[8:11]), refs[11]
-    outs, swapped, refs = refs[12:17], refs[17:19], refs[19:]
+    grads = list(refs[8:11])
+    outs, swapped, refs = refs[11:16], refs[16], refs[17:]
     leave_q, tiles, held, out, keep, leave, come, total, sums, rows_t, block = refs[:11]
     send2, recv2, load2, sems = refs[11:15]
-    scratch, rest = refs[15:-9], refs[-9:]
+    scratch, rest = refs[15:-6], refs[-6:]
     place = Place()
     work = AttentionBackward(place, qkv, away, grad, out, keep, leave, come, send2, recv2)
     finish = Finish(
         work, tiles, weight, rows_ref, rows_t, first_grad, total, block, sums, held, probs, load2, sems
     )
     reduce = Reduce(place, parts, grads + [leave_q, None], outs, scratch, *rest[:3])
-    swaps = [
-        Swap(place, [out_block], [swapped[0]], *rest[3:6]),
-        Swap(place, [block], [swapped[1]], *rest[6:9]),
-    ]
+    swap = Swap(place, [block], [swapped], *rest[3:6])
     for shard in range(LINE * PAIR):
         reduce.own[4][shard] = table_ref[pl.ds(shard * TABLE_ROWS, TABLE_ROWS), :]
     greet(place)
-    for step in in_order(finish_actions(reduce, finish, swaps), order):
+    for step in in_order(finish_actions(reduce, finish, swap), order):
         step()
     work.finish()
-    for swap in swaps:
-        swap.finish()
-
-
-def finish(rows, saved, grad, first_grad, table, weight, grads, block, parts, collective_id, order):
+    swap.finish()
+
+
+def finish(rows, saved, grad, first_grad, table, weight, grads, parts, collective_id, order):
     qkv, away, probs = saved
     count, width = rows.shape
     pairs = width // SPAN
@@ -1628,9 +1641,9 @@
     return pl.pallas_call(
         functools.partial(finish_kernel, parts, order),
         out_shape=[jax.ShapeDtypeStruct((p.rows, p.columns), p.dtype) for p in parts]
-        + [jax.ShapeDtypeStruct(block.shape, BF16)] * 2,
-        in_specs=[whole] * 5 + [far] * 7,
-        out_specs=[whole] * len(parts) + [far] * 2,
+        + [jax.ShapeDtypeStruct((2, count // 2, width), BF16)],
+        in_specs=[whole] * 5 + [far] * 6,
+        out_specs=[whole] * len(parts) + [far],
         scratch_shapes=[
             pltpu.VMEM((LINE * PAIR, queries.half_rows, queries.half_columns), BF16),
             pltpu.VMEM((2, width, tile), BF16),
@@ -1642,7 +1655,7 @@
             pltpu.VMEM((count, width), F32),
             pltpu.VMEM((8, width), F32),
             pltpu.VMEM((width, count), BF16),
-            pltpu.VMEM(block.shape, BF16),
+            pltpu.VMEM((2, count // 2, width), BF16),
             pltpu.SemaphoreType.DMA((2, pairs)),
             pltpu.SemaphoreType.DMA((2, pairs)),
             pltpu.SemaphoreType.DMA((2,)),
@@ -1654,12 +1667,12 @@
             pltpu.SemaphoreType.DMA((len(labels.numbers),)),
             pltpu.SemaphoreType.DMA((len(parts) * 2 * len(SPOTS),)),
         ]
-        + swap_scratch(1) * 2,
+        + swap_scratch(1),
         compiler_params=pltpu.CompilerParams(
             collective_id=collective_id, has_side_effects=True, vmem_limit_bytes=VMEM
         ),
         name="attention_backward_reduce",
-    )(rows, qkv, away, grad, table, first_grad, probs, weight, *grads, block)
+    )(rows, qkv, away, grad, table, first_grad, probs, weight, *grads)
 
 
 def exact_gelu(hidden):
@@ -1902,7 +1915,6 @@
         table += jnp.pad(vector.astype(F32).reshape(lines, LANES), filled)
         row += lines
     query_weight, key_weight, value_weight, output_weight, inner_weight, outer_weight = weights
-    blocks = (inputs.reshape(micro, block_len, width), cotangent.reshape(micro, block_len, width))
     shard_rows, hidden = inner_weight.shape
     flows = [Flow(0, TABLE_ROWS, lambda core, side: (0, TABLE_ROWS, 0, LANES), cores=False)]
     flows += column_flows(1, shard_rows, 3 * width, *GATHER_SPLIT[0])
@@ -1916,7 +1928,6 @@
         full_inner,
         full_outer,
         in_rows,
-        cot_rows,
         qkv,
         context,
         probs,
@@ -1924,7 +1935,7 @@
     ) = start(
         (table.astype(BF16),) + weights,
         ((0, 0), (1, 0), (1, width), (1, 2 * width), (2, 0), (3, 0), (4, 0)),
-        blocks,
+        inputs.reshape(micro, block_len, width),
         lengths,
         flows,
         shards,
@@ -1932,9 +1943,16 @@
         GATHER_ORDER,
     )
     in_rows = in_rows.reshape(rows, width)
-    cot_rows = cot_rows.reshape(rows, width)
     output, first_grad, context_grad, table_grad, output_part, inner_part, outer_part = middle(
-        in_rows, context, cot_rows, lengths, tables, full_output, full_inner, full_outer
+        3,
+        in_rows,
+        context,
+        cotangent.reshape(micro, block_len, width),
+        lengths,
+        tables,
+        full_output,
+        full_inner,
+        full_outer,
     )
     sums = finish(
         in_rows,
@@ -1944,7 +1962,6 @@
         table_grad,
         full_qkv,
         (inner_part, outer_part, output_part),
-        output.reshape(micro, block_len, width),
         [
             column_part(shard_rows, hidden, *REDUCE_SPLIT[0]),
             row_part(hidden // shards, width, *REDUCE_SPLIT[1]),
@@ -1955,10 +1972,10 @@
         2,
         REDUCE_ORDER,
     )
-    inner_share, outer_share, output_share, qkv_share, table_share, outs, grads = sums
+    inner_share, outer_share, output_share, qkv_share, table_share, grads = sums
     lines = tuple(vector.shape[0] // LANES for vector in vectors)
     wide = widen(
-        (qkv_share, output_share, inner_share, outer_share, grads, outs),
+        (qkv_share, output_share, inner_share, outer_share, grads, output),
         (3, 1, 1, 1, 1, 1),
         (F32,) * 5 + (BF16,),
         table_share,

time: 269 us -> 266 us (0.989)
  Pallas kernels: 267 us -> 263 us
    pallas_call x1, Pallas kernels: 109 us -> 106 us  [start(): pl.pallas_call(functools.partial(start_kernel, flows, spots, order), out_...]
where the time goes in v4:
time: 266 us; the launch traced here: 265 us
  Pallas kernels  263 us (99%)
    pallas_call x1, Pallas kernels, finish(): pl.pallas_call(functools.partial(finish_kernel, parts, order), out_shape=...  122 us
    pallas_call x1, Pallas kernels, start(): pl.pallas_call(functools.partial(start_kernel, flows, spots, order), out_...  106 us
    pallas_call x1, Pallas kernels, middle(): pl.pallas_call(middle_kernel, out_shape=[jax.ShapeDtypeStruct(cot.shape,...  29.7 us

profile of v4, /device:TPU:1, one launch (start us, length us, event | category | flops | bytes accessed | tf_op | source)
XLA Modules:
  0.0 265.3 jit_solution(8061585226202032811)
XLA Ops:
  0.7 1.4 add_convert_fusion.refs_0_
  2.1 106.4 %gather_attention_forward.1 = (bf16[128,128]{1,0:T(8,128)(2,1)}, bf16[1024,3072]{1,0:T(8,128)(2,1)}, bf16[1024,1024]{1,0:T(8,128)(2,1)}, bf16[1024,4096]{1,0:T(8...) custom-call(bf16[16,128]{1,0:T(8,128)(2,1)} %add_convert_fusion.refs, ...), custom_call_target="tpu_custom_call" | custom-call | tf_op jit(solution)/shard_map/gather_attention_forward/pallas_call | solution.py:1397
  108.4 29.7 %feed_forward.1 = (bf16[2,128,1024]{2,1,0:T(8,128)(2,1)}, f32[256,1024]{1,0:T(8,128)}, bf16[256,1024]{1,0:T(8,128)(2,1)}, f32[128,128]{1,0:T(8,128)}, bf16[1024,...) custom-call(bf16[256,1024]{1,0:T(8,128)(2,1)} %bitcast.19, ...), custom_call_target="tpu_custom_call" | custom-call | tf_op jit(solution)/shard_map/feed_forward/pallas_call | solution.py:1079
  138.1 122.4 %attention_backward_reduce.1 = (bf16[128,4096]{1,0:T(8,128)(2,1)}, bf16[512,1024]{1,0:T(8,128)(2,1)}, bf16[128,1024]{1,0:T(8,128)(2,1)}, bf16[128,3072]{1,0:T(8,...) custom-call(bf16[256,1024]{1,0:T(8,128)(2,1)} %bitcast.20, bf16[256,3072]{1,0:T(8,128)(2,1)} %get-tuple-element.58.refs_1_, ...), custom_call_target="tpu_custom_call" | custom-call | tf_op jit(solution)/shard_map/attention_backward_reduce/pallas_call | solution.py:1641
  260.5 4.6 %widen_results.1 = (f32[128,1024]{1,0:T(8,128)}, f32[128,1024]{1,0:T(8,128)}, f32[128,1024]{1,0:T(8,128)}, f32[128,1024]{1,0:T(8,128)}, f32[128,4096]{1,0:T(8,12...) custom-call(bf16[128,3072]{1,0:T(8,128)(2,1)} %get-tuple-element.73., ...), custom_call_target="tpu_custom_call" | custom-call | tf_op jit(solution)/shard_map/widen_results/pallas_call | solution.py:1175

commit v5 on v4

--- a/solution.py
+++ b/solution.py
@@ -13,33 +13,34 @@
 BF16 = jnp.bfloat16
 
 GATHER_SPLIT = ((256, 384), (256, 128), (1024, 128), (128, 64))
-REDUCE_SPLIT = ((768, 256), (160, 48), (256, 128), (1024, 256))
+REDUCE_SPLIT = ((1024, 384), (160, 0), (256, 128), (768, 256))
 GATHER_ORDER = (
-    10, 3, 2, 7, 4, 0, 8, 66, 64, 30, 5, 28, 1, 38, 43, 77, 72, 132, 15, 134, 98, 47, 111, 35,
-    166, 69, 140, 200, 145, 29, 103, 32, 97, 9, 183, 162, 74, 89, 128, 36, 100, 179, 114, 60, 63,
-    81, 106, 213, 67, 96, 180, 115, 34, 102, 68, 49, 12, 217, 94, 65, 201, 62, 149, 142, 141, 18,
-    164, 13, 208, 184, 99, 146, 31, 40, 168, 137, 76, 129, 78, 131, 16, 42, 83, 50, 136, 6, 61,
-    48, 51, 101, 209, 112, 174, 107, 151, 93, 117, 110, 225, 82, 171, 33, 14, 170, 123, 45, 214,
-    205, 130, 153, 144, 118, 52, 21, 19, 55, 202, 165, 119, 181, 169, 53, 175, 73, 113, 90, 218,
-    185, 152, 135, 116, 198, 133, 124, 199, 196, 150, 23, 120, 46, 85, 219, 59, 172, 167, 204,
-    203, 37, 108, 222, 22, 84, 148, 80, 188, 86, 71, 138, 79, 221, 220, 216, 20, 230, 212, 39, 11,
-    75, 210, 186, 178, 215, 154, 191, 182, 147, 232, 233, 70, 91, 234, 235, 17, 24, 104, 139, 105,
-    26, 121, 157, 236, 155, 176, 195, 163, 109, 143, 57, 226, 54, 159, 161, 92, 95, 211, 27, 25,
-    237, 197, 173, 56, 41, 177, 125, 127, 58, 231, 207, 238, 223, 160, 189, 193, 227, 44, 229,
-    126, 87, 88, 206, 122, 158, 187, 156, 239, 228, 190, 192, 194, 224, 240,
+    2, 3, 7, 64, 0, 10, 30, 72, 132, 1, 5, 38, 28, 200, 140, 43, 29, 77, 62, 15, 111, 98, 96, 8,
+    179, 32, 63, 180, 217, 69, 66, 164, 166, 81, 208, 40, 97, 134, 137, 99, 131, 4, 55, 145, 74,
+    100, 149, 39, 47, 183, 202, 83, 68, 9, 108, 34, 31, 213, 205, 148, 49, 12, 115, 106, 114, 45,
+    142, 136, 13, 151, 35, 46, 16, 48, 76, 204, 162, 230, 219, 203, 42, 130, 41, 117, 85, 17, 82,
+    102, 6, 184, 168, 174, 138, 101, 84, 116, 167, 201, 123, 152, 103, 143, 89, 144, 118, 94, 198,
+    165, 78, 222, 185, 169, 153, 14, 220, 70, 33, 128, 86, 50, 175, 23, 110, 107, 75, 199, 181,
+    65, 79, 25, 171, 67, 225, 147, 37, 218, 135, 71, 133, 150, 90, 191, 157, 176, 21, 196, 154,
+    52, 20, 18, 209, 120, 80, 206, 216, 192, 26, 60, 36, 170, 113, 231, 24, 182, 163, 141, 11,
+    186, 56, 215, 232, 22, 95, 59, 233, 178, 93, 214, 212, 51, 210, 91, 234, 223, 235, 197, 105,
+    158, 161, 226, 19, 127, 57, 53, 139, 236, 73, 119, 159, 195, 221, 27, 188, 211, 146, 44, 87,
+    237, 173, 121, 229, 124, 58, 112, 109, 54, 160, 177, 88, 129, 92, 61, 125, 155, 207, 172, 238,
+    122, 227, 104, 126, 156, 193, 189, 187, 239, 228, 190, 194, 224, 240,
 )
 REDUCE_ORDER = (
-    14, 8, 4, 7, 0, 116, 5, 10, 197, 9, 2, 1, 85, 39, 84, 198, 40, 123, 12, 35, 3, 15, 86, 87,
-    199, 92, 91, 200, 37, 36, 42, 89, 11, 94, 38, 201, 43, 32, 31, 69, 93, 29, 13, 88, 67, 68,
-    202, 203, 23, 70, 102, 205, 181, 18, 51, 117, 90, 61, 28, 19, 180, 24, 183, 22, 96, 95, 16,
-    132, 44, 100, 134, 118, 204, 104, 121, 17, 21, 148, 33, 110, 45, 124, 71, 72, 120, 34, 125,
-    77, 6, 101, 188, 20, 73, 74, 150, 119, 149, 47, 46, 151, 41, 57, 97, 190, 75, 136, 76, 103,
-    26, 156, 187, 133, 184, 126, 153, 168, 78, 164, 25, 185, 155, 106, 30, 127, 98, 182, 206, 152,
-    207, 105, 208, 158, 128, 79, 157, 122, 165, 189, 55, 53, 27, 52, 48, 108, 166, 80, 81, 154,
-    186, 135, 107, 172, 49, 170, 174, 54, 138, 160, 167, 129, 99, 159, 112, 169, 192, 56, 142,
-    191, 82, 59, 111, 130, 140, 161, 162, 109, 171, 176, 58, 63, 137, 173, 175, 139, 193, 194,
-    113, 114, 144, 62, 60, 131, 143, 177, 178, 141, 83, 50, 64, 65, 163, 145, 146, 115, 66, 179,
-    195, 147, 196,
+    33, 7, 9, 0, 8, 215, 84, 10, 85, 216, 1, 87, 86, 12, 5, 100, 29, 4, 102, 103, 101, 2, 217, 16,
+    91, 92, 89, 11, 35, 218, 36, 3, 40, 106, 107, 93, 37, 18, 94, 39, 219, 88, 42, 31, 38, 220,
+    221, 43, 24, 22, 25, 23, 110, 15, 17, 28, 26, 96, 44, 222, 153, 67, 68, 150, 151, 53, 57, 21,
+    13, 6, 14, 104, 105, 154, 30, 152, 69, 189, 45, 108, 149, 19, 118, 95, 109, 71, 72, 223, 90,
+    203, 198, 77, 201, 122, 167, 111, 120, 117, 183, 199, 41, 184, 181, 20, 119, 182, 165, 121,
+    169, 156, 200, 47, 51, 73, 27, 157, 191, 54, 185, 46, 32, 155, 224, 225, 159, 226, 158, 171,
+    97, 98, 55, 133, 124, 70, 79, 205, 141, 143, 75, 76, 74, 160, 186, 59, 161, 187, 139, 58, 61,
+    135, 188, 112, 113, 48, 137, 49, 202, 52, 173, 206, 126, 114, 125, 193, 168, 166, 208, 34,
+    123, 175, 162, 163, 190, 127, 99, 78, 192, 134, 172, 207, 56, 50, 128, 209, 210, 129, 170,
+    136, 80, 81, 138, 194, 60, 195, 115, 62, 63, 204, 130, 140, 131, 82, 177, 145, 196, 174, 176,
+    64, 65, 144, 132, 116, 142, 178, 179, 164, 146, 147, 211, 212, 83, 180, 197, 66, 148, 213,
+    214,
 )
 
 MESH = pl.DeviceIdType.MESH

time: 266 us -> 264 us (level)
  no operation moved by 1% of the time
where the time goes in v5:
time: 264 us; the launch traced here: 263 us
  Pallas kernels  261 us (99%)
    pallas_call x1, Pallas kernels, finish(): pl.pallas_call(functools.partial(finish_kernel, parts, order), out_shape=...  120 us
    pallas_call x1, Pallas kernels, start(): pl.pallas_call(functools.partial(start_kernel, flows, spots, order), out_...  107 us
    pallas_call x1, Pallas kernels, middle(): pl.pallas_call(middle_kernel, out_shape=[jax.ShapeDtypeStruct(cot.shape,...  29.8 us

profile of v5, /device:TPU:1, one launch (start us, length us, event | category | flops | bytes accessed | tf_op | source)
XLA Modules:
  0.0 263.4 jit_solution(16503497968696716115)
XLA Ops:
  0.7 1.4 add_convert_fusion.refs_0_
  2.1 106.5 %gather_attention_forward.1 = (bf16[128,128]{1,0:T(8,128)(2,1)}, bf16[1024,3072]{1,0:T(8,128)(2,1)}, bf16[1024,1024]{1,0:T(8,128)(2,1)}, bf16[1024,4096]{1,0:T(8...) custom-call(bf16[16,128]{1,0:T(8,128)(2,1)} %add_convert_fusion.refs, ...), custom_call_target="tpu_custom_call" | custom-call | tf_op jit(solution)/shard_map/gather_attention_forward/pallas_call | solution.py:1398
  108.6 29.8 %feed_forward.1 = (bf16[2,128,1024]{2,1,0:T(8,128)(2,1)}, f32[256,1024]{1,0:T(8,128)}, bf16[256,1024]{1,0:T(8,128)(2,1)}, f32[128,128]{1,0:T(8,128)}, bf16[1024,...) custom-call(bf16[256,1024]{1,0:T(8,128)(2,1)} %bitcast.19, ...), custom_call_target="tpu_custom_call" | custom-call | tf_op jit(solution)/shard_map/feed_forward/pallas_call | solution.py:1080
  138.4 120.3 %attention_backward_reduce.1 = (bf16[128,4096]{1,0:T(8,128)(2,1)}, bf16[512,1024]{1,0:T(8,128)(2,1)}, bf16[128,1024]{1,0:T(8,128)(2,1)}, bf16[128,3072]{1,0:T(8,...) custom-call(bf16[256,1024]{1,0:T(8,128)(2,1)} %bitcast.20, bf16[256,3072]{1,0:T(8,128)(2,1)} %get-tuple-element.58.refs_1_, ...), custom_call_target="tpu_custom_call" | custom-call | tf_op jit(solution)/shard_map/attention_backward_reduce/pallas_call | solution.py:1642
  258.6 4.6 %widen_results.1 = (f32[128,1024]{1,0:T(8,128)}, f32[128,1024]{1,0:T(8,128)}, f32[128,1024]{1,0:T(8,128)}, f32[128,1024]{1,0:T(8,128)}, f32[128,4096]{1,0:T(8,12...) custom-call(bf16[128,3072]{1,0:T(8,128)(2,1)} %get-tuple-element.73., ...), custom_call_target="tpu_custom_call" | custom-call | tf_op jit(solution)/shard_map/widen_results/pallas_call | solution.py:1176

commit v6 on v5

--- a/solution.py
+++ b/solution.py
@@ -1138,12 +1138,14 @@
         pltpu.make_async_copy(here, there, load.at[k])
         for k, (here, there) in enumerate(zip(ins + (table,), narrow + (held,)))
     ]
-    for copy in loads:
-        copy.start()
+    for k in (0, 1, count):
+        loads[k].start()
     copies = []
     at = 0
     for k, parts in enumerate(splits):
         loads[k].wait()
+        if k + 2 < count:
+            loads[k + 2].start()
         columns = narrow[k].shape[-1] // parts
         for part in range(parts):
             wides[at][...] = narrow[k][..., part * columns : (part + 1) * columns].astype(

time: 264 us -> 265 us (level)
  no operation moved by 1% of the time
where the time goes in v6:
time: 265 us
  Pallas kernels  263 us (99%)
    pallas_call x1, Pallas kernels, finish(): pl.pallas_call(functools.partial(finish_kernel, parts, order), out_shape=...  120 us
    pallas_call x1, Pallas kernels, start(): pl.pallas_call(functools.partial(start_kernel, flows, spots, order), out_...  107 us
    pallas_call x1, Pallas kernels, middle(): pl.pallas_call(middle_kernel, out_shape=[jax.ShapeDtypeStruct(cot.shape,...  29.8 us
    pallas_call x1, Pallas kernels, widen(): pl.pallas_call(functools.partial(widen_kernel, splits, lines), out_shape=...  5.99 us

profile of v6, /device:TPU:1, one launch (start us, length us, event | category | flops | bytes accessed | tf_op | source)
XLA Modules:
  0.0 264.8 jit_solution(14716763762542863369)
XLA Ops:
  0.7 1.4 add_convert_fusion.refs_0_
  2.1 106.5 %gather_attention_forward.1 = (bf16[128,128]{1,0:T(8,128)(2,1)}, bf16[1024,3072]{1,0:T(8,128)(2,1)}, bf16[1024,1024]{1,0:T(8,128)(2,1)}, bf16[1024,4096]{1,0:T(8...) custom-call(bf16[16,128]{1,0:T(8,128)(2,1)} %add_convert_fusion.refs, ...), custom_call_target="tpu_custom_call" | custom-call | tf_op jit(solution)/shard_map/gather_attention_forward/pallas_call | solution.py:1400
  108.6 29.8 %feed_forward.1 = (bf16[2,128,1024]{2,1,0:T(8,128)(2,1)}, f32[256,1024]{1,0:T(8,128)}, bf16[256,1024]{1,0:T(8,128)(2,1)}, f32[128,128]{1,0:T(8,128)}, bf16[1024,...) custom-call(bf16[256,1024]{1,0:T(8,128)(2,1)} %bitcast.19, ...), custom_call_target="tpu_custom_call" | custom-call | tf_op jit(solution)/shard_map/feed_forward/pallas_call | solution.py:1080
  138.4 120.3 %attention_backward_reduce.1 = (bf16[128,4096]{1,0:T(8,128)(2,1)}, bf16[512,1024]{1,0:T(8,128)(2,1)}, bf16[128,1024]{1,0:T(8,128)(2,1)}, bf16[128,3072]{1,0:T(8,...) custom-call(bf16[256,1024]{1,0:T(8,128)(2,1)} %bitcast.20, bf16[256,3072]{1,0:T(8,128)(2,1)} %get-tuple-element.58.refs_1_, ...), custom_call_target="tpu_custom_call" | custom-call | tf_op jit(solution)/shard_map/attention_backward_reduce/pallas_call | solution.py:1644
  258.6 6.0 %widen_results.1 = (f32[128,1024]{1,0:T(8,128)}, f32[128,1024]{1,0:T(8,128)}, f32[128,1024]{1,0:T(8,128)}, f32[128,1024]{1,0:T(8,128)}, f32[128,4096]{1,0:T(8,12...) custom-call(bf16[128,3072]{1,0:T(8,128)(2,1)} %get-tuple-element.73., ...), custom_call_target="tpu_custom_call" | custom-call | tf_op jit(solution)/shard_map/widen_results/pallas_call | solution.py:1178
